TPU v7x, 32 devices: a whole 2x2x4 slice. The times are simulated.
32 devices in a mesh: groups: 2 (over y), space: 8 (over z, x), dp: 2 (over core).
Axes of the slice: x: 2, y: 2, z: 4, core: 2. Of those that a mesh axis runs over, the one named last changes fastest.
Arguments:
- features: bfloat16 [4, 16, 8, 8, 512], P(('groups', 'dp'), 'space'), parts along dimension 0, may hold values from -6 to 6
- cotangent: bfloat16 [4, 16, 8, 8, 512], P(('groups', 'dp'), 'space'), parts along dimension 0, may hold values from -6 to 6
- kernel: bfloat16 [3, 3, 3, 64, 64], replicated, may hold values from -0.15625 to 0.15625
- neighbours: int32 [4, 16, 6], P(('groups', 'dp'), 'space'), parts along dimension 0, may hold values from -1 to 15, as said below
Outputs:
- response: bfloat16 [4, 16, 8, 8, 512], P(('groups', 'dp'), 'space'), parts along dimension 0
- feature_grad: bfloat16 [4, 16, 8, 8, 512], P(('groups', 'dp'), 'space'), parts along dimension 0
- kernel_grad: float32 [6, 3, 3, 64, 64], P('groups'), parts along dimension 0
There are 2 independent parts, one for each index of `groups`. A program takes and returns all parts, laid end to end along the dimension named above; an argument that names none is the same for every part. Nothing has to cross between parts.
Inputs may be any that keep to these rules, and one draw needn't show every extreme that they name: `neighbours`: the active bricks lie on a lattice of 3 by 8 by 4 bricks. Tile t sits at position p = t + 2: it covers lattice row p // 4 of the first dimension, rows 2 * (p % 4) to 2 * (p % 4) + 1 of the second and all rows of the third; it holds exactly 2 active bricks, in slots 2 * t to 2 * t + 1, listed by second then third lattice coordinate. In each realization one third-dimension row z is drawn, and every tile holds the bricks at z in its first and in its last second-dimension row; its other bricks are drawn at random. Directions are first dimension down, up, second down, up, third down, up; the relation is symmetric (if brick u is the up neighbour of s, s is the down neighbour of u), and -1 marks a neighbour that is inactive or outside the lattice.
All inputs are finite; a program needn't handle non-finite values.
Results may differ from a plain program's by a relative error of at most 0.0045.
Values may be sent and summed in bfloat16 or wider, within the bound.
No kernel may reach another device: no remote copies, remote signals or barrier semaphores. Data moves between devices by JAX's collectives and lax.ppermute only.
A program may use at most 64 MiB of HBM per device.

v0:
```python
import math

import jax
import jax.numpy as jnp
from jax import lax
from jax.sharding import PartitionSpec as P

TILES_Y = 4


def shifted(x, axis, by):
    count = lax.axis_size(axis)
    pairs = [(i, i + by) for i in range(count) if 0 <= i + by < count]
    return lax.ppermute(x, axis, pairs)


def choose_rows(tables, shifts, column, source_device, flat_slot, present, position):
    stacked = jnp.concatenate(tables, axis=0)
    row_count = tables[0].shape[0]
    source_pick = jnp.zeros_like(flat_slot[:, column])
    for number, offset in enumerate(shifts):
        source_pick = jnp.where(source_device[:, column] == position + offset, number, source_pick)
    row_index = source_pick * row_count + flat_slot[:, column]
    picked = jnp.take(stacked, row_index, axis=0)
    present_rows = present[:, column].reshape((-1,) + (1,) * (picked.ndim - 1))
    return jnp.where(present_rows, picked, jnp.zeros_like(picked))


def make_banded(weights, channels):
    toeplitz = jnp.zeros((3, 3, 4, channels, 2, channels), jnp.bfloat16)
    for out_cell in range(2):
        for tap_z in range(3):
            toeplitz = toeplitz.at[:, :, out_cell + tap_z, :, out_cell, :].set(weights[:, :, tap_z])
    return toeplitz.reshape(3, 3, 4 * channels, 2 * channels)


def make_windows(extended, channels, pairs_z):
    return jnp.stack(
        [
            extended[..., 2 * channels * block_index : 2 * channels * block_index + 4 * channels]
            for block_index in range(pairs_z)
        ],
        axis=3,
    )


def correlate(windows, banded, rows_all, brick_edge, pairs_z, channels):
    result = jnp.zeros((rows_all, brick_edge, brick_edge, pairs_z, 2 * channels), jnp.float32)
    for row_offset in range(3):
        for col_offset in range(3):
            window_part = windows[
                :, row_offset : row_offset + brick_edge, col_offset : col_offset + brick_edge
            ]
            result = result + jnp.einsum(
                "nabjk,kc->nabjc",
                window_part,
                banded[row_offset, col_offset],
                preferred_element_type=jnp.float32,
            )
    return result


def body(features, cotangent, kernel, neighbours):
    realizations = features.shape[0]
    bricks = features.shape[1]
    brick_edge = features.shape[2]
    channels = kernel.shape[-1]
    rows_all = realizations * bricks
    tile_stride = TILES_Y
    pairs_z = brick_edge // 2
    position = lax.axis_index("space")
    neighbour_slots = neighbours.reshape(rows_all, 6)
    present = neighbour_slots >= 0
    safe_links = jnp.where(present, neighbour_slots, 0)
    source_device = safe_links // bricks
    base_rows = jnp.repeat(jnp.arange(realizations, dtype=jnp.int32) * bricks, bricks)[:, None]
    flat_slot = base_rows + safe_links % bricks

    def select(tables, shifts, column):
        return choose_rows(tables, shifts, column, source_device, flat_slot, present, position)

    volume = features.reshape(rows_all, brick_edge, brick_edge, brick_edge * channels)
    upper_face = volume[:, brick_edge - 1]
    lower_face = volume[:, 0]
    from_below = shifted(upper_face, "space", tile_stride)
    from_above = shifted(lower_face, "space", -tile_stride)
    below_part = select([upper_face, from_below], [0, -tile_stride], 0)
    above_part = select([lower_face, from_above], [0, tile_stride], 1)
    layered_x = jnp.concatenate([below_part[:, None], volume, above_part[:, None]], axis=1)
    upper_face = layered_x[:, :, brick_edge - 1]
    lower_face = layered_x[:, :, 0]
    from_below = shifted(upper_face, "space", 1)
    from_above = shifted(lower_face, "space", -1)
    below_part = select([upper_face, from_below], [0, -1], 2)
    above_part = select([lower_face, from_above], [0, 1], 3)
    layered_y = jnp.concatenate([below_part[:, :, None], layered_x, above_part[:, :, None]], axis=2)
    upper_face = layered_y[..., (brick_edge - 1) * channels :]
    lower_face = layered_y[..., :channels]
    extended = jnp.concatenate(
        [select([upper_face], [0], 4), layered_y, select([lower_face], [0], 5)], axis=-1
    )
    banded = make_banded(kernel, channels)
    windows = make_windows(extended, channels, pairs_z)
    result = correlate(windows, banded, rows_all, brick_edge, pairs_z, channels)
    response = result.reshape(features.shape).astype(jnp.bfloat16)
    cotangent_pairs = cotangent.reshape(rows_all, brick_edge, brick_edge, pairs_z, 2 * channels)
    band_terms = []
    for row_offset in range(3):
        for col_offset in range(3):
            window_part = windows[
                :, row_offset : row_offset + brick_edge, col_offset : col_offset + brick_edge
            ]
            band_terms.append(
                jnp.einsum(
                    "nabjk,nabjc->kc",
                    window_part,
                    cotangent_pairs,
                    preferred_element_type=jnp.float32,
                )
            )
    band_grad = jnp.stack(band_terms).reshape(3, 3, 4, channels, 2, channels)
    kernel_local = jnp.stack(
        [
            band_grad[:, :, tap_z, :, 0, :] + band_grad[:, :, tap_z + 1, :, 1, :]
            for tap_z in range(3)
        ],
        axis=2,
    )
    cells_all = rows_all * lax.axis_size("dp") * lax.axis_size("space") * brick_edge**3
    factor = 1.0 / math.sqrt(cells_all)
    kernel_grad = lax.psum(kernel_local, ("space", "dp")) * factor
    spread = jnp.zeros(
        (rows_all, brick_edge + 2, brick_edge + 2, pairs_z, 4 * channels), jnp.float32
    )
    for row_offset in range(3):
        for col_offset in range(3):
            contribution = jnp.einsum(
                "nabjc,kc->nabjk",
                cotangent_pairs,
                banded[row_offset, col_offset],
                preferred_element_type=jnp.float32,
            )
            spread = spread.at[
                :, row_offset : row_offset + brick_edge, col_offset : col_offset + brick_edge
            ].add(contribution)
    widened = jnp.zeros(
        (rows_all, brick_edge + 2, brick_edge + 2, (brick_edge + 2) * channels), jnp.float32
    )
    for block_index in range(pairs_z):
        widened = widened.at[
            ..., 2 * channels * block_index : 2 * channels * block_index + 4 * channels
        ].add(spread[..., block_index, :])
    lower_rim = widened[..., :channels]
    upper_rim = widened[..., (brick_edge + 1) * channels :]
    trimmed_z = widened[..., channels : (brick_edge + 1) * channels]
    trimmed_z = trimmed_z.at[..., (brick_edge - 1) * channels :].add(select([lower_rim], [0], 5))
    trimmed_z = trimmed_z.at[..., :channels].add(select([upper_rim], [0], 4))
    lower_rim = trimmed_z[:, :, 0]
    upper_rim = trimmed_z[:, :, brick_edge + 1]
    trimmed_y = trimmed_z[:, :, 1 : brick_edge + 1]
    from_below = shifted(upper_rim.astype(jnp.bfloat16), "space", 1).astype(upper_rim.dtype)
    from_above = shifted(lower_rim.astype(jnp.bfloat16), "space", -1).astype(lower_rim.dtype)
    trimmed_y = trimmed_y.at[:, :, brick_edge - 1].add(select([lower_rim, from_above], [0, 1], 3))
    trimmed_y = trimmed_y.at[:, :, 0].add(select([upper_rim, from_below], [0, -1], 2))
    lower_rim = trimmed_y[:, 0]
    upper_rim = trimmed_y[:, brick_edge + 1]
    trimmed_x = trimmed_y[:, 1 : brick_edge + 1]
    from_below = shifted(upper_rim.astype(jnp.bfloat16), "space", tile_stride).astype(
        upper_rim.dtype
    )
    from_above = shifted(lower_rim.astype(jnp.bfloat16), "space", -tile_stride).astype(
        lower_rim.dtype
    )
    trimmed_x = trimmed_x.at[:, brick_edge - 1].add(
        select([lower_rim, from_above], [0, tile_stride], 1)
    )
    trimmed_x = trimmed_x.at[:, 0].add(select([upper_rim, from_below], [0, -tile_stride], 0))
    feature_grad = trimmed_x.reshape(features.shape).astype(jnp.bfloat16)
    return (response, feature_grad, kernel_grad)


def solution(mesh):
    in_specs = (
        P(("groups", "dp"), "space", None, None, None),
        P(("groups", "dp"), "space", None, None, None),
        P(),
        P(("groups", "dp"), "space", None),
    )
    out_specs = (
        P(("groups", "dp"), "space", None, None, None),
        P(("groups", "dp"), "space", None, None, None),
        P("groups", None, None, None, None),
    )
    return jax.shard_map(body, mesh=mesh, in_specs=in_specs, out_specs=out_specs, check_vma=False)
```

profile of v0, /device:TPU:0, one launch (start us, length us, event | category | flops | bytes accessed | tf_op | source)
XLA Modules:
  0.0 196.4 jit_solution(7922815339144183871)
XLA Ops:
  7.2 0.8 slice_bitcast_fusion.10
  8.0 5.9 %collective-permute-start = (bf16[2,8,512]{2,1,0:T(8,128)(2,1)S(1)}, bf16[2,8,512]{2,1,0:T(8,128)(2,1)S(1)}, u32[]{:S(2)}, u32[]{:S(2)}) collective-permute-start(bf16[2,8,512]{2,1,0:T(8,128)(2,1)S(1)} %get-tuple-element.377), channel_id=1, source_target_pairs={{0,8},{2,10},{4,12},{6,14},{1,9},{3,11},{5,13},{7,15},{16,24},{18,... | collective-permute-start | bytes 49160 | tf_op jit(solution)/shard_map/ppermute | solution.py:14
  14.0 1.3 collective-permute-start.1
  15.3 0.7 bitcast_compare_fusion
  16.0 0.7 and_select_fusion.1
  16.7 0.3 slice_reduce_fusion.7
  17.0 0.6 fusion.134
  17.6 0.6 fusion.133
  18.1 0.9 slice_bitcast_fusion.6
  19.1 0.3 scatter.20
  19.5 1.2 copy.377
  20.7 0.5 reshape.1187
  21.4 0.7 and_reduce_fusion
  22.5 1.5 fusion.10
  24.0 2.8 %scatter-add.65 = f32[2,10,10,4,256]{4,2,1,0,3:T(8,128)S(1)} dynamic-update-slice(f32[2,10,10,4,256]{4,2,1,0,3:T(8,128)S(1)} %scatter-add.64, f32[2,8,8,4,256]{4,2,1,0,3:T(8,128)S(1)} %fusion.10, s32[]{:T(128)} %constant.794.clone.1, s32[]{:T(128)} %bitcast.54, s32[]{:T(128)} %bitcast.55, s32[]{:T(128)} %constant.794.clone.1, s32[]{:T(128)} %constant.794.clone.1) | dynamic-update-slice | bytes 1048580 | tf_op jit(solution)/shard_map/scatter-add | solution.py:145
  26.9 2.1 %fusion.9 = f32[2,8,8,4,256]{4,2,1,0,3:T(8,128)S(1)} fusion(f32[2,10,10,4,256]{4,2,1,0,3:T(8,128)S(1)} %scatter-add.65, s32[]{:T(128)} %bitcast.59, s32[]{:T(128)} %bitcast.60, pred[]{:T(512)} %and_reduce_fusion, bf16[3,3,256,128]{3,2,1,0:T(8,128)(2,1)S(1)} %reshape.1187, bf16[1,2,8,8,512]{4,3,2,1,0:T(8,128)(2,1)S(1)} %copy-done), kind=kOutput, calls=%fused_computation.28 | convolution fusion | flops 33816576 | bytes 1245193 | tf_op jit(solution)/shard_map/nabjc,kc->nabjk/dot_general | solution.py:137
  29.0 2.9 %scatter-add.66 = f32[2,10,10,4,256]{4,2,1,0,3:T(8,128)S(1)} dynamic-update-slice(f32[2,10,10,4,256]{4,2,1,0,3:T(8,128)S(1)} %scatter-add.65, f32[2,8,8,4,256]{4,2,1,0,3:T(8,128)S(1)} %fusion.9, s32[]{:T(128)} %constant.794.clone.1, s32[]{:T(128)} %bitcast.59, s32[]{:T(128)} %bitcast.60, s32[]{:T(128)} %constant.794.clone.1, s32[]{:T(128)} %constant.794.clone.1) | dynamic-update-slice | bytes 1048580 | tf_op jit(solution)/shard_map/scatter-add | solution.py:145
  31.9 0.3 fusion.7
  32.4 1.5 scatter-add.70
  34.2 1.5 scatter-add.71
  35.7 0.3 fusion.3
  36.3 1.5 scatter-add.75
  38.0 1.5 scatter-add.76
  40.2 0.3 slice_reduce_fusion.5
  40.5 0.6 gather_fusion.6
  41.2 0.6 gather_fusion.7
  41.7 3.1 %scatter-add.85 = f32[2,10,10,512]{3,2,1,0:T(8,128)S(1)} dynamic-update-slice(f32[2,10,10,512]{3,2,1,0:T(8,128)S(1)} %slice.1260, f32[2,10,10,64]{3,2,1,0:T(8,128)S(1)} %get-tuple-element.368, s32[]{:T(128)} %constant.794.clone.1, s32[]{:T(128)} %constant.794.clone.1, s32[]{:T(128)} %constant.794.clone.1, s32[]{:T(128)} %constant.811.clone.1) | dynamic-update-slice | bytes 102404 | tf_op jit(solution)/shard_map/scatter-add | solution.py:156
  45.0 0.5 scatter-add.86
  45.6 1.3 collective-permute-start.4
  46.9 4.5 %collective-permute-start.5 = (bf16[2,10,512]{2,0,1:T(2,128)(2,1)S(1)}, bf16[2,10,512]{2,0,1:T(2,128)(2,1)S(1)}, u32[]{:S(2)}, u32[]{:S(2)}) collective-permute-start(bf16[2,10,512]{2,0,1:T(2,128)(2,1)S(1)} %bitcast.421), channel_id=1, source_target_pairs={{0,2},{2,4},{4,6},{6,8},{8,10},{10,12},{12,14},{1,3},{3,5},{5,7},{... | collective-permute-start | bytes 61448 | tf_op jit(solution)/shard_map/ppermute | solution.py:14
  51.8 0.5 gather_fusion
  52.3 0.5 gather_fusion.1
  53.2 1.3 collective-permute-start.3
  54.5 4.9 %collective-permute-start.2 = (bf16[2,10,512]{2,1,0:T(8,128)(2,1)S(1)}, bf16[2,10,512]{2,1,0:T(8,128)(2,1)S(1)}, u32[]{:S(2)}, u32[]{:S(2)}) collective-permute-start(bf16[2,10,512]{2,1,0:T(8,128)(2,1)S(1)} %copy.364), channel_id=1, source_target_pairs={{0,2},{2,4},{4,6},{6,8},{8,10},{10,12},{12,14},{1,3},{3,5},{5,7},{... | collective-permute-start | bytes 61448 | tf_op jit(solution)/shard_map/ppermute | solution.py:14
  59.6 0.6 gather_fusion.8
  60.3 0.6 gather_fusion.9
  61.4 5.4 %collective-permute-start.7 = (bf16[2,8,512]{2,1,0:T(8,128)(2,1)S(1)}, bf16[2,8,512]{2,1,0:T(8,128)(2,1)S(1)}, u32[]{:S(2)}, u32[]{:S(2)}) collective-permute-start(bf16[2,8,512]{2,1,0:T(8,128)(2,1)S(1)} %get-tuple-element.365), channel_id=1, source_target_pairs={{0,8},{2,10},{4,12},{6,14},{1,9},{3,11},{5,13},{7,15},{16,24},{18,... | collective-permute-start | bytes 49160 | tf_op jit(solution)/shard_map/ppermute | solution.py:14
  66.9 1.5 collective-permute-start.6
  68.4 0.5 gather_fusion.3
  69.1 0.5 gather_fusion.2
  70.3 0.6 gather_fusion.4
  70.9 0.6 gather_fusion.5
  71.6 0.4 fusion.37
  72.3 1.4 fusion.129
  74.0 0.2 convolution_add_fusion.6
  74.7 0.2 convolution_add_fusion.3
  75.5 0.6 gather_fusion.11
  76.1 0.6 gather_fusion.10
  76.8 0.7 copy.421
  77.5 0.9 fusion.21
  78.4 0.9 fusion.20
  79.4 0.9 fusion.19
  80.3 0.9 fusion.18
  81.3 0.9 fusion.17
  82.2 0.9 fusion.16
  83.2 0.9 fusion.15
  84.1 0.9 fusion.14
  85.0 0.9 fusion.13
  85.9 2.7 %reshape.1202 = f32[3,3,4,64,2,64]{5,4,3,2,1,0:T(2,128)S(1)} reshape(f32[9,256,128]{2,1,0:T(8,128)} %fusion.13) | data formatting | bytes 2359296 | tf_op jit(solution)/shard_map/reshape | solution.py:121
  88.6 1.9 fusion.128
  90.7 1.0 pad_maximum_fusion
  91.7 1.7 fusion.12
  93.4 94.0 %all-reduce.5.cloned.1.call-done = f32[3,3,3,64,64]{4,3,2,1,0:T(8,128)} async-done(((f32[3,3,3,64,64]{4,3,2,1,0:T(8,128)}), f32[3,3,3,64,64]{4,3,2,1,0:T(8,128)}) %all-reduce.5.cloned.1.call-update) | async-done | bytes 442384 | tf_op jit(solution)/shard_map/psum | solution.py:131
  187.4 2.2 %broadcast_multiply_fusion = f32[3,3,3,64,64]{4,3,2,1,0:T(8,128)} fusion(f32[3,3,3,64,64]{4,3,2,1,0:T(8,128)} %all-reduce.5.cloned.1.call-done), kind=kLoop, calls=%fused_computation.62 | loop fusion | flops 110592 | bytes 884736 | tf_op jit(solution)/shard_map/mul | solution.py:131
  (130 shorter events, 6.6 us)
Async XLA Ops:
  7.2 14.9 %copy-start = (bf16[1,2,8,8,512]{4,3,2,1,0:T(8,128)(2,1)S(1)}, bf16[1,2,8,8,512]{4,3,2,1,0:T(8,128)(2,1)}, u32[]{:S(2)}) copy-start(bf16[1,2,8,8,512]{4,3,2,1,0:T(8,128)(2,1)} %param.67) | copy-start | bytes 393220
  7.2 12.2 %copy-start.2 = (bf16[3,3,3,64,64]{4,3,2,1,0:T(8,128)(2,1)S(1)}, bf16[3,3,3,64,64]{4,3,2,1,0:T(8,128)(2,1)}, u32[]{:S(2)}) copy-start(bf16[3,3,3,64,64]{4,3,2,1,0:T(8,128)(2,1)} %param.68) | copy-start | bytes 663556
  7.2 180.2 %all-reduce.5.cloned.1.call-start = ((), (), s32[]{:S(2)}) async-start(), calls=%async_computation | async-start | bytes 1769472 | tf_op jit(solution)/shard_map/psum | solution.py:131
  8.0 43.7 %collective-permute-start = (bf16[2,8,512]{2,1,0:T(8,128)(2,1)S(1)}, bf16[2,8,512]{2,1,0:T(8,128)(2,1)S(1)}, u32[]{:S(2)}, u32[]{:S(2)}) collective-permute-start(bf16[2,8,512]{2,1,0:T(8,128)(2,1)S(1)} %get-tuple-element.377), channel_id=1, source_target_pairs={{0,8},{2,10},{4,12},{6,14},{1,9},{3,11},{5,13},{7,15},{16,24},{18,... | collective-permute-start | bytes 49160 | tf_op jit(solution)/shard_map/ppermute | solution.py:14
  14.0 38.3 %collective-permute-start.1 = (bf16[2,8,512]{2,1,0:T(8,128)(2,1)S(1)}, bf16[2,8,512]{2,1,0:T(8,128)(2,1)S(1)}, u32[]{:S(2)}, u32[]{:S(2)}) collective-permute-start(bf16[2,8,512]{2,1,0:T(8,128)(2,1)S(1)} %get-tuple-element.378), channel_id=1, source_target_pairs={{8,0},{10,2},{12,4},{14,6},{9,1},{11,3},{13,5},{15,7},{24,16},{26,... | collective-permute-start | bytes 49160 | tf_op jit(solution)/shard_map/ppermute | solution.py:14
  20.7 0.7 copy-start.10
  21.4 53.8 %copy-start.1 = (bf16[3,3,256,128]{3,2,1,0:T(8,128)(2,1)}, bf16[3,3,256,128]{3,2,1,0:T(8,128)(2,1)S(1)}, u32[]{:S(2)}) copy-start(bf16[3,3,256,128]{3,2,1,0:T(8,128)(2,1)S(1)} %reshape.1187) | copy-start | bytes 1769476
  44.9 8.1 %copy-start.3 = (bf16[1,2,8,8,512]{4,3,2,1,0:T(8,128)(2,1)S(1)}, bf16[1,2,8,8,512]{4,3,2,1,0:T(8,128)(2,1)}, u32[]{:S(2)}) copy-start(bf16[1,2,8,8,512]{4,3,2,1,0:T(8,128)(2,1)} %param.66) | copy-start | bytes 393220
  45.6 13.9 %collective-permute-start.4 = (bf16[2,10,512]{2,0,1:T(2,128)(2,1)S(1)}, bf16[2,10,512]{2,0,1:T(2,128)(2,1)S(1)}, u32[]{:S(2)}, u32[]{:S(2)}) collective-permute-start(bf16[2,10,512]{2,0,1:T(2,128)(2,1)S(1)} %bitcast.420), channel_id=1, source_target_pairs={{2,0},{4,2},{6,4},{8,6},{10,8},{12,10},{14,12},{3,1},{5,3},{7,5},{... | collective-permute-start | bytes 61448 | tf_op jit(solution)/shard_map/ppermute | solution.py:14
  46.9 12.5 %collective-permute-start.5 = (bf16[2,10,512]{2,0,1:T(2,128)(2,1)S(1)}, bf16[2,10,512]{2,0,1:T(2,128)(2,1)S(1)}, u32[]{:S(2)}, u32[]{:S(2)}) collective-permute-start(bf16[2,10,512]{2,0,1:T(2,128)(2,1)S(1)} %bitcast.421), channel_id=1, source_target_pairs={{0,2},{2,4},{4,6},{6,8},{8,10},{10,12},{12,14},{1,3},{3,5},{5,7},{... | collective-permute-start | bytes 61448 | tf_op jit(solution)/shard_map/ppermute | solution.py:14
  53.2 15.2 %collective-permute-start.3 = (bf16[2,10,512]{2,1,0:T(8,128)(2,1)S(1)}, bf16[2,10,512]{2,1,0:T(8,128)(2,1)S(1)}, u32[]{:S(2)}, u32[]{:S(2)}) collective-permute-start(bf16[2,10,512]{2,1,0:T(8,128)(2,1)S(1)} %copy.368), channel_id=1, source_target_pairs={{2,0},{4,2},{6,4},{8,6},{10,8},{12,10},{14,12},{3,1},{5,3},{7,5},{... | collective-permute-start | bytes 61448 | tf_op jit(solution)/shard_map/ppermute | solution.py:14
  54.5 14.6 %collective-permute-start.2 = (bf16[2,10,512]{2,1,0:T(8,128)(2,1)S(1)}, bf16[2,10,512]{2,1,0:T(8,128)(2,1)S(1)}, u32[]{:S(2)}, u32[]{:S(2)}) collective-permute-start(bf16[2,10,512]{2,1,0:T(8,128)(2,1)S(1)} %copy.364), channel_id=1, source_target_pairs={{0,2},{2,4},{4,6},{6,8},{8,10},{10,12},{12,14},{1,3},{3,5},{5,7},{... | collective-permute-start | bytes 61448 | tf_op jit(solution)/shard_map/ppermute | solution.py:14
  61.4 14.0 %collective-permute-start.7 = (bf16[2,8,512]{2,1,0:T(8,128)(2,1)S(1)}, bf16[2,8,512]{2,1,0:T(8,128)(2,1)S(1)}, u32[]{:S(2)}, u32[]{:S(2)}) collective-permute-start(bf16[2,8,512]{2,1,0:T(8,128)(2,1)S(1)} %get-tuple-element.365), channel_id=1, source_target_pairs={{0,8},{2,10},{4,12},{6,14},{1,9},{3,11},{5,13},{7,15},{16,24},{18,... | collective-permute-start | bytes 49160 | tf_op jit(solution)/shard_map/ppermute | solution.py:14
  66.9 9.1 %collective-permute-start.6 = (bf16[2,8,512]{2,1,0:T(8,128)(2,1)S(1)}, bf16[2,8,512]{2,1,0:T(8,128)(2,1)S(1)}, u32[]{:S(2)}, u32[]{:S(2)}) collective-permute-start(bf16[2,8,512]{2,1,0:T(8,128)(2,1)S(1)} %get-tuple-element.366), channel_id=1, source_target_pairs={{8,0},{10,2},{12,4},{14,6},{9,1},{11,3},{13,5},{15,7},{24,16},{26,... | collective-permute-start | bytes 49160 | tf_op jit(solution)/shard_map/ppermute | solution.py:14
  75.4 2.1 %copy-start.9 = (bf16[2,8,8,4,256]{4,2,3,1,0:T(8,128)(2,1)S(1)}, bf16[2,8,8,4,256]{4,2,3,1,0:T(8,128)(2,1)}, u32[]{:S(2)}) copy-start(bf16[2,8,8,4,256]{4,2,3,1,0:T(8,128)(2,1)} %get-tuple-element.360) | copy-start | bytes 786436
  77.5 1.0 copy-start.8
  78.4 0.9 copy-start.7
  79.4 0.9 copy-start.6
  80.3 0.9 copy-start.5
  81.3 0.9 copy-start.4
Sparse Core Ops, SparseCore 0:
  91.8 95.5 all-reduce.4
where the time goes:
time: 197 us; the launch traced here: 196 us
  waiting for transfers between devices  94 us (48%)
  local copies, waits for them, and re-layouts  35.9 us (18%)
  starting transfers between devices  26.2 us (13%)
  matrix products  17.3 us (9%)
  between operations  15.1 us (8%)
  other arithmetic  7.91 us (4%)
    psum x1, waiting for transfers between devices, body(): kernel_grad = lax.psum(kernel_local, ('space', 'dp')) * factor  94 us
    ppermute x8, starting transfers between devices, shifted(): return lax.ppermute(x, axis, pairs)  26.2 us
    scatter-add x7, local copies, waits for them, and re-layouts, body(): spread = spread.at[:, row_offset:row_offset + brick_edge, col_offset:col_...  12 us
    dot_general x9, matrix products, body(): jnp.einsum('nabjk,nabjc->kc', window_part, cotangent_pairs, preferred_ele...  8.32 us
    gather x12, local copies, waits for them, and re-layouts, choose_rows(): picked = jnp.take(stacked, row_index, axis=0)  6.66 us
    dot_general x9, matrix products, body(): jnp.einsum('nabjc,kc->nabjk', cotangent_pairs, banded[row_offset, col_off...  5.35 us
  transfers between devices with their start and end apart: 9, of which 1 were waited for; matrix products, arithmetic and copies ran while one was open for 22% of the time, Pallas kernels for 0%

commit v1 on v0

v1 whole, which is shorter than its diff:
```python
import functools
import math

import jax
import jax.numpy as jnp
import numpy as np
from jax import lax
from jax.experimental import pallas as pl
from jax.experimental.pallas import tpu as pltpu
from jax.sharding import PartitionSpec as P

TILES_Y = 4
F32 = jnp.float32
BF16 = jnp.bfloat16


def step_y(tile, sign, tiles):
    column = (tile + TILES_Y // 2) % TILES_Y + sign
    near = tile + sign
    return near if 0 <= column < TILES_Y and 0 <= near < tiles else None


def step_x(tile, sign, tiles):
    near = tile + sign * TILES_Y
    return near if 0 <= near < tiles else None


def path(tile, first, second, tiles):
    for axis, sign in (first, second):
        tile = None if tile is None else (step_x if axis == "x" else step_y)(tile, sign, tiles)
    return tile


def rounds(edges):
    found = []
    for edge in edges:
        for one in found:
            if edge[0] not in one and edge[1] not in one:
                break
        else:
            one = {}
            found.append(one)
        one[edge[0]] = (edge[1], edge[2])
        one[edge[1]] = (edge[0], edge[3])
    return found


def make_plan(tiles):
    along_x, along_y, corners = [], [], []
    for tile in range(tiles):
        up = step_x(tile, 1, tiles)
        if up is not None:
            along_x.append((tile, up, (1,), (0,)))
        up = step_y(tile, 1, tiles)
        if up is not None:
            along_y.append((tile, up, (1,), (0,)))
        for sign in (-1, 1):
            column = (tile + TILES_Y // 2) % TILES_Y + sign
            far = tile + TILES_Y + sign
            if not 0 <= column < TILES_Y or far >= tiles:
                continue
            x_up, x_down, y_to, y_back = ("x", 1), ("x", -1), ("y", sign), ("y", -sign)
            here = (path(tile, y_to, x_up, tiles) == far, path(tile, x_up, y_to, tiles) == far)
            there = (path(far, y_back, x_down, tiles) == tile, path(far, x_down, y_back, tiles) == tile)
            if any(here) or any(there):
                side = int(sign > 0)
                corners.append((tile, far, (2 + side, *map(int, here)), (1 - side, *map(int, there))))
    plan = [rounds(along_x), rounds(along_y), rounds(corners)]
    table = []
    for tile in range(tiles):
        row = []
        for kind, width in zip(plan, (1, 1, 3)):
            for one in kind:
                row.extend(one[tile][1] if tile in one else (-1,) + (0,) * (width - 1))
        table.append(row)
    pairs = [[[(tile, one[tile][0]) for tile in sorted(one)] for one in kind] for kind in plan]
    return pairs, np.asarray(table, np.int32)


class Roles:
    def __init__(self, table_ref, counts):
        self.row = lax.axis_index("space")
        self.table, self.counts = table_ref, counts

    def x(self, number):
        return self.table[self.row, number]

    def y(self, number):
        return self.table[self.row, self.counts[0] + number]

    def corner(self, number, field):
        return self.table[self.row, self.counts[0] + self.counts[1] + 3 * number + field]


def faces_kernel(counts, table_ref, f_ref, c_ref, *out_refs):
    roles = Roles(table_ref, counts)
    edge = f_ref.shape[1]
    x_refs = out_refs[: counts[0]]
    y_refs = out_refs[counts[0] : counts[0] + counts[1]]
    corner_refs = out_refs[counts[0] + counts[1] :]
    for number, out in enumerate(x_refs):
        plane = jnp.where(roles.x(number) == 1, edge - 1, 0)
        for source, ref in enumerate((f_ref, c_ref)):
            for brick in range(2):
                out[source, brick] = ref[brick, plane]
    rows = []
    for ref in (f_ref, c_ref):
        low = ref[0].astype(F32)[:, 0, :]
        high = ref[1].astype(F32)[:, edge - 1, :]
        rows.append((low, high))
    for number, out in enumerate(y_refs):
        up = roles.y(number) == 1
        for source, (low, high) in enumerate(rows):
            out[source] = jnp.where(up, high, low).astype(BF16)
    for number, out in enumerate(corner_refs):
        slot = roles.corner(number, 0)
        for source, (low, high) in enumerate(rows):
            at_low = jnp.where(slot >= 2, low[edge - 1 : edge], low[0:1])
            at_high = jnp.where(slot >= 2, high[edge - 1 : edge], high[0:1])
            line = jnp.where(slot % 2 == 1, at_high, at_low)
            out[source] = jnp.broadcast_to(line, out.shape[1:]).astype(BF16)


def padded(x, channels):
    zeros = jnp.zeros(x.shape[:-1] + (2 * channels,), F32)
    return pltpu.roll(jnp.concatenate([x, zeros], axis=-1), channels, x.ndim - 1)


def masked(keep, x):
    return jnp.where(keep, x, jnp.zeros_like(x))


def weights_kernel(kernel_ref, forward_ref, backward_ref, wide):
    channels = kernel_ref.shape[-1]
    wide[...] = jnp.zeros_like(wide)
    wide[:, :, :channels] = kernel_ref[...].astype(F32)
    for tap in range(9):
        plain = [wide[3 * tap + d] for d in range(3)]
        moved = [pltpu.roll(x, channels, 1) for x in plain]
        steps = (plain[0], plain[1] + moved[0], plain[2] + moved[1], moved[2])
        for number, block in enumerate(steps):
            forward_ref[tap, channels * number : channels * (number + 1), :] = block.astype(BF16)
        last = 8 - tap
        lanes = 2 * channels
        backward_ref[last, :channels, :lanes] = (plain[2] + moved[1]).astype(BF16)
        backward_ref[last, :channels, lanes:] = plain[0].astype(BF16)
        backward_ref[last, channels:, :lanes] = moved[2].astype(BF16)
        backward_ref[last, channels:, lanes:] = (plain[1] + moved[0]).astype(BF16)


def kernel_grad_kernel(counts, channels, table_ref, link_ref, f_ref, c_ref, *refs):
    roles = Roles(table_ref, counts)
    x_refs = refs[: counts[0]]
    y_refs = refs[counts[0] : counts[0] + counts[1]]
    keep_ref, send_ref, wide, tall, packed = refs[counts[0] + counts[1] :]
    bricks, edge, _, width = f_ref.shape
    rows = edge * edge
    wide[:, edge : edge + rows, :] = padded(f_ref[...].astype(F32).reshape(bricks, rows, width), channels)
    for side in range(2):
        start = side * (edge + rows)
        plane = jnp.zeros((bricks, edge, width), F32)
        for number, ref in enumerate(x_refs):
            plane = jnp.where(roles.x(number) == side, ref[0].astype(F32), plane)
        plane = padded(plane, channels)
        for brick in range(bricks):
            wide[brick, start : start + edge, :] = masked(link_ref[brick, side] >= 0, plane[brick])
    own = c_ref[...].astype(F32)
    tall[:, :, edge : 2 * edge, :] = own
    tall[1, :, edge - 1 : edge, :] = masked(link_ref[1, 2] >= 0, own[0, :, edge - 1 :, :])
    tall[0, :, 2 * edge : 2 * edge + 1, :] = masked(link_ref[0, 3] >= 0, own[1, :, 0:1, :])
    for side in range(2):
        row = jnp.zeros((edge, width), F32)
        for number, ref in enumerate(y_refs):
            row = jnp.where(roles.y(number) == side, ref[1].astype(F32), row)
        at = 2 * edge if side else edge - 1
        tall[side, :, at : at + 1, :] = masked(link_ref[side, 2 + side] >= 0, row)[:, None, :]
    lanes = 2 * channels
    pairs = width // lanes
    right = []
    for col in range(3):
        value = tall[:, :, edge + 1 - col : 2 * edge + 1 - col, :].reshape(bricks * rows, width).astype(BF16)
        right.append(jnp.concatenate([value[:, lanes * k : lanes * (k + 1)] for k in range(pairs)], axis=0))
    right = jnp.concatenate(right, axis=1)
    low = lax.broadcasted_iota(jnp.int32, (3 * channels // 2, lanes), 1) < channels
    half = 3 * channels // 2
    for row in range(3):
        value = wide[:, edge * row : edge * row + rows, :].reshape(bricks * rows, -1).astype(BF16)
        left = jnp.concatenate([value[:, lanes * k : lanes * (k + 2)] for k in range(pairs)], axis=0)
        grad = lax.dot_general(left, right, (((0,), (0,)), ((), ())), preferred_element_type=F32)
        for col in range(3):
            block = grad[:, lanes * col : lanes * (col + 1)]
            moved = pltpu.roll(block, channels, 1)
            first = block[:half] + moved[channels : channels + half]
            second = moved[half : 2 * half] + block[channels + half :]
            at = half * (3 * row + col)
            packed[at : at + half, :] = jnp.where(low, first, second)
    count = keep_ref.shape[0]
    core = lax.axis_index("dp")
    keep_ref[...] = packed[pl.ds(pl.multiple_of(core * count, 8), count), :]
    send_ref[...] = packed[pl.ds(pl.multiple_of((1 - core) * count, 8), count), :]


def conv_kernel(counts, channels, source, table_ref, link_ref, v_ref, weight_ref, *refs):
    roles = Roles(table_ref, counts)
    x_refs = refs[: counts[0]]
    y_refs = refs[counts[0] : counts[0] + counts[1]]
    corner_refs = refs[counts[0] + counts[1] : sum(counts)]
    out_ref, ext = refs[sum(counts) :]
    bricks, edge, _, width = v_ref.shape
    rows = edge * edge
    first, last = edge, 2 * edge - 1
    ext[:, 1 : edge + 1, first : last + 1, :] = padded(v_ref[...].astype(F32), channels)
    for side in range(2):
        plane = jnp.zeros((bricks, edge, width), F32)
        for number, ref in enumerate(x_refs):
            plane = jnp.where(roles.x(number) == side, ref[source].astype(F32), plane)
        plane = padded(plane, channels)
        for brick in range(bricks):
            ext[brick, side * (edge + 1), first : last + 1, :] = masked(link_ref[brick, side] >= 0, plane[brick])
    for side in range(2):
        row = jnp.zeros((edge, width), F32)
        for number, ref in enumerate(y_refs):
            row = jnp.where(roles.y(number) == side, ref[source].astype(F32), row)
        at = last + 1 if side else first - 1
        row = masked(link_ref[side, 2 + side] >= 0, padded(row, channels))
        ext[side, 1 : edge + 1, at : at + 1, :] = row[:, None, :]
        for across in range(2):
            line = jnp.zeros((1, width), F32)
            for number, ref in enumerate(corner_refs):
                hit = (roles.corner(number, 0) == 2 * across + side) & (roles.corner(number, 1 + source) == 1)
                line = jnp.where(hit, ref[source, 0:1].astype(F32), line)
            ext[side, across * (edge + 1), at : at + 1, :] = padded(line, channels)
    ext[1, :, first - 1 : first, :] = masked(link_ref[1, 2] >= 0, ext[0, :, last : last + 1, :])
    ext[0, :, last + 1 : last + 2, :] = masked(link_ref[0, 3] >= 0, ext[1, :, first : first + 1, :])
    lanes = 2 * channels
    pairs = width // lanes
    total = jnp.zeros((pairs * bricks * rows, lanes), F32)
    contract = 0 if source == 0 else 1
    for col in range(3):
        for row in range(3):
            value = ext[:, row : row + edge, first - 1 + col : last + col, :]
            value = value.reshape(bricks * rows, -1).astype(BF16)
            left = jnp.concatenate([value[:, lanes * k : lanes * (k + 2)] for k in range(pairs)], axis=0)
            total = total + lax.dot_general(
                left, weight_ref[3 * row + col], (((1,), (contract,)), ((), ())), preferred_element_type=F32
            )
    for k in range(pairs):
        out_ref[:, lanes * k : lanes * (k + 1)] = total[bricks * rows * k : bricks * rows * (k + 1)].astype(BF16)


def unpack_kernel(factor, own_ref, other_ref, out_ref, packed):
    count = own_ref.shape[0]
    core = lax.axis_index("dp")
    packed[pl.ds(pl.multiple_of(core * count, 8), count), :] = own_ref[...] * factor
    packed[pl.ds(pl.multiple_of((1 - core) * count, 8), count), :] = other_ref[...] * factor
    taps, rows, channels = out_ref.shape
    half = rows // 2
    for tap in range(taps):
        block = packed[half * tap : half * (tap + 1), :]
        out_ref[tap, :half, :] = block[:, :channels]
        out_ref[tap, half:, :] = pltpu.roll(block, channels, 1)[:, :channels]


VMEM = pl.BlockSpec(memory_space=pltpu.VMEM)
SMEM = pl.BlockSpec(memory_space=pltpu.SMEM)


def call(kernel, in_specs, out_shapes, scratch=(), flops=0, name=None):
    several = isinstance(out_shapes, list)
    return pl.pallas_call(
        kernel,
        in_specs=in_specs,
        out_specs=[VMEM] * len(out_shapes) if several else VMEM,
        out_shape=out_shapes,
        scratch_shapes=list(scratch),
        compiler_params=pltpu.CompilerParams(vmem_limit_bytes=24 * 2**20),
        cost_estimate=pl.CostEstimate(flops=flops, bytes_accessed=2**20, transcendentals=0),
        name=name,
    )


def body(tiles, features, cotangent, kernel, neighbours):
    pairs, table = make_plan(tiles)
    counts = tuple(len(kind) for kind in pairs)
    table = jnp.asarray(table)
    bricks, edge = features.shape[1:3]
    width = features.shape[-1]
    channels = kernel.shape[-1]
    rows = edge * edge
    lanes = 2 * channels
    shape = jax.ShapeDtypeStruct
    f = features.reshape(bricks, edge, edge, width)
    c = cotangent.reshape(bricks, edge, edge, width)
    links = neighbours.reshape(bricks, 6)

    face_shapes = [(2, bricks, edge, width)] * counts[0] + [(2, edge, width)] * counts[1] + [(2, 8, width)] * counts[2]
    faces = call(
        functools.partial(faces_kernel, counts),
        [SMEM, VMEM, VMEM],
        [shape(s, BF16) for s in face_shapes],
        name="faces",
    )(table, f, c)
    flat_pairs = [one for kind in pairs for one in kind]
    near = counts[0] + counts[1]
    got = [lax.ppermute(x, "space", one) for x, one in zip(faces[:near], flat_pairs)]
    forward, backward = call(
        weights_kernel,
        [VMEM],
        [shape((9, 4 * channels, lanes), BF16), shape((9, lanes, 4 * channels), BF16)],
        [pltpu.VMEM((27, channels, lanes), F32)],
        name="weights",
    )(kernel.reshape(27, channels, channels))

    count = 27 * channels * channels // lanes // 2
    keep, send = call(
        functools.partial(kernel_grad_kernel, counts, channels),
        [SMEM, SMEM, VMEM, VMEM] + [VMEM] * near,
        [shape((count, lanes), F32)] * 2,
        [
            pltpu.VMEM((bricks, rows + 2 * edge, width + lanes), F32),
            pltpu.VMEM((bricks, edge, 3 * edge, width), F32),
            pltpu.VMEM((2 * count, lanes), F32),
        ],
        flops=2 * 768 * 384 * 512,
        name="kernel_grad",
    )(table, links, f, c, *got)

    swap = [(0, 1), (1, 0)]
    part = keep + lax.ppermute(send, "dp", swap)
    got += [lax.ppermute(x, "space", one) for x, one in zip(faces[near:], flat_pairs[near:])]

    def conv(source, x, weight):
        return call(
            functools.partial(conv_kernel, counts, channels, source),
            [SMEM, SMEM, VMEM, VMEM] + [VMEM] * len(got),
            shape((bricks * rows, width), BF16),
            [pltpu.VMEM((bricks, edge + 2, 3 * edge, width + lanes), F32)],
            flops=2 * 512 * 256 * 128 * 9,
            name="response" if source == 0 else "feature_grad",
        )(table, links, x, weight, *got)

    response = conv(0, f, forward).reshape(features.shape)
    feature_grad = conv(1, c, backward).reshape(features.shape)
    steps = tiles.bit_length() - 1
    wire = BF16 if steps <= 3 else F32
    for number in range(steps):
        mine = lax.optimization_barrier(part.astype(wire))
        theirs = lax.ppermute(mine, "space", [(i, i ^ (1 << number)) for i in range(tiles)])
        part = mine.astype(F32) + theirs.astype(F32)
    other = lax.ppermute(part, "dp", swap)
    cells = bricks * tiles * lax.axis_size("dp") * edge**3
    kernel_grad = call(
        functools.partial(unpack_kernel, 1.0 / math.sqrt(cells)),
        [VMEM, VMEM],
        shape((9, 3 * channels, channels), F32),
        [pltpu.VMEM((2 * count, lanes), F32)],
        name="unpack",
    )(part, other).reshape(kernel.shape)
    return response, feature_grad, kernel_grad


def solution(mesh):
    bricks_spec = P(("groups", "dp"), "space", None, None, None)
    return jax.shard_map(
        functools.partial(body, mesh.shape["space"]),
        mesh=mesh,
        in_specs=(bricks_spec, bricks_spec, P(), P(("groups", "dp"), "space", None)),
        out_specs=(bricks_spec, bricks_spec, P("groups", None, None, None, None)),
        check_vma=False,
    )
```

time: 197 us -> 52.2 us (0.26)
  waiting for transfers between devices: 94 us -> 19.9 us
  local copies, waits for them, and re-layouts: 35.9 us -> 2.52 us
  matrix products: 17.3 us -> 0 us
  between operations: 15.1 us -> 0.76 us
  Pallas kernels: 0 us -> 8.22 us
  other arithmetic: 7.91 us -> 0.11 us
  starting transfers between devices: 26.2 us -> 20.4 us
    psum x1 -> x0, waiting for transfers between devices: 94 us -> none  [body(): kernel_grad = lax.psum(kernel_local, ('space', 'dp')) * factor]
    ppermute x8 -> x10, waiting for transfers between devices: 0.02 us -> 19.9 us  [the longest x3 11.9 us: body(): lax.ppermute(mine, 'space', [(i, i ^ 1 << number) for i in range(tiles)])]
    dot_general x27 -> x0, matrix products: 17.3 us -> none  [the longest x9 8.32 us: body(): jnp.einsum('nabjk,nabjc->kc', window_part, cotangent_pairs, preferred_ele...]
    scatter-add x13 -> x0, local copies, waits for them, and re-layouts: 16 us -> none  [the longest x7 12 us: body(): spread = spread.at[:, row_offset:row_offset + brick_edge, col_offset:col_...]
    pallas_call x0 -> x6, Pallas kernels: none -> 8.22 us  [the longest x2 4.3 us: conv(): call(functools.partial(conv_kernel, counts, channels, source), [SMEM, SME...]
    gather x12 -> x0, local copies, waits for them, and re-layouts: 6.66 us -> none  [choose_rows(): picked = jnp.take(stacked, row_index, axis=0)]
    ppermute x8 -> x10, starting transfers between devices: 26.2 us -> 20.4 us  [the longest x5 12 us: body(): lax.ppermute(x, 'space', one)]
    slice x15 -> x0, local copies, waits for them, and re-layouts: 4.17 us -> none  [the longest x1 1.91 us: body(): band_grad[:, :, tap_z + 1, :, 1, :]]
  transfers between devices with their start and end apart: 9 -> 10, of which waited for: 1 -> 7; matrix products, arithmetic and copies ran while one was open for 22% -> 0% of each run, Pallas kernels for 0% -> 9%
where the time goes in v1:
time: 52.2 us; the launch traced here: 52 us
  starting transfers between devices  20.4 us (39%)
  waiting for transfers between devices  19.9 us (38%)
  Pallas kernels  8.22 us (16%)
  local copies, waits for them, and re-layouts  2.52 us (5%)
  between operations  0.76 us (1%)
    ppermute x5, starting transfers between devices, body(): lax.ppermute(x, 'space', one)  12 us
    ppermute x3, waiting for transfers between devices, body(): lax.ppermute(mine, 'space', [(i, i ^ 1 << number) for i in range(tiles)])  11.9 us
    ppermute x3, starting transfers between devices, body(): lax.ppermute(mine, 'space', [(i, i ^ 1 << number) for i in range(tiles)])  8.31 us
    ppermute x5, waiting for transfers between devices, body(): lax.ppermute(x, 'space', one)  6.57 us
    pallas_call x2, Pallas kernels, conv(): call(functools.partial(conv_kernel, counts, channels, source), [SMEM, SME...  4.3 us
    unnamed x16, local copies, waits for them, and re-layouts  2.52 us
    pallas_call x1, Pallas kernels, body(): call(functools.partial(kernel_grad_kernel, counts, channels), [SMEM, SMEM...  1.69 us
    ppermute x1, waiting for transfers between devices, body(): part = keep + lax.ppermute(send, 'dp', swap)  1.46 us
  transfers between devices with their start and end apart: 10, of which 7 were waited for; matrix products, arithmetic and copies ran while one was open for 0% of the time, Pallas kernels for 9%

profile of v1, /device:TPU:0, one launch (start us, length us, event | category | flops | bytes accessed | tf_op | source)
XLA Modules:
  0.0 52.0 jit_solution(7588403756122905760)
XLA Ops:
  0.6 0.0 copy-start.1
  0.6 0.9 %copy-done.1 = bf16[1,2,8,8,512]{4,3,2,1,0:T(8,128)(2,1)S(1)} copy-done((bf16[1,2,8,8,512]{4,3,2,1,0:T(8,128)(2,1)S(1)}, bf16[1,2,8,8,512]{4,3,2,1,0:T(8,128)(2,1)}, u32[]{:S(2)}) %copy-start.1) | copy-done | bytes 131096
  1.5 0.0 copy-start.3
  1.5 0.9 %copy-done.3 = bf16[1,2,8,8,512]{4,3,2,1,0:T(8,128)(2,1)S(1)} copy-done((bf16[1,2,8,8,512]{4,3,2,1,0:T(8,128)(2,1)S(1)}, bf16[1,2,8,8,512]{4,3,2,1,0:T(8,128)(2,1)}, u32[]{:S(2)}) %copy-start.3) | copy-done | bytes 131096
  2.4 0.0 copy-start.5
  2.4 0.7 %copy-done.5 = s32[8,9]{1,0:T(8,128)S(1)} copy-done((s32[8,9]{1,0:T(8,128)S(1)}, s32[8,9]{1,0:T(8,128)}, u32[]{:S(2)}) %copy-start.5) | copy-done | bytes 312
  3.1 0.7 %faces.1 = (bf16[2,2,8,512]{3,2,1,0:T(8,128)(2,1)S(1)}, bf16[2,8,512]{2,1,0:T(8,128)(2,1)S(1)}, bf16[2,8,512]{2,1,0:T(8,128)(2,1)S(1)}, bf16[2,8,512]{2,1,0:T(8,128)(2,1)S(1)}, bf16[2,8,512]{2,1,0:T(8,128)(2,1)S(1)}) custom-call(s32[8,9]{1,0:T(8,128)S(1)} %copy-done.5, bf16[2,8,8,512]{3,2,1,0:T(8,128)(2,1)S(1)} %bitcast.8, bf16[2,8,8,512]{3,2,1,0:T(8,128)(2,1)S(1)} %bitcast.11), custom_call_target="tpu_custom_call" | custom-call | bytes 1048576 | tf_op jit(solution)/shard_map/faces/pallas_call | solution.py:297
  3.9 4.1 %collective-permute-start = (bf16[2,2,8,512]{3,2,1,0:T(8,128)(2,1)S(1)}, bf16[2,2,8,512]{3,2,1,0:T(8,128)(2,1)S(1)}, u32[]{:S(2)}, u32[]{:S(2)}) collective-permute-start(bf16[2,2,8,512]{3,2,1,0:T(8,128)(2,1)S(1)} %get-tuple-element.13), channel_id=1, source_target_pairs={{0,8},{2,10},{4,12},{6,14},{8,0},{10,2},{12,4},{14,6},{1,9},{3,11}... | collective-permute-start | bytes 98312 | tf_op jit(solution)/shard_map/ppermute | solution.py:305
  8.0 1.5 %collective-permute-start.1 = (bf16[2,8,512]{2,1,0:T(8,128)(2,1)S(1)}, bf16[2,8,512]{2,1,0:T(8,128)(2,1)S(1)}, u32[]{:S(2)}, u32[]{:S(2)}) collective-permute-start(bf16[2,8,512]{2,1,0:T(8,128)(2,1)S(1)} %get-tuple-element.14), channel_id=1, source_target_pairs={{0,2},{2,0},{4,6},{6,4},{8,10},{10,8},{12,14},{14,12},{1,3},{3,1},... | collective-permute-start | bytes 49160 | tf_op jit(solution)/shard_map/ppermute | solution.py:305
  9.5 0.0 copy-start.7
  9.5 0.8 %collective-permute-start.2 = (bf16[2,8,512]{2,1,0:T(8,128)(2,1)S(1)}, bf16[2,8,512]{2,1,0:T(8,128)(2,1)S(1)}, u32[]{:S(2)}, u32[]{:S(2)}) collective-permute-start(bf16[2,8,512]{2,1,0:T(8,128)(2,1)S(1)} %get-tuple-element.15), channel_id=1, source_target_pairs={{6,8},{8,6},{7,9},{9,7},{22,24},{24,22},{23,25},{25,23}} | collective-permute-start | bytes 49160 | tf_op jit(solution)/shard_map/ppermute | solution.py:305
  10.3 1.5 %collective-permute-done.1.refs_1_ = bf16[2,8,512]{2,1,0:T(8,128)(2,1)S(1)} collective-permute-done((bf16[2,8,512]{2,1,0:T(8,128)(2,1)S(1)}, bf16[2,8,512]{2,1,0:T(8,128)(2,1)S(1)}, u32[]{:S(2)}, u32[]{:S(2)}) %collective-permute-start.1) | collective-permute-done | bytes 16416 | tf_op jit(solution)/shard_map/ppermute | solution.py:305
  11.7 0.0 collective-permute-done.2.refs_2_
  11.7 0.0 collective-permute-done.refs_0_
  11.7 0.0 copy-done.7
  11.7 1.7 %kernel_grad.1 = (f32[432,128]{1,0:T(8,128)S(1)}, f32[432,128]{1,0:T(8,128)S(1)}) custom-call(s32[8,9]{1,0:T(8,128)S(1)} %copy-done.5, s32[2,6]{1,0:T(2,128)S(1)} %bitcast.14, bf16[2,8,8,512]{3,2,1,0:T(8,128)(2,1)S(1)} %bitcast.9, bf16[2,8,8,512]{3,2,1,0:T(8,128)(2,1)S(1)} %bitcast.12, bf16[2,2,8,512]{3,2,1,0:T(8,128)(2,1)S(1)} %collective-permute-done.refs_0_, ...), custom_call_target="tpu_custom_call" | custom-call | flops 301989888 | bytes 1048576 | tf_op jit(solution)/shard_map/kernel_grad/pallas_call | solution.py:315
  13.4 0.1 collective-permute-start.5
  13.5 1.5 %collective-permute-done.5 = f32[432,128]{1,0:T(8,128)S(1)} collective-permute-done((f32[432,128]{1,0:T(8,128)S(1)}, f32[432,128]{1,0:T(8,128)S(1)}, u32[]{:S(2)}, u32[]{:S(2)}) %collective-permute-start.5) | collective-permute-done | bytes 221216 | tf_op jit(solution)/shard_map/ppermute | solution.py:329
  15.0 1.6 %collective-permute-start.6 = (bf16[432,128]{1,0:T(8,128)(2,1)S(1)}, bf16[432,128]{1,0:T(8,128)(2,1)S(1)}, u32[]{:S(2)}, u32[]{:S(2)}) collective-permute-start(bf16[432,128]{1,0:T(8,128)(2,1)S(1)} %add_convert_fusion.2), channel_id=1, source_target_pairs={{0,2},{2,0},{4,6},{6,4},{8,10},{10,8},{12,14},{14,12},{1,3},{3,1},... | collective-permute-start | bytes 331784 | tf_op jit(solution)/shard_map/ppermute | solution.py:348
  16.5 3.6 %collective-permute-done.6 = bf16[432,128]{1,0:T(8,128)(2,1)S(1)} collective-permute-done((bf16[432,128]{1,0:T(8,128)(2,1)S(1)}, bf16[432,128]{1,0:T(8,128)(2,1)S(1)}, u32[]{:S(2)}, u32[]{:S(2)}) %collective-permute-start.6) | collective-permute-done | bytes 110624 | tf_op jit(solution)/shard_map/ppermute | solution.py:348
  20.2 0.0 copy-start
  20.2 4.8 %collective-permute-start.7 = (bf16[432,128]{1,0:T(8,128)(2,1)S(1)}, bf16[432,128]{1,0:T(8,128)(2,1)S(1)}, u32[]{:S(2)}, u32[]{:S(2)}) collective-permute-start(bf16[432,128]{1,0:T(8,128)(2,1)S(1)} %add_convert_fusion.1), channel_id=1, source_target_pairs={{0,4},{2,6},{4,0},{6,2},{8,12},{10,14},{12,8},{14,10},{1,5},{3,7},... | collective-permute-start | bytes 331784 | tf_op jit(solution)/shard_map/ppermute | solution.py:348
  25.0 2.9 %collective-permute-done.7 = bf16[432,128]{1,0:T(8,128)(2,1)S(1)} collective-permute-done((bf16[432,128]{1,0:T(8,128)(2,1)S(1)}, bf16[432,128]{1,0:T(8,128)(2,1)S(1)}, u32[]{:S(2)}, u32[]{:S(2)}) %collective-permute-start.7) | collective-permute-done | bytes 110624 | tf_op jit(solution)/shard_map/ppermute | solution.py:348
  27.9 1.9 %collective-permute-start.8 = (bf16[432,128]{1,0:T(8,128)(2,1)S(1)}, bf16[432,128]{1,0:T(8,128)(2,1)S(1)}, u32[]{:S(2)}, u32[]{:S(2)}) collective-permute-start(bf16[432,128]{1,0:T(8,128)(2,1)S(1)} %add_convert_fusion), channel_id=1, source_target_pairs={{0,8},{2,10},{4,12},{6,14},{8,0},{10,2},{12,4},{14,6},{1,9},{3,11}... | collective-permute-start | bytes 331784 | tf_op jit(solution)/shard_map/ppermute | solution.py:348
  29.8 5.4 %collective-permute-done.8 = bf16[432,128]{1,0:T(8,128)(2,1)S(1)} collective-permute-done((bf16[432,128]{1,0:T(8,128)(2,1)S(1)}, bf16[432,128]{1,0:T(8,128)(2,1)S(1)}, u32[]{:S(2)}, u32[]{:S(2)}) %collective-permute-start.8) | collective-permute-done | bytes 110624 | tf_op jit(solution)/shard_map/ppermute | solution.py:348
  35.3 0.1 collective-permute-start.9
  35.4 3.7 %collective-permute-start.3 = (bf16[2,8,512]{2,1,0:T(8,128)(2,1)S(1)}, bf16[2,8,512]{2,1,0:T(8,128)(2,1)S(1)}, u32[]{:S(2)}, u32[]{:S(2)}) collective-permute-start(bf16[2,8,512]{2,1,0:T(8,128)(2,1)S(1)} %get-tuple-element.16), channel_id=1, source_target_pairs={{0,6},{2,8},{4,14},{6,0},{8,2},{14,4},{1,7},{3,9},{5,15},{7,1},{9,... | collective-permute-start | bytes 49160 | tf_op jit(solution)/shard_map/ppermute | solution.py:330
  39.1 1.9 %collective-permute-start.4 = (bf16[2,8,512]{2,1,0:T(8,128)(2,1)S(1)}, bf16[2,8,512]{2,1,0:T(8,128)(2,1)S(1)}, u32[]{:S(2)}, u32[]{:S(2)}) collective-permute-start(bf16[2,8,512]{2,1,0:T(8,128)(2,1)S(1)} %get-tuple-element.17), channel_id=1, source_target_pairs={{0,10},{6,12},{8,14},{10,0},{12,6},{14,8},{1,11},{7,13},{9,15},{11... | collective-permute-start | bytes 49160 | tf_op jit(solution)/shard_map/ppermute | solution.py:330
  41.0 0.0 copy-done
  41.0 0.0 copy-start.2
  41.0 0.0 copy-start.6
  41.0 0.3 weights.1
  41.4 0.5 collective-permute-done.3.refs_3_
  41.9 4.6 %collective-permute-done.4.refs_4_ = bf16[2,8,512]{2,1,0:T(8,128)(2,1)S(1)} collective-permute-done((bf16[2,8,512]{2,1,0:T(8,128)(2,1)S(1)}, bf16[2,8,512]{2,1,0:T(8,128)(2,1)S(1)}, u32[]{:S(2)}, u32[]{:S(2)}) %collective-permute-start.4) | collective-permute-done | bytes 16416 | tf_op jit(solution)/shard_map/ppermute | solution.py:330
  46.5 0.0 copy-done.2
  46.5 0.0 copy-done.6
  46.5 0.0 copy-start.4
  46.5 2.2 %response.1 = bf16[128,512]{1,0:T(8,128)(2,1)} custom-call(s32[8,9]{1,0:T(8,128)S(1)} %copy-done.6, s32[2,6]{1,0:T(2,128)S(1)} %bitcast.15, bf16[2,8,8,512]{3,2,1,0:T(8,128)(2,1)S(1)} %bitcast.10, bf16[9,256,128]{2,1,0:T(8,128)(2,1)S(1)} %get-tuple-element.12.weight_ref, bf16[2,2,8,512]{3,2,1,0:T(8,128)(2,1)S(1)} %collective-permute-done.refs_0_, ...), custom_call_target="tpu_custom_call" | custom-call | flops 301989888 | bytes 1048576 | tf_op jit(solution)/shard_map/response/pallas_call | solution.py:333
  48.7 0.0 copy-done.4
  48.7 2.1 %feature_grad.1 = bf16[128,512]{1,0:T(8,128)(2,1)} custom-call(s32[8,9]{1,0:T(8,128)S(1)} %copy-done.6, s32[2,6]{1,0:T(2,128)S(1)} %bitcast.16, bf16[2,8,8,512]{3,2,1,0:T(8,128)(2,1)S(1)} %bitcast.13, bf16[9,128,256]{2,1,0:T(8,128)(2,1)S(1)} %get-tuple-element.18.weight_ref, bf16[2,2,8,512]{3,2,1,0:T(8,128)(2,1)S(1)} %collective-permute-done.refs_0_, ...), custom_call_target="tpu_custom_call" | custom-call | flops 301989888 | bytes 1048576 | tf_op jit(solution)/shard_map/feature_grad/pallas_call | solution.py:333
  50.8 0.0 collective-permute-done.9.other_ref
  50.8 1.2 %unpack.1 = f32[9,192,64]{2,1,0:T(8,128)} custom-call(f32[432,128]{1,0:T(8,128)S(1)} %convert_add_fusion.own_ref, f32[432,128]{1,0:T(8,128)S(1)} %collective-permute-done.9.other_ref), custom_call_target="tpu_custom_call" | custom-call | bytes 1048576 | tf_op jit(solution)/shard_map/unpack/pallas_call | solution.py:352
  (4 shorter events, 0.1 us)
Async XLA Ops:
  0.6 0.9 %copy-start.1 = (bf16[1,2,8,8,512]{4,3,2,1,0:T(8,128)(2,1)S(1)}, bf16[1,2,8,8,512]{4,3,2,1,0:T(8,128)(2,1)}, u32[]{:S(2)}) copy-start(bf16[1,2,8,8,512]{4,3,2,1,0:T(8,128)(2,1)} %param.5) | copy-start | bytes 393220
  1.5 0.9 %copy-start.3 = (bf16[1,2,8,8,512]{4,3,2,1,0:T(8,128)(2,1)S(1)}, bf16[1,2,8,8,512]{4,3,2,1,0:T(8,128)(2,1)}, u32[]{:S(2)}) copy-start(bf16[1,2,8,8,512]{4,3,2,1,0:T(8,128)(2,1)} %param.6) | copy-start | bytes 393220
  2.4 0.7 %copy-start.5 = (s32[8,9]{1,0:T(8,128)S(1)}, s32[8,9]{1,0:T(8,128)}, u32[]{:S(2)}) copy-start(s32[8,9]{1,0:T(8,128)} %constant.2.clone.table_ref) | copy-start | bytes 868
  3.9 7.8 %collective-permute-start = (bf16[2,2,8,512]{3,2,1,0:T(8,128)(2,1)S(1)}, bf16[2,2,8,512]{3,2,1,0:T(8,128)(2,1)S(1)}, u32[]{:S(2)}, u32[]{:S(2)}) collective-permute-start(bf16[2,2,8,512]{3,2,1,0:T(8,128)(2,1)S(1)} %get-tuple-element.13), channel_id=1, source_target_pairs={{0,8},{2,10},{4,12},{6,14},{8,0},{10,2},{12,4},{14,6},{1,9},{3,11}... | collective-permute-start | bytes 98312 | tf_op jit(solution)/shard_map/ppermute | solution.py:305
  8.0 3.7 %collective-permute-start.1 = (bf16[2,8,512]{2,1,0:T(8,128)(2,1)S(1)}, bf16[2,8,512]{2,1,0:T(8,128)(2,1)S(1)}, u32[]{:S(2)}, u32[]{:S(2)}) collective-permute-start(bf16[2,8,512]{2,1,0:T(8,128)(2,1)S(1)} %get-tuple-element.14), channel_id=1, source_target_pairs={{0,2},{2,0},{4,6},{6,4},{8,10},{10,8},{12,14},{14,12},{1,3},{3,1},... | collective-permute-start | bytes 49160 | tf_op jit(solution)/shard_map/ppermute | solution.py:305
  9.5 2.3 %copy-start.7 = (s32[1,2,6]{2,1,0:T(2,128)S(1)}, s32[1,2,6]{2,1,0:T(2,128)}, u32[]{:S(2)}) copy-start(s32[1,2,6]{2,1,0:T(2,128)} %param.8) | copy-start | bytes 148
  9.5 2.2 %collective-permute-start.2 = (bf16[2,8,512]{2,1,0:T(8,128)(2,1)S(1)}, bf16[2,8,512]{2,1,0:T(8,128)(2,1)S(1)}, u32[]{:S(2)}, u32[]{:S(2)}) collective-permute-start(bf16[2,8,512]{2,1,0:T(8,128)(2,1)S(1)} %get-tuple-element.15), channel_id=1, source_target_pairs={{6,8},{8,6},{7,9},{9,7},{22,24},{24,22},{23,25},{25,23}} | collective-permute-start | bytes 49160 | tf_op jit(solution)/shard_map/ppermute | solution.py:305
  13.4 1.5 %collective-permute-start.5 = (f32[432,128]{1,0:T(8,128)S(1)}, f32[432,128]{1,0:T(8,128)S(1)}, u32[]{:S(2)}, u32[]{:S(2)}) collective-permute-start(f32[432,128]{1,0:T(8,128)S(1)} %get-tuple-element.20), channel_id=1, source_target_pairs={{0,1},{1,0},{2,3},{3,2},{4,5},{5,4},{6,7},{7,6},{8,9},{9,8},{10,11... | collective-permute-start | bytes 663560 | tf_op jit(solution)/shard_map/ppermute | solution.py:329
  15.0 5.2 %collective-permute-start.6 = (bf16[432,128]{1,0:T(8,128)(2,1)S(1)}, bf16[432,128]{1,0:T(8,128)(2,1)S(1)}, u32[]{:S(2)}, u32[]{:S(2)}) collective-permute-start(bf16[432,128]{1,0:T(8,128)(2,1)S(1)} %add_convert_fusion.2), channel_id=1, source_target_pairs={{0,2},{2,0},{4,6},{6,4},{8,10},{10,8},{12,14},{14,12},{1,3},{3,1},... | collective-permute-start | bytes 331784 | tf_op jit(solution)/shard_map/ppermute | solution.py:348
  20.2 20.8 %copy-start = (bf16[3,3,3,64,64]{4,3,2,1,0:T(8,128)(2,1)S(1)}, bf16[3,3,3,64,64]{4,3,2,1,0:T(8,128)(2,1)}, u32[]{:S(2)}) copy-start(bf16[3,3,3,64,64]{4,3,2,1,0:T(8,128)(2,1)} %param.7) | copy-start | bytes 663556
  20.2 7.7 %collective-permute-start.7 = (bf16[432,128]{1,0:T(8,128)(2,1)S(1)}, bf16[432,128]{1,0:T(8,128)(2,1)S(1)}, u32[]{:S(2)}, u32[]{:S(2)}) collective-permute-start(bf16[432,128]{1,0:T(8,128)(2,1)S(1)} %add_convert_fusion.1), channel_id=1, source_target_pairs={{0,4},{2,6},{4,0},{6,2},{8,12},{10,14},{12,8},{14,10},{1,5},{3,7},... | collective-permute-start | bytes 331784 | tf_op jit(solution)/shard_map/ppermute | solution.py:348
  27.9 7.3 %collective-permute-start.8 = (bf16[432,128]{1,0:T(8,128)(2,1)S(1)}, bf16[432,128]{1,0:T(8,128)(2,1)S(1)}, u32[]{:S(2)}, u32[]{:S(2)}) collective-permute-start(bf16[432,128]{1,0:T(8,128)(2,1)S(1)} %add_convert_fusion), channel_id=1, source_target_pairs={{0,8},{2,10},{4,12},{6,14},{8,0},{10,2},{12,4},{14,6},{1,9},{3,11}... | collective-permute-start | bytes 331784 | tf_op jit(solution)/shard_map/ppermute | solution.py:348
  35.3 15.5 %collective-permute-start.9 = (f32[432,128]{1,0:T(8,128)S(1)}, f32[432,128]{1,0:T(8,128)S(1)}, u32[]{:S(2)}, u32[]{:S(2)}) collective-permute-start(f32[432,128]{1,0:T(8,128)S(1)} %convert_add_fusion.own_ref), channel_id=1, source_target_pairs={{0,1},{1,0},{2,3},{3,2},{4,5},{5,4},{6,7},{7,6},{8,9},{9,8},{10,11... | collective-permute-start | bytes 663560 | tf_op jit(solution)/shard_map/ppermute | solution.py:350
  35.4 6.5 %collective-permute-start.3 = (bf16[2,8,512]{2,1,0:T(8,128)(2,1)S(1)}, bf16[2,8,512]{2,1,0:T(8,128)(2,1)S(1)}, u32[]{:S(2)}, u32[]{:S(2)}) collective-permute-start(bf16[2,8,512]{2,1,0:T(8,128)(2,1)S(1)} %get-tuple-element.16), channel_id=1, source_target_pairs={{0,6},{2,8},{4,14},{6,0},{8,2},{14,4},{1,7},{3,9},{5,15},{7,1},{9,... | collective-permute-start | bytes 49160 | tf_op jit(solution)/shard_map/ppermute | solution.py:330
  39.1 7.4 %collective-permute-start.4 = (bf16[2,8,512]{2,1,0:T(8,128)(2,1)S(1)}, bf16[2,8,512]{2,1,0:T(8,128)(2,1)S(1)}, u32[]{:S(2)}, u32[]{:S(2)}) collective-permute-start(bf16[2,8,512]{2,1,0:T(8,128)(2,1)S(1)} %get-tuple-element.17), channel_id=1, source_target_pairs={{0,10},{6,12},{8,14},{10,0},{12,6},{14,8},{1,11},{7,13},{9,15},{11... | collective-permute-start | bytes 49160 | tf_op jit(solution)/shard_map/ppermute | solution.py:330
  41.0 5.5 %copy-start.2 = (bf16[1,2,8,8,512]{4,3,2,1,0:T(8,128)(2,1)S(1)}, bf16[1,2,8,8,512]{4,3,2,1,0:T(8,128)(2,1)}, u32[]{:S(2)}) copy-start(bf16[1,2,8,8,512]{4,3,2,1,0:T(8,128)(2,1)} %param.5) | copy-start | bytes 393220
  41.0 5.5 %copy-start.6 = (s32[8,9]{1,0:T(8,128)S(1)}, s32[8,9]{1,0:T(8,128)}, u32[]{:S(2)}) copy-start(s32[8,9]{1,0:T(8,128)} %constant.2.clone.table_ref) | copy-start | bytes 868
  46.5 2.2 %copy-start.4 = (bf16[1,2,8,8,512]{4,3,2,1,0:T(8,128)(2,1)S(1)}, bf16[1,2,8,8,512]{4,3,2,1,0:T(8,128)(2,1)}, u32[]{:S(2)}) copy-start(bf16[1,2,8,8,512]{4,3,2,1,0:T(8,128)(2,1)} %param.6) | copy-start | bytes 393220

commit v2 on v1

v2 whole, which is shorter than its diff:
```python
import functools
import math

import jax
import jax.numpy as jnp
from jax import lax
from jax.experimental import pallas as pl
from jax.experimental.pallas import tpu as pltpu
from jax.sharding import PartitionSpec as P

TILES_Y = 4
F32 = jnp.float32
BF16 = jnp.bfloat16


def step_y(tile, sign, tiles):
    column = (tile + TILES_Y // 2) % TILES_Y + sign
    near = tile + sign
    return near if 0 <= column < TILES_Y and 0 <= near < tiles else None


def step_x(tile, sign, tiles):
    near = tile + sign * TILES_Y
    return near if 0 <= near < tiles else None


def rounds(edges):
    found = []
    for low, high in edges:
        for one in found:
            if low not in one and high not in one:
                break
        else:
            one = {}
            found.append(one)
        one[low] = (high, 1)
        one[high] = (low, 0)
    return found


def detours(tiles):
    found = []
    for tile in range(tiles):
        for across in range(2):
            for along in range(2):
                sender = step_y(tile, 2 * along - 1, tiles)
                if sender is None or step_x(sender, 2 * across - 1, tiles) is None:
                    continue
                if step_x(tile, 2 * across - 1, tiles) is not None:
                    continue
                for one in found:
                    if all(hop[0] != sender and hop[1] != tile for hop in one):
                        break
                else:
                    one = []
                    found.append(one)
                one.append((sender, tile, across, along))
    return found


def make_plan(tiles):
    def edges(step):
        return [(tile, step(tile, 1, tiles)) for tile in range(tiles) if step(tile, 1, tiles) is not None]

    along_x, along_y, hops = rounds(edges(step_x)), rounds(edges(step_y)), detours(tiles)
    pairs = [[[(tile, one[tile][0]) for tile in sorted(one)] for one in kind] for kind in (along_x, along_y)]
    pairs.append([[hop[:2] for hop in one] for one in hops])
    roles = [[{tile: one[tile][1] for tile in one} for one in kind] for kind in (along_x, along_y)]
    roles.append([{hop[0]: (hop[2], 1 - hop[3]) for hop in one} for one in hops])
    roles.append([{hop[1]: hop[2:] for hop in one} for one in hops])
    return pairs, roles


class Roles:
    def __init__(self, roles, tiles):
        self.roles, self.tiles = roles, tiles
        self.counts = [len(kind) for kind in roles[:3]]
        self.tile = lax.axis_index("space")

    def any(self, kind, number, test):
        words = []
        for start in range(0, self.tiles, 32):
            here = [t for t in range(start, min(start + 32, self.tiles)) if t in self.roles[kind][number]]
            word = sum(1 << (t - start) for t in here if test(self.roles[kind][number][t]))
            words.append(word - (1 << 32) if word >> 31 else word)
        word = jnp.int32(words[0])
        for number, other in enumerate(words[1:], 1):
            word = jnp.where(self.tile // 32 == number, jnp.int32(other), word)
        return (lax.shift_right_logical(word, self.tile % 32) & 1) == 1

    def side(self, kind, number, side):
        return self.any(kind, number, lambda role: role == side)

    def linked(self, side):
        found = jnp.bool_(False)
        for number in range(self.counts[1]):
            found = found | self.side(1, number, side)
        return found


def masked(keep, x):
    return jnp.where(keep, x, jnp.zeros_like(x))


def faces_kernel(roles, tiles, f_hbm, c_hbm, link_hbm, *refs):
    roles = Roles(roles, tiles)
    counts = roles.counts
    x_refs = refs[: counts[0]]
    y_refs = refs[counts[0] : counts[0] + counts[1]]
    f_ref, c_ref, link_ref, arrived = refs[counts[0] + counts[1] :]
    copies = [
        pltpu.make_async_copy(f_hbm, f_ref, arrived.at[0]),
        pltpu.make_async_copy(c_hbm, c_ref, arrived.at[1]),
        pltpu.make_async_copy(link_hbm, link_ref, arrived.at[2]),
    ]
    for copy in copies:
        copy.start()
    for copy in copies:
        copy.wait()
    edge = f_ref.shape[1]
    linked = [[link_ref[brick, way] >= 0 for way in range(4)] for brick in range(2)]
    for number, out in enumerate(x_refs):
        up = roles.side(0, number, 1)
        plane = jnp.where(up, edge - 1, 0)
        for brick in range(2):
            keep = jnp.where(up, linked[brick][1], linked[brick][0])
            for source, ref in enumerate((f_ref, c_ref)):
                out[source, brick] = masked(keep, ref[brick, plane])
    rows = []
    for ref in (f_ref, c_ref):
        low = ref[0].astype(F32)[:, 0, :]
        high = ref[1].astype(F32)[:, edge - 1, :]
        rows.append((low, high))
    for number, out in enumerate(y_refs):
        up = roles.side(1, number, 1)
        keep = jnp.where(up, linked[1][3], linked[0][2])
        for source, (low, high) in enumerate(rows):
            out[source] = masked(keep, jnp.where(up, high, low)).astype(BF16)


def padded(x, channels):
    zeros = jnp.zeros(x.shape[:-1] + (2 * channels,), F32)
    return pltpu.roll(jnp.concatenate([x, zeros], axis=-1), channels, x.ndim - 1)


def weights_kernel(kernel_ref, forward_ref, backward_ref, wide):
    channels = kernel_ref.shape[-1]
    wide[...] = jnp.zeros_like(wide)
    wide[:, :, :channels] = kernel_ref[...].astype(F32)
    for tap in range(9):
        plain = [wide[3 * tap + d] for d in range(3)]
        moved = [pltpu.roll(x, channels, 1) for x in plain]
        steps = (plain[0], plain[1] + moved[0], plain[2] + moved[1], moved[2])
        for number, block in enumerate(steps):
            forward_ref[tap, channels * number : channels * (number + 1), :] = block.astype(BF16)
        last = 8 - tap
        lanes = 2 * channels
        backward_ref[last, :channels, :lanes] = (plain[2] + moved[1]).astype(BF16)
        backward_ref[last, :channels, lanes:] = plain[0].astype(BF16)
        backward_ref[last, channels:, :lanes] = moved[2].astype(BF16)
        backward_ref[last, channels:, lanes:] = (plain[1] + moved[0]).astype(BF16)


def store_line(lines, number, line):
    lanes = lines.shape[1]
    each = line.shape[1] // lanes
    for k in range(each):
        lines[each * number + k : each * number + k + 1, :] = line[:, lanes * k : lanes * (k + 1)]


def load_line(rows, number, each):
    return jnp.concatenate([rows[each * number + k : each * number + k + 1] for k in range(each)], axis=1)


def kernel_grad_kernel(roles, tiles, channels, f_ref, c_ref, *refs):
    roles = Roles(roles, tiles)
    counts = roles.counts
    x_refs = refs[: counts[0]]
    y_refs = refs[counts[0] : counts[0] + counts[1]]
    near = counts[0] + counts[1]
    keep_ref, send_ref = refs[near : near + 2]
    line_refs = refs[near + 2 : near + 2 + counts[0]]
    hop_refs = refs[near + 2 + counts[0] : near + 2 + counts[0] + counts[2]]
    wide, tall, packed, lines = refs[near + 2 + counts[0] + counts[2] :]
    bricks, edge, _, width = f_ref.shape
    rows = edge * edge
    wide[:, edge : edge + rows, :] = padded(f_ref[...].astype(F32).reshape(bricks, rows, width), channels)
    planes = []
    for side in range(2):
        start = side * (edge + rows)
        plane = jnp.zeros((bricks, edge, width), F32)
        for number, ref in enumerate(x_refs):
            plane = jnp.where(roles.side(0, number, side), ref[0].astype(F32), plane)
        planes.append(plane)
        plane = padded(plane, channels)
        for brick in range(bricks):
            wide[brick, start : start + edge, :] = plane[brick]
    own = c_ref[...].astype(F32)
    tall[:, :, edge : 2 * edge, :] = own
    tall[1, :, edge - 1 : edge, :] = own[0, :, edge - 1 :, :]
    tall[0, :, 2 * edge : 2 * edge + 1, :] = own[1, :, 0:1, :]
    halo = {}
    for side in range(2):
        for source in range(2):
            row = jnp.zeros((edge, width), F32)
            for number, ref in enumerate(y_refs):
                row = jnp.where(roles.side(1, number, side), ref[source].astype(F32), row)
            halo[source, side] = row
        at = 2 * edge if side else edge - 1
        tall[side, :, at : at + 1, :] = halo[1, side][:, None, :]
    lanes = 2 * channels
    pairs = width // lanes
    right = []
    for col in range(3):
        value = tall[:, :, edge + 1 - col : 2 * edge + 1 - col, :].reshape(bricks * rows, width).astype(BF16)
        right.append(jnp.concatenate([value[:, lanes * k : lanes * (k + 1)] for k in range(pairs)], axis=0))
    right = jnp.concatenate(right, axis=1)
    low = lax.broadcasted_iota(jnp.int32, (3 * channels // 2, lanes), 1) < channels
    half = 3 * channels // 2
    for row in range(3):
        value = wide[:, edge * row : edge * row + rows, :].reshape(bricks * rows, -1).astype(BF16)
        left = jnp.concatenate([value[:, lanes * k : lanes * (k + 2)] for k in range(pairs)], axis=0)
        grad = lax.dot_general(left, right, (((0,), (0,)), ((), ())), preferred_element_type=F32)
        for col in range(3):
            block = grad[:, lanes * col : lanes * (col + 1)]
            moved = pltpu.roll(block, channels, 1)
            first = block[:half] + moved[channels : channels + half]
            second = moved[half : 2 * half] + block[channels + half :]
            at = half * (3 * row + col)
            packed[at : at + half, :] = jnp.where(low, first, second)
    for number, out in enumerate(line_refs):
        up = roles.side(0, number, 1)
        for (source, side), row in halo.items():
            store_line(lines, 2 * source + side, jnp.where(up, row[edge - 1 : edge], row[0:1]))
        out[...] = lines[...].astype(BF16)
    for number, out in enumerate(hop_refs):
        line = jnp.zeros((1, width), F32)
        for across in range(2):
            for side in range(2):
                at = (edge - 1) * side
                hit = roles.any(2, number, lambda role: role == (across, side))
                line = jnp.where(hit, planes[across][side, at : at + 1, :], line)
        store_line(lines, 0, line)
        out[...] = lines[...].astype(BF16)
    count = keep_ref.shape[0]
    core = lax.axis_index("dp")
    keep_ref[...] = packed[pl.ds(pl.multiple_of(core * count, 8), count), :]
    send_ref[...] = packed[pl.ds(pl.multiple_of((1 - core) * count, 8), count), :]


def conv_kernel(roles, tiles, channels, source, v_ref, *refs):
    roles = Roles(roles, tiles)
    counts = roles.counts
    x_refs = refs[: counts[0]]
    y_refs = refs[counts[0] : counts[0] + counts[1]]
    near = counts[0] + counts[1]
    line_refs = refs[near : near + counts[0]]
    hop_refs = refs[near + counts[0] : near + counts[0] + counts[2]]
    weight_ref, out_ref, ext = refs[near + counts[0] + counts[2] :]
    bricks, edge, _, width = v_ref.shape
    rows = edge * edge
    first, last = edge, 2 * edge - 1
    ext[:, 1 : edge + 1, first : last + 1, :] = padded(v_ref[...].astype(F32), channels)
    for side in range(2):
        plane = jnp.zeros((bricks, edge, width), F32)
        for number, ref in enumerate(x_refs):
            plane = jnp.where(roles.side(0, number, side), ref[source].astype(F32), plane)
        plane = padded(plane, channels)
        for brick in range(bricks):
            ext[brick, side * (edge + 1), first : last + 1, :] = plane[brick]
    each = width // line_refs[0].shape[1]
    arrived = [ref[ref.shape[0] - 4 * each :, :].astype(F32) for ref in line_refs]
    hops = [load_line(ref[...].astype(F32), 0, each) for ref in hop_refs]
    for side in range(2):
        row = jnp.zeros((edge, width), F32)
        for number, ref in enumerate(y_refs):
            row = jnp.where(roles.side(1, number, side), ref[source].astype(F32), row)
        at = last + 1 if side else first - 1
        row = padded(row, channels)
        ext[side, 1 : edge + 1, at : at + 1, :] = row[:, None, :]
        for across in range(2):
            line = jnp.zeros((1, width), F32)
            for number, value in enumerate(arrived):
                line = jnp.where(roles.side(0, number, across), load_line(value, 2 * source + side, each), line)
            if source == 0:
                line = masked(roles.linked(side), line)
                for number, value in enumerate(hops):
                    line = jnp.where(roles.any(3, number, lambda role: role == (across, side)), value, line)
            ext[side, across * (edge + 1), at : at + 1, :] = padded(line, channels)
    ext[1, :, first - 1 : first, :] = ext[0, :, last : last + 1, :]
    ext[0, :, last + 1 : last + 2, :] = ext[1, :, first : first + 1, :]
    lanes = 2 * channels
    pairs = width // lanes
    total = jnp.zeros((pairs * bricks * rows, lanes), F32)
    contract = 0 if source == 0 else 1
    for col in range(3):
        for row in range(3):
            value = ext[:, row : row + edge, first - 1 + col : last + col, :]
            value = value.reshape(bricks * rows, -1).astype(BF16)
            left = jnp.concatenate([value[:, lanes * k : lanes * (k + 2)] for k in range(pairs)], axis=0)
            total = total + lax.dot_general(
                left, weight_ref[3 * row + col], (((1,), (contract,)), ((), ())), preferred_element_type=F32
            )
    for k in range(pairs):
        out_ref[:, lanes * k : lanes * (k + 1)] = total[bricks * rows * k : bricks * rows * (k + 1)].astype(BF16)


def unpack_kernel(factor, own_ref, other_ref, out_ref, packed):
    count = own_ref.shape[0]
    core = lax.axis_index("dp")
    packed[pl.ds(pl.multiple_of(core * count, 8), count), :] = own_ref[...] * factor
    packed[pl.ds(pl.multiple_of((1 - core) * count, 8), count), :] = other_ref[...] * factor
    taps, rows, channels = out_ref.shape
    half = rows // 2
    for tap in range(taps):
        block = packed[half * tap : half * (tap + 1), :]
        out_ref[tap, :half, :] = block[:, :channels]
        out_ref[tap, half:, :] = pltpu.roll(block, channels, 1)[:, :channels]


VMEM = pl.BlockSpec(memory_space=pltpu.VMEM)
HBM = pl.BlockSpec(memory_space=pltpu.HBM)


def call(kernel, in_specs, out_shapes, scratch=(), flops=0, name=None, vmem=24 * 2**20):
    several = isinstance(out_shapes, list)
    return pl.pallas_call(
        kernel,
        in_specs=in_specs,
        out_specs=[VMEM] * len(out_shapes) if several else VMEM,
        out_shape=out_shapes,
        scratch_shapes=list(scratch),
        compiler_params=pltpu.CompilerParams(vmem_limit_bytes=vmem),
        cost_estimate=pl.CostEstimate(flops=flops, bytes_accessed=2**20, transcendentals=0),
        name=name,
    )


def body(tiles, features, cotangent, kernel, neighbours):
    pairs, roles = make_plan(tiles)
    counts = [len(kind) for kind in pairs]
    bricks, edge = features.shape[1:3]
    width = features.shape[-1]
    channels = kernel.shape[-1]
    rows = edge * edge
    lanes = 2 * channels
    shape = jax.ShapeDtypeStruct
    f = features.reshape(bricks, edge, edge, width)
    c = cotangent.reshape(bricks, edge, edge, width)
    links = neighbours.reshape(bricks, 6)

    near = counts[0] + counts[1]
    face_shapes = [(2, bricks, edge, width)] * counts[0] + [(2, edge, width)] * counts[1]
    faces = call(
        functools.partial(faces_kernel, roles, tiles),
        [HBM, HBM, HBM],
        [shape(s, BF16) for s in face_shapes],
        [
            pltpu.VMEM(f.shape, BF16),
            pltpu.VMEM(c.shape, BF16),
            pltpu.SMEM(links.shape, jnp.int32),
            pltpu.SemaphoreType.DMA((3,)),
        ],
        name="faces",
        vmem=None,
    )(f, c, links)
    got = [lax.ppermute(x, "space", one) for x, one in zip(faces, pairs[0] + pairs[1])]
    count = 27 * channels * channels // lanes // 2
    line_rows = 4 * width // lanes
    keep, send, *lines = call(
        functools.partial(kernel_grad_kernel, roles, tiles, channels),
        [VMEM, VMEM] + [VMEM] * near,
        [shape((count, lanes), F32)] * 2 + [shape((line_rows, lanes), BF16)] * (counts[0] + counts[2]),
        [
            pltpu.VMEM((bricks, rows + 2 * edge, width + lanes), F32),
            pltpu.VMEM((bricks, edge, 3 * edge, width), F32),
            pltpu.VMEM((2 * count, lanes), F32),
            pltpu.VMEM((line_rows, lanes), F32),
        ],
        flops=2 * 768 * 384 * 512,
        name="kernel_grad",
    )(f, c, *got)

    forward, backward = call(
        weights_kernel,
        [VMEM],
        [shape((9, 4 * channels, lanes), BF16), shape((9, lanes, 4 * channels), BF16)],
        [pltpu.VMEM((27, channels, lanes), F32)],
        name="weights",
    )(kernel.reshape(27, channels, channels))

    def conv(source, x, weight):
        return call(
            functools.partial(conv_kernel, roles, tiles, channels, source),
            [VMEM] * (2 + len(got)),
            shape((bricks * rows, width), BF16),
            [pltpu.VMEM((bricks, edge + 2, 3 * edge, width + lanes), F32)],
            flops=2 * 512 * 256 * 128 * 9,
            name="response" if source == 0 else "feature_grad",
        )(x, *got, weight)

    swap = [(0, 1), (1, 0)]
    part = keep + lax.ppermute(send, "dp", swap)
    steps = [[(i, i ^ (1 << bit)) for i in range(tiles)] for bit in range(tiles.bit_length() - 1)]
    wire = BF16 if len(steps) <= 3 else F32
    joined = len(pairs[0]) == 1 and pairs[0][0] in steps and wire == BF16
    if joined:
        steps.sort(key=lambda step: step != pairs[0][0])
    hops = [lax.ppermute(x, "space", one) for x, one in zip(lines[counts[0] :], pairs[2])]
    lines = lines[: counts[0]]
    if not joined:
        got += [lax.ppermute(x, "space", one) for x, one in zip(lines, pairs[0])]
    for number, step in enumerate(steps):
        mine = part.astype(wire)
        if number == 0 and joined:
            mine = lax.optimization_barrier(jnp.concatenate([mine, lines[0]], axis=0))
        if number == 1:
            mine, hops, forward, backward = lax.optimization_barrier((mine, hops, forward, backward))
            got += hops
            response = conv(0, f, forward)
            feature_grad = conv(1, c, backward)
        elif number == 2:
            mine, response = lax.optimization_barrier((mine, response))
        else:
            mine = lax.optimization_barrier(mine)
        theirs = lax.ppermute(mine, "space", step)
        if number == 0 and joined:
            got.append(theirs)
            mine, theirs = mine[:count], theirs[:count]
        part = mine.astype(F32) + theirs.astype(F32)
    part, feature_grad = lax.optimization_barrier((part, feature_grad))
    response, feature_grad = (x.reshape(features.shape) for x in (response, feature_grad))
    other = lax.ppermute(part, "dp", swap)
    cells = bricks * tiles * lax.axis_size("dp") * edge**3
    kernel_grad = call(
        functools.partial(unpack_kernel, 1.0 / math.sqrt(cells)),
        [VMEM, VMEM],
        shape((9, 3 * channels, channels), F32),
        [pltpu.VMEM((2 * count, lanes), F32)],
        name="unpack",
    )(part, other).reshape(kernel.shape)
    return response, feature_grad, kernel_grad


def solution(mesh):
    bricks_spec = P(("groups", "dp"), "space", None, None, None)
    return jax.shard_map(
        functools.partial(body, mesh.shape["space"]),
        mesh=mesh,
        in_specs=(bricks_spec, bricks_spec, P(), P(("groups", "dp"), "space", None)),
        out_specs=(bricks_spec, bricks_spec, P("groups", None, None, None, None)),
        check_vma=False,
    )
```

time: 52.2 us -> 35.7 us (0.68)
  starting transfers between devices: 20.4 us -> 13 us
  waiting for transfers between devices: 19.9 us -> 14.2 us
  local copies, waits for them, and re-layouts: 2.52 us -> 0.01 us
  Pallas kernels: 8.22 us -> 7.39 us
    ppermute x5 -> x4, starting transfers between devices: 12 us -> 6.9 us  [body(): lax.ppermute(x, 'space', one)]
    ppermute x5 -> x4, waiting for transfers between devices: 6.57 us -> 1.81 us  [body(): lax.ppermute(x, 'space', one)]
    unnamed x16 -> x6, local copies, waits for them, and re-layouts: 2.52 us -> 0.01 us
    ppermute x3, waiting for transfers between devices: 11.9 us -> 9.46 us  [body(): theirs = lax.ppermute(mine, 'space', step)]
    ppermute x3, starting transfers between devices: 8.31 us -> 5.98 us  [body(): theirs = lax.ppermute(mine, 'space', step)]
    ppermute x1, waiting for transfers between devices: 0.01 us -> 1.46 us  [body(): other = lax.ppermute(part, 'dp', swap)]
    pallas_call x4, Pallas kernels: 6.72 us -> 5.89 us  [the longest x2 3.05 us: conv(): call(functools.partial(conv_kernel, roles, tiles, channels, source), [VME...]
  transfers between devices with their start and end apart: 10 -> 9, of which waited for: 7 -> 6; matrix products, arithmetic and copies ran while one was open for 0% -> 0% of each run, Pallas kernels for 9% -> 10%
where the time goes in v2:
time: 35.7 us; the launch traced here: 35.5 us
  waiting for transfers between devices  14.2 us (40%)
  starting transfers between devices  13 us (36%)
  Pallas kernels  7.39 us (21%)
  between operations  0.76 us (2%)
    ppermute x3, waiting for transfers between devices, body(): theirs = lax.ppermute(mine, 'space', step)  9.46 us
    ppermute x4, starting transfers between devices, body(): lax.ppermute(x, 'space', one)  6.9 us
    ppermute x3, starting transfers between devices, body(): theirs = lax.ppermute(mine, 'space', step)  5.98 us
    pallas_call x2, Pallas kernels, conv(): call(functools.partial(conv_kernel, roles, tiles, channels, source), [VME...  3.05 us
    ppermute x4, waiting for transfers between devices, body(): lax.ppermute(x, 'space', one)  1.81 us
    pallas_call x1, Pallas kernels, body(): call(functools.partial(faces_kernel, roles, tiles), [HBM, HBM, HBM], [sha...  1.79 us
    ppermute x1, waiting for transfers between devices, body(): part = keep + lax.ppermute(send, 'dp', swap)  1.46 us
    ppermute x1, waiting for transfers between devices, body(): other = lax.ppermute(part, 'dp', swap)  1.46 us
  transfers between devices with their start and end apart: 9, of which 6 were waited for; matrix products, arithmetic and copies ran while one was open for 0% of the time, Pallas kernels for 10%

profile of v2, /device:TPU:0, one launch (start us, length us, event | category | flops | bytes accessed | tf_op | source)
XLA Modules:
  0.0 35.5 jit_solution(6572555685846153131)
XLA Ops:
  0.6 0.0 copy-start.1
  0.6 0.0 copy-start.2
  0.7 1.8 %faces.1 = (bf16[2,2,8,512]{3,2,1,0:T(8,128)(2,1)}, bf16[2,8,512]{2,1,0:T(8,128)(2,1)}, bf16[2,8,512]{2,1,0:T(8,128)(2,1)}) custom-call(bf16[2,8,8,512]{3,2,1,0:T(8,128)(2,1)} %bitcast.8, bf16[2,8,8,512]{3,2,1,0:T(8,128)(2,1)} %bitcast.11, s32[2,6]{1,0:T(2,128)} %bitcast.15), custom_call_target="tpu_custom_call" | custom-call | bytes 1048576 | tf_op jit(solution)/shard_map/faces/pallas_call | solution.py:354
  2.4 4.1 %collective-permute-start = (bf16[2,2,8,512]{3,2,1,0:T(8,128)(2,1)}, bf16[2,2,8,512]{3,2,1,0:T(8,128)(2,1)S(1)}, u32[]{:S(2)}, u32[]{:S(2)}) collective-permute-start(bf16[2,2,8,512]{3,2,1,0:T(8,128)(2,1)} %get-tuple-element.20), channel_id=1, source_target_pairs={{0,8},{2,10},{4,12},{6,14},{8,0},{10,2},{12,4},{14,6},{1,9},{3,11}... | collective-permute-start | bytes 98312 | tf_op jit(solution)/shard_map/ppermute | solution.py:367
  6.5 1.5 %collective-permute-start.1 = (bf16[2,8,512]{2,1,0:T(8,128)(2,1)}, bf16[2,8,512]{2,1,0:T(8,128)(2,1)S(1)}, u32[]{:S(2)}, u32[]{:S(2)}) collective-permute-start(bf16[2,8,512]{2,1,0:T(8,128)(2,1)} %get-tuple-element.21), channel_id=1, source_target_pairs={{0,2},{2,0},{4,6},{6,4},{8,10},{10,8},{12,14},{14,12},{1,3},{3,1},... | collective-permute-start | bytes 49160 | tf_op jit(solution)/shard_map/ppermute | solution.py:367
  8.0 0.7 %collective-permute-start.2 = (bf16[2,8,512]{2,1,0:T(8,128)(2,1)}, bf16[2,8,512]{2,1,0:T(8,128)(2,1)S(1)}, u32[]{:S(2)}, u32[]{:S(2)}) collective-permute-start(bf16[2,8,512]{2,1,0:T(8,128)(2,1)} %get-tuple-element.22), channel_id=1, source_target_pairs={{6,8},{8,6},{7,9},{9,7},{22,24},{24,22},{23,25},{25,23}} | collective-permute-start | bytes 49160 | tf_op jit(solution)/shard_map/ppermute | solution.py:367
  8.7 1.8 %collective-permute-done.1.refs_1_ = bf16[2,8,512]{2,1,0:T(8,128)(2,1)S(1)} collective-permute-done((bf16[2,8,512]{2,1,0:T(8,128)(2,1)}, bf16[2,8,512]{2,1,0:T(8,128)(2,1)S(1)}, u32[]{:S(2)}, u32[]{:S(2)}) %collective-permute-start.1) | collective-permute-done | bytes 16416 | tf_op jit(solution)/shard_map/ppermute | solution.py:367
  10.5 0.0 collective-permute-done.2.refs_2_
  10.5 0.0 collective-permute-done.refs_0_
  10.5 0.0 copy-done.1
  10.5 0.0 copy-done.2
  10.5 1.1 %kernel_grad.1 = (f32[432,128]{1,0:T(8,128)S(1)}, f32[432,128]{1,0:T(8,128)S(1)}, bf16[16,128]{1,0:T(8,128)(2,1)S(1)}, bf16[16,128]{1,0:T(8,128)(2,1)S(1)}) custom-call(bf16[2,8,8,512]{3,2,1,0:T(8,128)(2,1)S(1)} %bitcast.9, bf16[2,8,8,512]{3,2,1,0:T(8,128)(2,1)S(1)} %bitcast.12, bf16[2,2,8,512]{3,2,1,0:T(8,128)(2,1)S(1)} %collective-permute-done.refs_0_, ...), custom_call_target="tpu_custom_call" | custom-call | flops 301989888 | bytes 1048576 | tf_op jit(solution)/shard_map/kernel_grad/pallas_call | solution.py:370
  11.6 0.0 copy-start
  11.6 0.1 collective-permute-start.3
  11.7 1.5 %collective-permute-done.3 = f32[432,128]{1,0:T(8,128)S(1)} collective-permute-done((f32[432,128]{1,0:T(8,128)S(1)}, f32[432,128]{1,0:T(8,128)S(1)}, u32[]{:S(2)}, u32[]{:S(2)}) %collective-permute-start.3) | collective-permute-done | bytes 221216 | tf_op jit(solution)/shard_map/ppermute | solution.py:403
  13.2 4.7 %collective-permute-start.4 = (bf16[448,128]{1,0:T(8,128)(2,1)S(1)}, bf16[448,128]{1,0:T(8,128)(2,1)S(1)}, u32[]{:S(2)}, u32[]{:S(2)}) collective-permute-start(bf16[448,128]{1,0:T(8,128)(2,1)S(1)} %pad_maximum_fusion), channel_id=1, source_target_pairs={{0,8},{2,10},{4,12},{6,14},{8,0},{10,2},{12,4},{14,6},{1,9},{3,11}... | collective-permute-start | bytes 344072 | tf_op jit(solution)/shard_map/ppermute | solution.py:426
  17.9 0.0 copy-done
  17.9 0.3 weights.1
  18.2 0.7 %collective-permute-start.5 = (bf16[16,128]{1,0:T(8,128)(2,1)S(1)}, bf16[16,128]{1,0:T(8,128)(2,1)S(1)}, u32[]{:S(2)}, u32[]{:S(2)}) collective-permute-start(bf16[16,128]{1,0:T(8,128)(2,1)S(1)} %get-tuple-element.26), channel_id=1, source_target_pairs={{8,6},{6,8},{9,7},{7,9},{24,22},{22,24},{25,23},{23,25}} | collective-permute-start | bytes 12296 | tf_op jit(solution)/shard_map/ppermute | solution.py:409
  18.9 3.9 %collective-permute-done.4.refs_3_ = bf16[448,128]{1,0:T(8,128)(2,1)S(1)} collective-permute-done((bf16[448,128]{1,0:T(8,128)(2,1)S(1)}, bf16[448,128]{1,0:T(8,128)(2,1)S(1)}, u32[]{:S(2)}, u32[]{:S(2)}) %collective-permute-start.4) | collective-permute-done | bytes 114720 | tf_op jit(solution)/shard_map/ppermute | solution.py:426
  22.8 0.0 collective-permute-done.5.refs_4_
  22.9 0.1 collective-permute-start.6
  22.9 1.5 %response.1 = bf16[128,512]{1,0:T(8,128)(2,1)} custom-call(bf16[2,8,8,512]{3,2,1,0:T(8,128)(2,1)S(1)} %bitcast.10, bf16[2,2,8,512]{3,2,1,0:T(8,128)(2,1)S(1)} %collective-permute-done.refs_0_, bf16[2,8,512]{2,1,0:T(8,128)(2,1)S(1)} %collective-permute-done.1.refs_1_, bf16[2,8,512]{2,1,0:T(8,128)(2,1)S(1)} %collective-permute-done.2.refs_2_, ...), custom_call_target="tpu_custom_call" | custom-call | flops 301989888 | bytes 1048576 | tf_op jit(solution)/shard_map/response/pallas_call | solution.py:393
  24.5 3.5 %collective-permute-done.6 = bf16[432,128]{1,0:T(8,128)(2,1)S(1)} collective-permute-done((bf16[432,128]{1,0:T(8,128)(2,1)S(1)}, bf16[432,128]{1,0:T(8,128)(2,1)S(1)}, u32[]{:S(2)}, u32[]{:S(2)}) %collective-permute-start.6) | collective-permute-done | bytes 110624 | tf_op jit(solution)/shard_map/ppermute | solution.py:426
  28.0 1.2 %collective-permute-start.7 = (bf16[432,128]{1,0:T(8,128)(2,1)S(1)}, bf16[432,128]{1,0:T(8,128)(2,1)S(1)}, u32[]{:S(2)}, u32[]{:S(2)}) collective-permute-start(bf16[432,128]{1,0:T(8,128)(2,1)S(1)} %add_convert_fusion), channel_id=1, source_target_pairs={{0,4},{2,6},{4,0},{6,2},{8,12},{10,14},{12,8},{14,10},{1,5},{3,7},... | collective-permute-start | bytes 331784 | tf_op jit(solution)/shard_map/ppermute | solution.py:426
  29.2 1.5 %feature_grad.1 = bf16[128,512]{1,0:T(8,128)(2,1)} custom-call(bf16[2,8,8,512]{3,2,1,0:T(8,128)(2,1)S(1)} %bitcast.13, bf16[2,2,8,512]{3,2,1,0:T(8,128)(2,1)S(1)} %collective-permute-done.refs_0_, bf16[2,8,512]{2,1,0:T(8,128)(2,1)S(1)} %collective-permute-done.1.refs_1_, bf16[2,8,512]{2,1,0:T(8,128)(2,1)S(1)} %collective-permute-done.2.refs_2_, ...), custom_call_target="tpu_custom_call" | custom-call | flops 301989888 | bytes 1048576 | tf_op jit(solution)/shard_map/feature_grad/pallas_call | solution.py:393
  30.8 2.0 %collective-permute-done.7 = bf16[432,128]{1,0:T(8,128)(2,1)S(1)} collective-permute-done((bf16[432,128]{1,0:T(8,128)(2,1)S(1)}, bf16[432,128]{1,0:T(8,128)(2,1)S(1)}, u32[]{:S(2)}, u32[]{:S(2)}) %collective-permute-start.7) | collective-permute-done | bytes 110624 | tf_op jit(solution)/shard_map/ppermute | solution.py:426
  32.8 0.1 collective-permute-start.8
  32.9 1.5 %collective-permute-done.8.other_ref = f32[432,128]{1,0:T(8,128)S(1)} collective-permute-done((f32[432,128]{1,0:T(8,128)S(1)}, f32[432,128]{1,0:T(8,128)S(1)}, u32[]{:S(2)}, u32[]{:S(2)}) %collective-permute-start.8) | collective-permute-done | bytes 221216 | tf_op jit(solution)/shard_map/ppermute | solution.py:433
  34.4 1.2 %unpack.1 = f32[9,192,64]{2,1,0:T(8,128)} custom-call(f32[432,128]{1,0:T(8,128)S(1)} %convert_add_fusion.own_ref, f32[432,128]{1,0:T(8,128)S(1)} %collective-permute-done.8.other_ref), custom_call_target="tpu_custom_call" | custom-call | bytes 1048576 | tf_op jit(solution)/shard_map/unpack/pallas_call | solution.py:435
  (5 shorter events, 0.1 us)
Async XLA Ops:
  0.6 9.9 %copy-start.1 = (bf16[1,2,8,8,512]{4,3,2,1,0:T(8,128)(2,1)S(1)}, bf16[1,2,8,8,512]{4,3,2,1,0:T(8,128)(2,1)}, u32[]{:S(2)}) copy-start(bf16[1,2,8,8,512]{4,3,2,1,0:T(8,128)(2,1)} %param.4) | copy-start | bytes 393220
  0.6 9.9 %copy-start.2 = (bf16[1,2,8,8,512]{4,3,2,1,0:T(8,128)(2,1)S(1)}, bf16[1,2,8,8,512]{4,3,2,1,0:T(8,128)(2,1)}, u32[]{:S(2)}) copy-start(bf16[1,2,8,8,512]{4,3,2,1,0:T(8,128)(2,1)} %param.5) | copy-start | bytes 393220
  2.4 8.1 %collective-permute-start = (bf16[2,2,8,512]{3,2,1,0:T(8,128)(2,1)}, bf16[2,2,8,512]{3,2,1,0:T(8,128)(2,1)S(1)}, u32[]{:S(2)}, u32[]{:S(2)}) collective-permute-start(bf16[2,2,8,512]{3,2,1,0:T(8,128)(2,1)} %get-tuple-element.20), channel_id=1, source_target_pairs={{0,8},{2,10},{4,12},{6,14},{8,0},{10,2},{12,4},{14,6},{1,9},{3,11}... | collective-permute-start | bytes 98312 | tf_op jit(solution)/shard_map/ppermute | solution.py:367
  6.5 3.9 %collective-permute-start.1 = (bf16[2,8,512]{2,1,0:T(8,128)(2,1)}, bf16[2,8,512]{2,1,0:T(8,128)(2,1)S(1)}, u32[]{:S(2)}, u32[]{:S(2)}) collective-permute-start(bf16[2,8,512]{2,1,0:T(8,128)(2,1)} %get-tuple-element.21), channel_id=1, source_target_pairs={{0,2},{2,0},{4,6},{6,4},{8,10},{10,8},{12,14},{14,12},{1,3},{3,1},... | collective-permute-start | bytes 49160 | tf_op jit(solution)/shard_map/ppermute | solution.py:367
  8.0 2.5 %collective-permute-start.2 = (bf16[2,8,512]{2,1,0:T(8,128)(2,1)}, bf16[2,8,512]{2,1,0:T(8,128)(2,1)S(1)}, u32[]{:S(2)}, u32[]{:S(2)}) collective-permute-start(bf16[2,8,512]{2,1,0:T(8,128)(2,1)} %get-tuple-element.22), channel_id=1, source_target_pairs={{6,8},{8,6},{7,9},{9,7},{22,24},{24,22},{23,25},{25,23}} | collective-permute-start | bytes 49160 | tf_op jit(solution)/shard_map/ppermute | solution.py:367
  11.6 6.3 %copy-start = (bf16[3,3,3,64,64]{4,3,2,1,0:T(8,128)(2,1)S(1)}, bf16[3,3,3,64,64]{4,3,2,1,0:T(8,128)(2,1)}, u32[]{:S(2)}) copy-start(bf16[3,3,3,64,64]{4,3,2,1,0:T(8,128)(2,1)} %param.6) | copy-start | bytes 663556
  11.6 1.5 %collective-permute-start.3 = (f32[432,128]{1,0:T(8,128)S(1)}, f32[432,128]{1,0:T(8,128)S(1)}, u32[]{:S(2)}, u32[]{:S(2)}) collective-permute-start(f32[432,128]{1,0:T(8,128)S(1)} %get-tuple-element.24), channel_id=1, source_target_pairs={{0,1},{1,0},{2,3},{3,2},{4,5},{5,4},{6,7},{7,6},{8,9},{9,8},{10,11... | collective-permute-start | bytes 663560 | tf_op jit(solution)/shard_map/ppermute | solution.py:403
  13.2 9.6 %collective-permute-start.4 = (bf16[448,128]{1,0:T(8,128)(2,1)S(1)}, bf16[448,128]{1,0:T(8,128)(2,1)S(1)}, u32[]{:S(2)}, u32[]{:S(2)}) collective-permute-start(bf16[448,128]{1,0:T(8,128)(2,1)S(1)} %pad_maximum_fusion), channel_id=1, source_target_pairs={{0,8},{2,10},{4,12},{6,14},{8,0},{10,2},{12,4},{14,6},{1,9},{3,11}... | collective-permute-start | bytes 344072 | tf_op jit(solution)/shard_map/ppermute | solution.py:426
  18.2 4.6 %collective-permute-start.5 = (bf16[16,128]{1,0:T(8,128)(2,1)S(1)}, bf16[16,128]{1,0:T(8,128)(2,1)S(1)}, u32[]{:S(2)}, u32[]{:S(2)}) collective-permute-start(bf16[16,128]{1,0:T(8,128)(2,1)S(1)} %get-tuple-element.26), channel_id=1, source_target_pairs={{8,6},{6,8},{9,7},{7,9},{24,22},{22,24},{25,23},{23,25}} | collective-permute-start | bytes 12296 | tf_op jit(solution)/shard_map/ppermute | solution.py:409
  22.9 5.1 %collective-permute-start.6 = (bf16[432,128]{1,0:T(8,128)(2,1)S(1)}, bf16[432,128]{1,0:T(8,128)(2,1)S(1)}, u32[]{:S(2)}, u32[]{:S(2)}) collective-permute-start(bf16[432,128]{1,0:T(8,128)(2,1)S(1)} %add_convert_fusion.1), channel_id=1, source_target_pairs={{0,2},{2,0},{4,6},{6,4},{8,10},{10,8},{12,14},{14,12},{1,3},{3,1},... | collective-permute-start | bytes 331784 | tf_op jit(solution)/shard_map/ppermute | solution.py:426
  28.0 4.8 %collective-permute-start.7 = (bf16[432,128]{1,0:T(8,128)(2,1)S(1)}, bf16[432,128]{1,0:T(8,128)(2,1)S(1)}, u32[]{:S(2)}, u32[]{:S(2)}) collective-permute-start(bf16[432,128]{1,0:T(8,128)(2,1)S(1)} %add_convert_fusion), channel_id=1, source_target_pairs={{0,4},{2,6},{4,0},{6,2},{8,12},{10,14},{12,8},{14,10},{1,5},{3,7},... | collective-permute-start | bytes 331784 | tf_op jit(solution)/shard_map/ppermute | solution.py:426
  32.8 1.5 %collective-permute-start.8 = (f32[432,128]{1,0:T(8,128)S(1)}, f32[432,128]{1,0:T(8,128)S(1)}, u32[]{:S(2)}, u32[]{:S(2)}) collective-permute-start(f32[432,128]{1,0:T(8,128)S(1)} %convert_add_fusion.own_ref), channel_id=1, source_target_pairs={{0,1},{1,0},{2,3},{3,2},{4,5},{5,4},{6,7},{7,6},{8,9},{9,8},{10,11... | collective-permute-start | bytes 663560 | tf_op jit(solution)/shard_map/ppermute | solution.py:433

commit v3 on v2

--- a/solution.py
+++ b/solution.py
@@ -58,6 +58,16 @@
     return found
 
 
+def completed(pairs, tiles):
+    idle = [tile for tile in range(tiles) if all(tile != a for a, _ in pairs) and all(tile != b for _, b in pairs)]
+    near = [tile for tile in idle if tile ^ 1 in idle]
+    rest = [tile for tile in idle if tile ^ 1 not in idle]
+    pairs = pairs + [(tile, tile ^ 1) for tile in near]
+    for low, high in zip(rest[::2], rest[1::2]):
+        pairs = pairs + [(low, high), (high, low)]
+    return sorted(pairs)
+
+
 def make_plan(tiles):
     def edges(step):
         return [(tile, step(tile, 1, tiles)) for tile in range(tiles) if step(tile, 1, tiles) is not None]
@@ -65,6 +75,7 @@
     along_x, along_y, hops = rounds(edges(step_x)), rounds(edges(step_y)), detours(tiles)
     pairs = [[[(tile, one[tile][0]) for tile in sorted(one)] for one in kind] for kind in (along_x, along_y)]
     pairs.append([[hop[:2] for hop in one] for one in hops])
+    pairs = [[completed(one, tiles) for one in kind] for kind in pairs]
     roles = [[{tile: one[tile][1] for tile in one} for one in kind] for kind in (along_x, along_y)]
     roles.append([{hop[0]: (hop[2], 1 - hop[3]) for hop in one} for one in hops])
     roles.append([{hop[1]: hop[2:] for hop in one} for one in hops])
@@ -248,15 +259,16 @@
     send_ref[...] = packed[pl.ds(pl.multiple_of((1 - core) * count, 8), count), :]
 
 
-def conv_kernel(roles, tiles, channels, source, v_ref, *refs):
+def conv_kernel(roles, tiles, channels, source, ways, v_ref, *refs):
     roles = Roles(roles, tiles)
     counts = roles.counts
     x_refs = refs[: counts[0]]
     y_refs = refs[counts[0] : counts[0] + counts[1]]
     near = counts[0] + counts[1]
-    line_refs = refs[near : near + counts[0]]
-    hop_refs = refs[near + counts[0] : near + counts[0] + counts[2]]
-    weight_ref, out_ref, ext = refs[near + counts[0] + counts[2] :]
+    hops_at = near + counts[0] * ways
+    line_refs = refs[near:hops_at]
+    hop_refs = refs[hops_at : hops_at + counts[2]]
+    weight_ref, out_ref, ext = refs[hops_at + counts[2] :]
     bricks, edge, _, width = v_ref.shape
     rows = edge * edge
     first, last = edge, 2 * edge - 1
@@ -270,6 +282,9 @@
             ext[brick, side * (edge + 1), first : last + 1, :] = plane[brick]
     each = width // line_refs[0].shape[1]
     arrived = [ref[ref.shape[0] - 4 * each :, :].astype(F32) for ref in line_refs]
+    if ways == 2:
+        first_core = lax.axis_index("dp") == 0
+        arrived = [jnp.where(first_core, *arrived)]
     hops = [load_line(ref[...].astype(F32), 0, each) for ref in hop_refs]
     for side in range(2):
         row = jnp.zeros((edge, width), F32)
@@ -391,7 +406,7 @@
 
     def conv(source, x, weight):
         return call(
-            functools.partial(conv_kernel, roles, tiles, channels, source),
+            functools.partial(conv_kernel, roles, tiles, channels, source, ready),
             [VMEM] * (2 + len(got)),
             shape((bricks * rows, width), BF16),
             [pltpu.VMEM((bricks, edge + 2, 3 * edge, width + lanes), F32)],
@@ -399,38 +414,49 @@
             name="response" if source == 0 else "feature_grad",
         )(x, *got, weight)
 
+    cores = lax.axis_size("dp")
     swap = [(0, 1), (1, 0)]
     part = keep + lax.ppermute(send, "dp", swap)
-    steps = [[(i, i ^ (1 << bit)) for i in range(tiles)] for bit in range(tiles.bit_length() - 1)]
-    wire = BF16 if len(steps) <= 3 else F32
-    joined = len(pairs[0]) == 1 and pairs[0][0] in steps and wire == BF16
+    bits = [1 << number for number in range(tiles.bit_length() - 1)]
+    orders = [bits, bits]
+    wire = BF16 if len(bits) <= 3 else F32
+    shared = [bit for bit in bits if pairs[0] == [[(i, i ^ bit) for i in range(tiles)]]]
+    joined = bool(shared) and len(bits) == 3
     if joined:
-        steps.sort(key=lambda step: step != pairs[0][0])
+        first, last = (bit for bit in bits if bit not in shared)
+        orders = [shared + [first, last], [last] + shared + [first]]
     hops = [lax.ppermute(x, "space", one) for x, one in zip(lines[counts[0] :], pairs[2])]
     lines = lines[: counts[0]]
     if not joined:
         got += [lax.ppermute(x, "space", one) for x, one in zip(lines, pairs[0])]
-    for number, step in enumerate(steps):
+    ready = 2 if joined else 1
+    for number in range(len(bits)):
+        step = [
+            (tile * cores + core, (tile ^ order[number]) * cores + core)
+            for tile in range(tiles)
+            for core, order in enumerate(orders)
+        ]
         mine = part.astype(wire)
-        if number == 0 and joined:
-            mine = lax.optimization_barrier(jnp.concatenate([mine, lines[0]], axis=0))
+        carries = joined and number < ready
+        if carries:
+            mine = jnp.concatenate([mine, lines[0]], axis=0)
         if number == 1:
             mine, hops, forward, backward = lax.optimization_barrier((mine, hops, forward, backward))
+        else:
+            mine = lax.optimization_barrier(mine)
+        if number == ready:
             got += hops
             response = conv(0, f, forward)
             feature_grad = conv(1, c, backward)
-        elif number == 2:
-            mine, response = lax.optimization_barrier((mine, response))
-        else:
-            mine = lax.optimization_barrier(mine)
-        theirs = lax.ppermute(mine, "space", step)
-        if number == 0 and joined:
+        theirs = lax.ppermute(mine, ("space", "dp"), step)
+        if carries:
             got.append(theirs)
             mine, theirs = mine[:count], theirs[:count]
         part = mine.astype(F32) + theirs.astype(F32)
-    part, feature_grad = lax.optimization_barrier((part, feature_grad))
+    part, response = lax.optimization_barrier((part, response))
+    other = lax.ppermute(part, "dp", swap)
+    other, feature_grad = lax.optimization_barrier((other, feature_grad))
     response, feature_grad = (x.reshape(features.shape) for x in (response, feature_grad))
-    other = lax.ppermute(part, "dp", swap)
     cells = bricks * tiles * lax.axis_size("dp") * edge**3
     kernel_grad = call(
         functools.partial(unpack_kernel, 1.0 / math.sqrt(cells)),

time: 35.7 us -> 33.6 us (0.941)
  starting transfers between devices: 13 us -> 11.9 us
  waiting for transfers between devices: 14.2 us -> 13.2 us
    ppermute x3, starting transfers between devices: 5.98 us -> 4.36 us  [body(): theirs = lax.ppermute(mine, ('space', 'dp'), step)]
    ppermute x4, waiting for transfers between devices: 1.81 us -> 3.42 us  [body(): lax.ppermute(x, 'space', one)]
    ppermute x1, waiting for transfers between devices: 1.46 us -> 0.01 us  [body(): other = lax.ppermute(part, 'dp', swap)]
    ppermute x3, waiting for transfers between devices: 9.46 us -> 8.34 us  [body(): theirs = lax.ppermute(mine, ('space', 'dp'), step)]
    ppermute x4, starting transfers between devices: 6.9 us -> 7.42 us  [body(): lax.ppermute(x, 'space', one)]
where the time goes in v3:
time: 33.6 us; the launch traced here: 33.5 us
  waiting for transfers between devices  13.2 us (39%)
  starting transfers between devices  11.9 us (35%)
  Pallas kernels  7.41 us (22%)
  between operations  0.74 us (2%)
    ppermute x3, waiting for transfers between devices, body(): theirs = lax.ppermute(mine, ('space', 'dp'), step)  8.34 us
    ppermute x4, starting transfers between devices, body(): lax.ppermute(x, 'space', one)  7.42 us
    ppermute x3, starting transfers between devices, body(): theirs = lax.ppermute(mine, ('space', 'dp'), step)  4.36 us
    ppermute x4, waiting for transfers between devices, body(): lax.ppermute(x, 'space', one)  3.42 us
    pallas_call x2, Pallas kernels, conv(): call(functools.partial(conv_kernel, roles, tiles, channels, source, ready...  3.06 us
    pallas_call x1, Pallas kernels, body(): call(functools.partial(faces_kernel, roles, tiles), [HBM, HBM, HBM], [sha...  1.79 us
    ppermute x1, waiting for transfers between devices, body(): part = keep + lax.ppermute(send, 'dp', swap)  1.46 us
    pallas_call x1, Pallas kernels, body(): call(functools.partial(unpack_kernel, 1.0 / math.sqrt(cells)), [VMEM, VME...  1.16 us
  transfers between devices with their start and end apart: 9, of which 6 were waited for; matrix products, arithmetic and copies ran while one was open for 0% of the time, Pallas kernels for 10%

profile of v3, /device:TPU:0, one launch (start us, length us, event | category | flops | bytes accessed | tf_op | source)
XLA Modules:
  0.0 33.5 jit_solution(9562545900406363873)
XLA Ops:
  0.6 0.0 copy-start
  0.6 0.0 copy-start.1
  0.7 1.8 %faces.1 = (bf16[2,2,8,512]{3,2,1,0:T(8,128)(2,1)}, bf16[2,8,512]{2,1,0:T(8,128)(2,1)}, bf16[2,8,512]{2,1,0:T(8,128)(2,1)}) custom-call(bf16[2,8,8,512]{3,2,1,0:T(8,128)(2,1)} %bitcast.7, bf16[2,8,8,512]{3,2,1,0:T(8,128)(2,1)} %bitcast.10, s32[2,6]{1,0:T(2,128)} %bitcast.17), custom_call_target="tpu_custom_call" | custom-call | bytes 1048576 | tf_op jit(solution)/shard_map/faces/pallas_call | solution.py:369
  2.4 4.1 %collective-permute-start = (bf16[2,2,8,512]{3,2,1,0:T(8,128)(2,1)}, bf16[2,2,8,512]{3,2,1,0:T(8,128)(2,1)S(1)}, u32[]{:S(2)}, u32[]{:S(2)}) collective-permute-start(bf16[2,2,8,512]{3,2,1,0:T(8,128)(2,1)} %get-tuple-element.20), channel_id=1, source_target_pairs={{0,8},{2,10},{4,12},{6,14},{8,0},{10,2},{12,4},{14,6},{1,9},{3,11}... | collective-permute-start | bytes 98312 | tf_op jit(solution)/shard_map/ppermute | solution.py:382
  6.5 1.5 %collective-permute-start.1 = (bf16[2,8,512]{2,1,0:T(8,128)(2,1)}, bf16[2,8,512]{2,1,0:T(8,128)(2,1)S(1)}, u32[]{:S(2)}, u32[]{:S(2)}) collective-permute-start(bf16[2,8,512]{2,1,0:T(8,128)(2,1)} %get-tuple-element.21), channel_id=1, source_target_pairs={{0,2},{2,0},{4,6},{6,4},{8,10},{10,8},{12,14},{14,12},{1,3},{3,1},... | collective-permute-start | bytes 49160 | tf_op jit(solution)/shard_map/ppermute | solution.py:382
  8.0 0.5 %collective-permute-start.2 = (bf16[2,8,512]{2,1,0:T(8,128)(2,1)}, bf16[2,8,512]{2,1,0:T(8,128)(2,1)S(1)}, u32[]{:S(2)}, u32[]{:S(2)}) collective-permute-start(bf16[2,8,512]{2,1,0:T(8,128)(2,1)} %get-tuple-element.22), channel_id=1, source_target_pairs={{0,2},{2,0},{4,10},{6,8},{8,6},{10,4},{12,14},{14,12},{1,3},{3,1},... | collective-permute-start | bytes 49160 | tf_op jit(solution)/shard_map/ppermute | solution.py:382
  8.6 1.9 %collective-permute-done.1.refs_1_ = bf16[2,8,512]{2,1,0:T(8,128)(2,1)S(1)} collective-permute-done((bf16[2,8,512]{2,1,0:T(8,128)(2,1)}, bf16[2,8,512]{2,1,0:T(8,128)(2,1)S(1)}, u32[]{:S(2)}, u32[]{:S(2)}) %collective-permute-start.1) | collective-permute-done | bytes 16416 | tf_op jit(solution)/shard_map/ppermute | solution.py:382
  10.5 1.5 %collective-permute-done.2.refs_2_ = bf16[2,8,512]{2,1,0:T(8,128)(2,1)S(1)} collective-permute-done((bf16[2,8,512]{2,1,0:T(8,128)(2,1)}, bf16[2,8,512]{2,1,0:T(8,128)(2,1)S(1)}, u32[]{:S(2)}, u32[]{:S(2)}) %collective-permute-start.2) | collective-permute-done | bytes 16416 | tf_op jit(solution)/shard_map/ppermute | solution.py:382
  12.0 0.0 collective-permute-done.refs_0_
  12.0 0.0 copy-done
  12.0 0.0 copy-done.1
  12.0 1.1 %kernel_grad.1 = (f32[432,128]{1,0:T(8,128)S(1)}, f32[432,128]{1,0:T(8,128)S(1)}, bf16[16,128]{1,0:T(8,128)(2,1)S(1)}, bf16[16,128]{1,0:T(8,128)(2,1)S(1)}) custom-call(bf16[2,8,8,512]{3,2,1,0:T(8,128)(2,1)S(1)} %bitcast.8, bf16[2,8,8,512]{3,2,1,0:T(8,128)(2,1)S(1)} %bitcast.11, bf16[2,2,8,512]{3,2,1,0:T(8,128)(2,1)S(1)} %collective-permute-done.refs_0_, ...), custom_call_target="tpu_custom_call" | custom-call | flops 301989888 | bytes 1048576 | tf_op jit(solution)/shard_map/kernel_grad/pallas_call | solution.py:385
  13.1 0.0 copy-start.2
  13.1 0.1 collective-permute-start.3
  13.2 1.5 %collective-permute-done.3 = f32[432,128]{1,0:T(8,128)S(1)} collective-permute-done((f32[432,128]{1,0:T(8,128)S(1)}, f32[432,128]{1,0:T(8,128)S(1)}, u32[]{:S(2)}, u32[]{:S(2)}) %collective-permute-start.3) | collective-permute-done | bytes 221216 | tf_op jit(solution)/shard_map/ppermute | solution.py:419
  14.7 1.3 %collective-permute-start.4 = (bf16[448,128]{1,0:T(8,128)(2,1)S(1)}, bf16[448,128]{1,0:T(8,128)(2,1)S(1)}, u32[]{:S(2)}, u32[]{:S(2)}) collective-permute-start(bf16[448,128]{1,0:T(8,128)(2,1)S(1)} %pad_maximum_fusion.1), channel_id=1, source_target_pairs={{0,8},{1,5},{2,10},{3,7},{4,12},{5,1},{6,14},{7,3},{8,0},{9,13},{1... | collective-permute-start | bytes 344072 | tf_op jit(solution)/shard_map/ppermute | solution.py:451
  16.0 0.0 copy-done.2
  16.0 0.3 %weights.1 = (bf16[9,256,128]{2,1,0:T(8,128)(2,1)S(1)}, bf16[9,128,256]{2,1,0:T(8,128)(2,1)S(1)}) custom-call(bf16[27,64,64]{2,1,0:T(8,128)(2,1)S(1)} %bitcast.13), custom_call_target="tpu_custom_call" | custom-call | bytes 1048576 | tf_op jit(solution)/shard_map/weights/pallas_call | solution.py:399
  16.3 1.3 %collective-permute-start.5 = (bf16[16,128]{1,0:T(8,128)(2,1)S(1)}, bf16[16,128]{1,0:T(8,128)(2,1)S(1)}, u32[]{:S(2)}, u32[]{:S(2)}) collective-permute-start(bf16[16,128]{1,0:T(8,128)(2,1)S(1)} %get-tuple-element.26), channel_id=1, source_target_pairs={{0,2},{2,0},{4,10},{6,8},{8,6},{10,4},{12,14},{14,12},{1,3},{3,1},... | collective-permute-start | bytes 12296 | tf_op jit(solution)/shard_map/ppermute | solution.py:428
  17.6 2.9 %collective-permute-done.4.refs_3_ = bf16[448,128]{1,0:T(8,128)(2,1)S(1)} collective-permute-done((bf16[448,128]{1,0:T(8,128)(2,1)S(1)}, bf16[448,128]{1,0:T(8,128)(2,1)S(1)}, u32[]{:S(2)}, u32[]{:S(2)}) %collective-permute-start.4) | collective-permute-done | bytes 114720 | tf_op jit(solution)/shard_map/ppermute | solution.py:451
  20.6 0.0 collective-permute-done.5.refs_5_
  20.6 0.6 %collective-permute-start.6 = (bf16[448,128]{1,0:T(8,128)(2,1)S(1)}, bf16[448,128]{1,0:T(8,128)(2,1)S(1)}, u32[]{:S(2)}, u32[]{:S(2)}) collective-permute-start(bf16[448,128]{1,0:T(8,128)(2,1)S(1)} %pad_maximum_fusion), channel_id=1, source_target_pairs={{0,2},{1,9},{2,0},{3,11},{4,6},{5,13},{6,4},{7,15},{8,10},{9,1},{1... | collective-permute-start | bytes 344072 | tf_op jit(solution)/shard_map/ppermute | solution.py:451
  21.2 4.2 %collective-permute-done.6.refs_4_ = bf16[448,128]{1,0:T(8,128)(2,1)S(1)} collective-permute-done((bf16[448,128]{1,0:T(8,128)(2,1)S(1)}, bf16[448,128]{1,0:T(8,128)(2,1)S(1)}, u32[]{:S(2)}, u32[]{:S(2)}) %collective-permute-start.6) | collective-permute-done | bytes 114720 | tf_op jit(solution)/shard_map/ppermute | solution.py:451
  25.5 2.4 %collective-permute-start.7 = (bf16[432,128]{1,0:T(8,128)(2,1)S(1)}, bf16[432,128]{1,0:T(8,128)(2,1)S(1)}, u32[]{:S(2)}, u32[]{:S(2)}) collective-permute-start(bf16[432,128]{1,0:T(8,128)(2,1)S(1)} %add_convert_fusion), channel_id=1, source_target_pairs={{0,4},{1,3},{2,6},{3,1},{4,0},{5,7},{6,2},{7,5},{8,12},{9,11},{10,... | collective-permute-start | bytes 331784 | tf_op jit(solution)/shard_map/ppermute | solution.py:451
  27.9 1.5 %response.1 = bf16[128,512]{1,0:T(8,128)(2,1)} custom-call(bf16[2,8,8,512]{3,2,1,0:T(8,128)(2,1)S(1)} %bitcast.9, bf16[2,2,8,512]{3,2,1,0:T(8,128)(2,1)S(1)} %collective-permute-done.refs_0_, bf16[2,8,512]{2,1,0:T(8,128)(2,1)S(1)} %collective-permute-done.1.refs_1_, bf16[2,8,512]{2,1,0:T(8,128)(2,1)S(1)} %collective-permute-done.2.refs_2_, ...), custom_call_target="tpu_custom_call" | custom-call | flops 301989888 | bytes 1048576 | tf_op jit(solution)/shard_map/response/pallas_call | solution.py:408
  29.5 1.2 %collective-permute-done.7 = bf16[432,128]{1,0:T(8,128)(2,1)S(1)} collective-permute-done((bf16[432,128]{1,0:T(8,128)(2,1)S(1)}, bf16[432,128]{1,0:T(8,128)(2,1)S(1)}, u32[]{:S(2)}, u32[]{:S(2)}) %collective-permute-start.7) | collective-permute-done | bytes 110624 | tf_op jit(solution)/shard_map/ppermute | solution.py:451
  30.7 0.1 collective-permute-start.8
  30.8 1.5 %feature_grad.1 = bf16[128,512]{1,0:T(8,128)(2,1)} custom-call(bf16[2,8,8,512]{3,2,1,0:T(8,128)(2,1)S(1)} %bitcast.12, bf16[2,2,8,512]{3,2,1,0:T(8,128)(2,1)S(1)} %collective-permute-done.refs_0_, bf16[2,8,512]{2,1,0:T(8,128)(2,1)S(1)} %collective-permute-done.1.refs_1_, bf16[2,8,512]{2,1,0:T(8,128)(2,1)S(1)} %collective-permute-done.2.refs_2_, ...), custom_call_target="tpu_custom_call" | custom-call | flops 301989888 | bytes 1048576 | tf_op jit(solution)/shard_map/feature_grad/pallas_call | solution.py:408
  32.3 0.0 collective-permute-done.8.other_ref
  32.3 1.2 %unpack.1 = f32[9,192,64]{2,1,0:T(8,128)} custom-call(f32[432,128]{1,0:T(8,128)S(1)} %convert_add_fusion.own_ref, f32[432,128]{1,0:T(8,128)S(1)} %collective-permute-done.8.other_ref), custom_call_target="tpu_custom_call" | custom-call | bytes 1048576 | tf_op jit(solution)/shard_map/unpack/pallas_call | solution.py:461
  (6 shorter events, 0.1 us)
Async XLA Ops:
  0.6 11.4 %copy-start = (bf16[1,2,8,8,512]{4,3,2,1,0:T(8,128)(2,1)S(1)}, bf16[1,2,8,8,512]{4,3,2,1,0:T(8,128)(2,1)}, u32[]{:S(2)}) copy-start(bf16[1,2,8,8,512]{4,3,2,1,0:T(8,128)(2,1)} %param.4) | copy-start | bytes 393220
  0.6 11.4 %copy-start.1 = (bf16[1,2,8,8,512]{4,3,2,1,0:T(8,128)(2,1)S(1)}, bf16[1,2,8,8,512]{4,3,2,1,0:T(8,128)(2,1)}, u32[]{:S(2)}) copy-start(bf16[1,2,8,8,512]{4,3,2,1,0:T(8,128)(2,1)} %param.5) | copy-start | bytes 393220
  2.4 9.5 %collective-permute-start = (bf16[2,2,8,512]{3,2,1,0:T(8,128)(2,1)}, bf16[2,2,8,512]{3,2,1,0:T(8,128)(2,1)S(1)}, u32[]{:S(2)}, u32[]{:S(2)}) collective-permute-start(bf16[2,2,8,512]{3,2,1,0:T(8,128)(2,1)} %get-tuple-element.20), channel_id=1, source_target_pairs={{0,8},{2,10},{4,12},{6,14},{8,0},{10,2},{12,4},{14,6},{1,9},{3,11}... | collective-permute-start | bytes 98312 | tf_op jit(solution)/shard_map/ppermute | solution.py:382
  6.5 3.9 %collective-permute-start.1 = (bf16[2,8,512]{2,1,0:T(8,128)(2,1)}, bf16[2,8,512]{2,1,0:T(8,128)(2,1)S(1)}, u32[]{:S(2)}, u32[]{:S(2)}) collective-permute-start(bf16[2,8,512]{2,1,0:T(8,128)(2,1)} %get-tuple-element.21), channel_id=1, source_target_pairs={{0,2},{2,0},{4,6},{6,4},{8,10},{10,8},{12,14},{14,12},{1,3},{3,1},... | collective-permute-start | bytes 49160 | tf_op jit(solution)/shard_map/ppermute | solution.py:382
  8.0 3.9 %collective-permute-start.2 = (bf16[2,8,512]{2,1,0:T(8,128)(2,1)}, bf16[2,8,512]{2,1,0:T(8,128)(2,1)S(1)}, u32[]{:S(2)}, u32[]{:S(2)}) collective-permute-start(bf16[2,8,512]{2,1,0:T(8,128)(2,1)} %get-tuple-element.22), channel_id=1, source_target_pairs={{0,2},{2,0},{4,10},{6,8},{8,6},{10,4},{12,14},{14,12},{1,3},{3,1},... | collective-permute-start | bytes 49160 | tf_op jit(solution)/shard_map/ppermute | solution.py:382
  13.1 2.9 %copy-start.2 = (bf16[3,3,3,64,64]{4,3,2,1,0:T(8,128)(2,1)S(1)}, bf16[3,3,3,64,64]{4,3,2,1,0:T(8,128)(2,1)}, u32[]{:S(2)}) copy-start(bf16[3,3,3,64,64]{4,3,2,1,0:T(8,128)(2,1)} %param.6) | copy-start | bytes 663556
  13.1 1.5 %collective-permute-start.3 = (f32[432,128]{1,0:T(8,128)S(1)}, f32[432,128]{1,0:T(8,128)S(1)}, u32[]{:S(2)}, u32[]{:S(2)}) collective-permute-start(f32[432,128]{1,0:T(8,128)S(1)} %get-tuple-element.24), channel_id=1, source_target_pairs={{0,1},{1,0},{2,3},{3,2},{4,5},{5,4},{6,7},{7,6},{8,9},{9,8},{10,11... | collective-permute-start | bytes 663560 | tf_op jit(solution)/shard_map/ppermute | solution.py:419
  14.7 5.9 %collective-permute-start.4 = (bf16[448,128]{1,0:T(8,128)(2,1)S(1)}, bf16[448,128]{1,0:T(8,128)(2,1)S(1)}, u32[]{:S(2)}, u32[]{:S(2)}) collective-permute-start(bf16[448,128]{1,0:T(8,128)(2,1)S(1)} %pad_maximum_fusion.1), channel_id=1, source_target_pairs={{0,8},{1,5},{2,10},{3,7},{4,12},{5,1},{6,14},{7,3},{8,0},{9,13},{1... | collective-permute-start | bytes 344072 | tf_op jit(solution)/shard_map/ppermute | solution.py:451
  16.3 4.3 %collective-permute-start.5 = (bf16[16,128]{1,0:T(8,128)(2,1)S(1)}, bf16[16,128]{1,0:T(8,128)(2,1)S(1)}, u32[]{:S(2)}, u32[]{:S(2)}) collective-permute-start(bf16[16,128]{1,0:T(8,128)(2,1)S(1)} %get-tuple-element.26), channel_id=1, source_target_pairs={{0,2},{2,0},{4,10},{6,8},{8,6},{10,4},{12,14},{14,12},{1,3},{3,1},... | collective-permute-start | bytes 12296 | tf_op jit(solution)/shard_map/ppermute | solution.py:428
  20.6 4.9 %collective-permute-start.6 = (bf16[448,128]{1,0:T(8,128)(2,1)S(1)}, bf16[448,128]{1,0:T(8,128)(2,1)S(1)}, u32[]{:S(2)}, u32[]{:S(2)}) collective-permute-start(bf16[448,128]{1,0:T(8,128)(2,1)S(1)} %pad_maximum_fusion), channel_id=1, source_target_pairs={{0,2},{1,9},{2,0},{3,11},{4,6},{5,13},{6,4},{7,15},{8,10},{9,1},{1... | collective-permute-start | bytes 344072 | tf_op jit(solution)/shard_map/ppermute | solution.py:451
  25.5 5.2 %collective-permute-start.7 = (bf16[432,128]{1,0:T(8,128)(2,1)S(1)}, bf16[432,128]{1,0:T(8,128)(2,1)S(1)}, u32[]{:S(2)}, u32[]{:S(2)}) collective-permute-start(bf16[432,128]{1,0:T(8,128)(2,1)S(1)} %add_convert_fusion), channel_id=1, source_target_pairs={{0,4},{1,3},{2,6},{3,1},{4,0},{5,7},{6,2},{7,5},{8,12},{9,11},{10,... | collective-permute-start | bytes 331784 | tf_op jit(solution)/shard_map/ppermute | solution.py:451
  30.7 1.6 %collective-permute-start.8 = (f32[432,128]{1,0:T(8,128)S(1)}, f32[432,128]{1,0:T(8,128)S(1)}, u32[]{:S(2)}, u32[]{:S(2)}) collective-permute-start(f32[432,128]{1,0:T(8,128)S(1)} %convert_add_fusion.own_ref), channel_id=1, source_target_pairs={{0,1},{1,0},{2,3},{3,2},{4,5},{5,4},{6,7},{7,6},{8,9},{9,8},{10,11... | collective-permute-start | bytes 663560 | tf_op jit(solution)/shard_map/ppermute | solution.py:457

commit v4 on v3

--- a/solution.py
+++ b/solution.py
@@ -113,40 +113,46 @@
     return jnp.where(keep, x, jnp.zeros_like(x))
 
 
-def faces_kernel(roles, tiles, f_hbm, c_hbm, link_hbm, *refs):
+def x_faces_kernel(roles, tiles, f_hbm, c_hbm, link_hbm, *refs):
     roles = Roles(roles, tiles)
-    counts = roles.counts
-    x_refs = refs[: counts[0]]
-    y_refs = refs[counts[0] : counts[0] + counts[1]]
-    f_ref, c_ref, link_ref, arrived = refs[counts[0] + counts[1] :]
-    copies = [
-        pltpu.make_async_copy(f_hbm, f_ref, arrived.at[0]),
-        pltpu.make_async_copy(c_hbm, c_ref, arrived.at[1]),
-        pltpu.make_async_copy(link_hbm, link_ref, arrived.at[2]),
-    ]
+    *x_refs, flag_ref, link_ref, arrived = refs
+    edge = f_hbm.shape[1]
+    copies = [pltpu.make_async_copy(link_hbm, link_ref, arrived.at[0])]
+    for number, out in enumerate(x_refs):
+        plane = jnp.where(roles.side(0, number, 1), edge - 1, 0)
+        for source, ref in enumerate((f_hbm, c_hbm)):
+            for brick in range(2):
+                at = arrived.at[len(copies)]
+                copies.append(pltpu.make_async_copy(ref.at[brick, plane], out.at[source, brick], at))
     for copy in copies:
         copy.start()
     for copy in copies:
         copy.wait()
-    edge = f_ref.shape[1]
     linked = [[link_ref[brick, way] >= 0 for way in range(4)] for brick in range(2)]
     for number, out in enumerate(x_refs):
         up = roles.side(0, number, 1)
-        plane = jnp.where(up, edge - 1, 0)
         for brick in range(2):
-            keep = jnp.where(up, linked[brick][1], linked[brick][0])
-            for source, ref in enumerate((f_ref, c_ref)):
-                out[source, brick] = masked(keep, ref[brick, plane])
+
+            @pl.when(jnp.logical_not(jnp.where(up, linked[brick][1], linked[brick][0])))
+            def _():
+                out[:, brick] = jnp.zeros_like(out[:, brick])
+
+    for row, flag in enumerate((linked[0][2], linked[1][3])):
+        flag_ref[8 * row : 8 * row + 8, :] = jnp.full((8, flag_ref.shape[1]), jnp.where(flag, 1.0, 0.0), F32)
+
+
+def y_faces_kernel(roles, tiles, f_ref, c_ref, flag_ref, *y_refs):
+    roles = Roles(roles, tiles)
+    edge = f_ref.shape[1]
     rows = []
     for ref in (f_ref, c_ref):
-        low = ref[0].astype(F32)[:, 0, :]
-        high = ref[1].astype(F32)[:, edge - 1, :]
+        low = ref[0].astype(F32)[:, 0, :] * flag_ref[:8]
+        high = ref[1].astype(F32)[:, edge - 1, :] * flag_ref[8:]
         rows.append((low, high))
     for number, out in enumerate(y_refs):
         up = roles.side(1, number, 1)
-        keep = jnp.where(up, linked[1][3], linked[0][2])
         for source, (low, high) in enumerate(rows):
-            out[source] = masked(keep, jnp.where(up, high, low)).astype(BF16)
+            out[source] = jnp.where(up, high, low).astype(BF16)
 
 
 def padded(x, channels):
@@ -320,29 +326,41 @@
         out_ref[:, lanes * k : lanes * (k + 1)] = total[bricks * rows * k : bricks * rows * (k + 1)].astype(BF16)
 
 
-def unpack_kernel(factor, own_ref, other_ref, out_ref, packed):
+def unpack_kernel(factor, own_ref, other_ref, out_hbm, out_ref, sent):
     count = own_ref.shape[0]
-    core = lax.axis_index("dp")
-    packed[pl.ds(pl.multiple_of(core * count, 8), count), :] = own_ref[...] * factor
-    packed[pl.ds(pl.multiple_of((1 - core) * count, 8), count), :] = other_ref[...] * factor
+    first_half = lax.axis_index("dp") == 0
     taps, rows, channels = out_ref.shape
     half = rows // 2
+
+    def packed(start, stop):
+        pieces = []
+        for low, ref, other in ((0, own_ref, other_ref), (count, other_ref, own_ref)):
+            here = slice(max(start - low, 0), min(stop - low, count))
+            if here.start < here.stop:
+                pieces.append(jnp.where(first_half, ref[here], other[here]))
+        return jnp.concatenate(pieces, axis=0) * factor
+
+    copies = []
     for tap in range(taps):
-        block = packed[half * tap : half * (tap + 1), :]
+        block = packed(half * tap, half * (tap + 1))
         out_ref[tap, :half, :] = block[:, :channels]
         out_ref[tap, half:, :] = pltpu.roll(block, channels, 1)[:, :channels]
+        copies.append(pltpu.make_async_copy(out_ref.at[tap], out_hbm.at[tap], sent.at[tap]))
+        copies[-1].start()
+    for copy in copies:
+        copy.wait()
 
 
 VMEM = pl.BlockSpec(memory_space=pltpu.VMEM)
 HBM = pl.BlockSpec(memory_space=pltpu.HBM)
 
 
-def call(kernel, in_specs, out_shapes, scratch=(), flops=0, name=None, vmem=24 * 2**20):
+def call(kernel, in_specs, out_shapes, scratch=(), flops=0, name=None, vmem=24 * 2**20, out=None):
     several = isinstance(out_shapes, list)
     return pl.pallas_call(
         kernel,
         in_specs=in_specs,
-        out_specs=[VMEM] * len(out_shapes) if several else VMEM,
+        out_specs=[VMEM] * len(out_shapes) if several else (out or VMEM),
         out_shape=out_shapes,
         scratch_shapes=list(scratch),
         compiler_params=pltpu.CompilerParams(vmem_limit_bytes=vmem),
@@ -365,21 +383,22 @@
     links = neighbours.reshape(bricks, 6)
 
     near = counts[0] + counts[1]
-    face_shapes = [(2, bricks, edge, width)] * counts[0] + [(2, edge, width)] * counts[1]
-    faces = call(
-        functools.partial(faces_kernel, roles, tiles),
+    *faces, flags = call(
+        functools.partial(x_faces_kernel, roles, tiles),
         [HBM, HBM, HBM],
-        [shape(s, BF16) for s in face_shapes],
-        [
-            pltpu.VMEM(f.shape, BF16),
-            pltpu.VMEM(c.shape, BF16),
-            pltpu.SMEM(links.shape, jnp.int32),
-            pltpu.SemaphoreType.DMA((3,)),
-        ],
-        name="faces",
+        [pltpu.VMEM((2, bricks, edge, width), BF16)] * counts[0] + [pltpu.VMEM((16, width), F32)],
+        [pltpu.SMEM(links.shape, jnp.int32), pltpu.SemaphoreType.DMA((4 * counts[0] + 1,))],
+        name="x_faces",
         vmem=None,
     )(f, c, links)
-    got = [lax.ppermute(x, "space", one) for x, one in zip(faces, pairs[0] + pairs[1])]
+    got = [lax.ppermute(x, "space", one) for x, one in zip(faces, pairs[0])]
+    faces = call(
+        functools.partial(y_faces_kernel, roles, tiles),
+        [VMEM] * 3,
+        [pltpu.VMEM((2, edge, width), BF16)] * counts[1],
+        name="y_faces",
+    )(f, c, flags)
+    got += [lax.ppermute(x, "space", one) for x, one in zip(faces, pairs[1])]
     count = 27 * channels * channels // lanes // 2
     line_rows = 4 * width // lanes
     keep, send, *lines = call(
@@ -462,8 +481,9 @@
         functools.partial(unpack_kernel, 1.0 / math.sqrt(cells)),
         [VMEM, VMEM],
         shape((9, 3 * channels, channels), F32),
-        [pltpu.VMEM((2 * count, lanes), F32)],
+        [pltpu.VMEM((9, 3 * channels, channels), F32), pltpu.SemaphoreType.DMA((9,))],
         name="unpack",
+        out=HBM,
     )(part, other).reshape(kernel.shape)
     return response, feature_grad, kernel_grad
 

time: 33.6 us -> 32.6 us (0.970)
  Pallas kernels: 7.41 us -> 6.47 us
    ppermute x0 -> x3, starting transfers between devices: none -> 6.19 us  [the longest x1 4.1 us: body(): got = [lax.ppermute(x, 'space', one) for x, one in zip(faces, pairs[0])]]
    ppermute x4 -> x1, starting transfers between devices: 7.42 us -> 1.34 us  [body(): lax.ppermute(x, 'space', one)]
    ppermute x4 -> x1, waiting for transfers between devices: 3.42 us -> 0.01 us  [body(): lax.ppermute(x, 'space', one)]
    ppermute x0 -> x3, waiting for transfers between devices: none -> 3.21 us  [the longest x2 3.2 us: body(): got += [lax.ppermute(x, 'space', one) for x, one in zip(faces, pairs[1])]]
    pallas_call x1 -> x2, Pallas kernels: 1.79 us -> 0.94 us  [the longest x1 0.89 us: body(): call(functools.partial(x_faces_kernel, roles, tiles), [HBM, HBM, HBM], [p...]
  transfers between devices with their start and end apart: 9 -> 9, of which waited for: 6 -> 6; matrix products, arithmetic and copies ran while one was open for 0% -> 0% of each run, Pallas kernels for 10% -> 11%
where the time goes in v4:
time: 32.6 us; the launch traced here: 32.4 us
  waiting for transfers between devices  12.9 us (40%)
  starting transfers between devices  12.1 us (37%)
  Pallas kernels  6.47 us (20%)
  between operations  0.74 us (2%)
    ppermute x3, waiting for transfers between devices, body(): theirs = lax.ppermute(mine, ('space', 'dp'), step)  8.24 us
    ppermute x3, starting transfers between devices, body(): theirs = lax.ppermute(mine, ('space', 'dp'), step)  4.42 us
    ppermute x1, starting transfers between devices, body(): got = [lax.ppermute(x, 'space', one) for x, one in zip(faces, pairs[0])]  4.1 us
    ppermute x2, waiting for transfers between devices, body(): got += [lax.ppermute(x, 'space', one) for x, one in zip(faces, pairs[1])]  3.2 us
    pallas_call x2, Pallas kernels, conv(): call(functools.partial(conv_kernel, roles, tiles, channels, source, ready...  3.06 us
    ppermute x2, starting transfers between devices, body(): got += [lax.ppermute(x, 'space', one) for x, one in zip(faces, pairs[1])]  2.09 us
    ppermute x1, waiting for transfers between devices, body(): part = keep + lax.ppermute(send, 'dp', swap)  1.46 us
    ppermute x1, starting transfers between devices, body(): lax.ppermute(x, 'space', one)  1.34 us
  transfers between devices with their start and end apart: 9, of which 6 were waited for; matrix products, arithmetic and copies ran while one was open for 0% of the time, Pallas kernels for 11%

profile of v4, /device:TPU:0, one launch (start us, length us, event | category | flops | bytes accessed | tf_op | source)
XLA Modules:
  0.0 32.4 jit_solution(12286819171655902010)
XLA Ops:
  0.6 0.0 copy-start
  0.6 0.0 copy-start.1
  0.7 0.9 %x_faces.1 = (bf16[2,2,8,512]{3,2,1,0:T(8,128)(2,1)S(1)}, f32[16,512]{1,0:T(8,128)S(1)}) custom-call(bf16[2,8,8,512]{3,2,1,0:T(8,128)(2,1)} %bitcast.7, bf16[2,8,8,512]{3,2,1,0:T(8,128)(2,1)} %bitcast.11, s32[2,6]{1,0:T(2,128)} %bitcast.19), custom_call_target="tpu_custom_call" | custom-call | bytes 1048576 | tf_op jit(solution)/shard_map/x_faces/pallas_call | solution.py:386
  1.5 4.1 %collective-permute-start = (bf16[2,2,8,512]{3,2,1,0:T(8,128)(2,1)S(1)}, bf16[2,2,8,512]{3,2,1,0:T(8,128)(2,1)S(1)}, u32[]{:S(2)}, u32[]{:S(2)}) collective-permute-start(bf16[2,2,8,512]{3,2,1,0:T(8,128)(2,1)S(1)} %get-tuple-element.21), channel_id=1, source_target_pairs={{0,8},{2,10},{4,12},{6,14},{8,0},{10,2},{12,4},{14,6},{1,9},{3,11}... | collective-permute-start | bytes 98312 | tf_op jit(solution)/shard_map/ppermute | solution.py:394
  5.6 0.0 copy-done
  5.6 0.0 copy-done.1
  5.7 0.1 y_faces.1
  5.7 1.6 %collective-permute-start.1 = (bf16[2,8,512]{2,1,0:T(8,128)(2,1)S(1)}, bf16[2,8,512]{2,1,0:T(8,128)(2,1)S(1)}, u32[]{:S(2)}, u32[]{:S(2)}) collective-permute-start(bf16[2,8,512]{2,1,0:T(8,128)(2,1)S(1)} %get-tuple-element.23), channel_id=1, source_target_pairs={{0,2},{2,0},{4,6},{6,4},{8,10},{10,8},{12,14},{14,12},{1,3},{3,1},... | collective-permute-start | bytes 49160 | tf_op jit(solution)/shard_map/ppermute | solution.py:401
  7.3 0.5 %collective-permute-start.2 = (bf16[2,8,512]{2,1,0:T(8,128)(2,1)S(1)}, bf16[2,8,512]{2,1,0:T(8,128)(2,1)S(1)}, u32[]{:S(2)}, u32[]{:S(2)}) collective-permute-start(bf16[2,8,512]{2,1,0:T(8,128)(2,1)S(1)} %get-tuple-element.24), channel_id=1, source_target_pairs={{0,2},{2,0},{4,10},{6,8},{8,6},{10,4},{12,14},{14,12},{1,3},{3,1},... | collective-permute-start | bytes 49160 | tf_op jit(solution)/shard_map/ppermute | solution.py:401
  7.8 1.7 %collective-permute-done.1.refs_1_ = bf16[2,8,512]{2,1,0:T(8,128)(2,1)S(1)} collective-permute-done((bf16[2,8,512]{2,1,0:T(8,128)(2,1)S(1)}, bf16[2,8,512]{2,1,0:T(8,128)(2,1)S(1)}, u32[]{:S(2)}, u32[]{:S(2)}) %collective-permute-start.1) | collective-permute-done | bytes 16416 | tf_op jit(solution)/shard_map/ppermute | solution.py:401
  9.5 1.5 %collective-permute-done.2.refs_2_ = bf16[2,8,512]{2,1,0:T(8,128)(2,1)S(1)} collective-permute-done((bf16[2,8,512]{2,1,0:T(8,128)(2,1)S(1)}, bf16[2,8,512]{2,1,0:T(8,128)(2,1)S(1)}, u32[]{:S(2)}, u32[]{:S(2)}) %collective-permute-start.2) | collective-permute-done | bytes 16416 | tf_op jit(solution)/shard_map/ppermute | solution.py:401
  11.0 0.0 collective-permute-done.refs_0_
  11.0 1.0 %kernel_grad.1 = (f32[432,128]{1,0:T(8,128)S(1)}, f32[432,128]{1,0:T(8,128)S(1)}, bf16[16,128]{1,0:T(8,128)(2,1)S(1)}, bf16[16,128]{1,0:T(8,128)(2,1)S(1)}) custom-call(bf16[2,8,8,512]{3,2,1,0:T(8,128)(2,1)S(1)} %bitcast.9, bf16[2,8,8,512]{3,2,1,0:T(8,128)(2,1)S(1)} %bitcast.13, bf16[2,2,8,512]{3,2,1,0:T(8,128)(2,1)S(1)} %collective-permute-done.refs_0_, ...), custom_call_target="tpu_custom_call" | custom-call | flops 301989888 | bytes 1048576 | tf_op jit(solution)/shard_map/kernel_grad/pallas_call | solution.py:404
  12.1 0.0 copy-start.2
  12.1 0.1 collective-permute-start.3
  12.2 1.5 %collective-permute-done.3 = f32[432,128]{1,0:T(8,128)S(1)} collective-permute-done((f32[432,128]{1,0:T(8,128)S(1)}, f32[432,128]{1,0:T(8,128)S(1)}, u32[]{:S(2)}, u32[]{:S(2)}) %collective-permute-start.3) | collective-permute-done | bytes 221216 | tf_op jit(solution)/shard_map/ppermute | solution.py:438
  13.7 1.3 %collective-permute-start.4 = (bf16[448,128]{1,0:T(8,128)(2,1)S(1)}, bf16[448,128]{1,0:T(8,128)(2,1)S(1)}, u32[]{:S(2)}, u32[]{:S(2)}) collective-permute-start(bf16[448,128]{1,0:T(8,128)(2,1)S(1)} %pad_maximum_fusion.1), channel_id=1, source_target_pairs={{0,8},{1,5},{2,10},{3,7},{4,12},{5,1},{6,14},{7,3},{8,0},{9,13},{1... | collective-permute-start | bytes 344072 | tf_op jit(solution)/shard_map/ppermute | solution.py:470
  15.0 0.0 copy-done.2
  15.0 0.3 %weights.1 = (bf16[9,256,128]{2,1,0:T(8,128)(2,1)S(1)}, bf16[9,128,256]{2,1,0:T(8,128)(2,1)S(1)}) custom-call(bf16[27,64,64]{2,1,0:T(8,128)(2,1)S(1)} %bitcast.15), custom_call_target="tpu_custom_call" | custom-call | bytes 1048576 | tf_op jit(solution)/shard_map/weights/pallas_call | solution.py:418
  15.3 1.3 %collective-permute-start.5 = (bf16[16,128]{1,0:T(8,128)(2,1)S(1)}, bf16[16,128]{1,0:T(8,128)(2,1)S(1)}, u32[]{:S(2)}, u32[]{:S(2)}) collective-permute-start(bf16[16,128]{1,0:T(8,128)(2,1)S(1)} %get-tuple-element.28), channel_id=1, source_target_pairs={{0,2},{2,0},{4,10},{6,8},{8,6},{10,4},{12,14},{14,12},{1,3},{3,1},... | collective-permute-start | bytes 12296 | tf_op jit(solution)/shard_map/ppermute | solution.py:447
  16.7 2.9 %collective-permute-done.4.refs_3_ = bf16[448,128]{1,0:T(8,128)(2,1)S(1)} collective-permute-done((bf16[448,128]{1,0:T(8,128)(2,1)S(1)}, bf16[448,128]{1,0:T(8,128)(2,1)S(1)}, u32[]{:S(2)}, u32[]{:S(2)}) %collective-permute-start.4) | collective-permute-done | bytes 114720 | tf_op jit(solution)/shard_map/ppermute | solution.py:470
  19.6 0.0 collective-permute-done.5.refs_5_
  19.6 0.7 %collective-permute-start.6 = (bf16[448,128]{1,0:T(8,128)(2,1)S(1)}, bf16[448,128]{1,0:T(8,128)(2,1)S(1)}, u32[]{:S(2)}, u32[]{:S(2)}) collective-permute-start(bf16[448,128]{1,0:T(8,128)(2,1)S(1)} %pad_maximum_fusion), channel_id=1, source_target_pairs={{0,2},{1,9},{2,0},{3,11},{4,6},{5,13},{6,4},{7,15},{8,10},{9,1},{1... | collective-permute-start | bytes 344072 | tf_op jit(solution)/shard_map/ppermute | solution.py:470
  20.3 4.2 %collective-permute-done.6.refs_4_ = bf16[448,128]{1,0:T(8,128)(2,1)S(1)} collective-permute-done((bf16[448,128]{1,0:T(8,128)(2,1)S(1)}, bf16[448,128]{1,0:T(8,128)(2,1)S(1)}, u32[]{:S(2)}, u32[]{:S(2)}) %collective-permute-start.6) | collective-permute-done | bytes 114720 | tf_op jit(solution)/shard_map/ppermute | solution.py:470
  24.5 2.4 %collective-permute-start.7 = (bf16[432,128]{1,0:T(8,128)(2,1)S(1)}, bf16[432,128]{1,0:T(8,128)(2,1)S(1)}, u32[]{:S(2)}, u32[]{:S(2)}) collective-permute-start(bf16[432,128]{1,0:T(8,128)(2,1)S(1)} %add_convert_fusion), channel_id=1, source_target_pairs={{0,4},{1,3},{2,6},{3,1},{4,0},{5,7},{6,2},{7,5},{8,12},{9,11},{10,... | collective-permute-start | bytes 331784 | tf_op jit(solution)/shard_map/ppermute | solution.py:470
  26.9 1.5 %response.1 = bf16[128,512]{1,0:T(8,128)(2,1)} custom-call(bf16[2,8,8,512]{3,2,1,0:T(8,128)(2,1)S(1)} %bitcast.10, bf16[2,2,8,512]{3,2,1,0:T(8,128)(2,1)S(1)} %collective-permute-done.refs_0_, bf16[2,8,512]{2,1,0:T(8,128)(2,1)S(1)} %collective-permute-done.1.refs_1_, bf16[2,8,512]{2,1,0:T(8,128)(2,1)S(1)} %collective-permute-done.2.refs_2_, ...), custom_call_target="tpu_custom_call" | custom-call | flops 301989888 | bytes 1048576 | tf_op jit(solution)/shard_map/response/pallas_call | solution.py:427
  28.5 1.2 %collective-permute-done.7 = bf16[432,128]{1,0:T(8,128)(2,1)S(1)} collective-permute-done((bf16[432,128]{1,0:T(8,128)(2,1)S(1)}, bf16[432,128]{1,0:T(8,128)(2,1)S(1)}, u32[]{:S(2)}, u32[]{:S(2)}) %collective-permute-start.7) | collective-permute-done | bytes 110624 | tf_op jit(solution)/shard_map/ppermute | solution.py:470
  29.7 0.1 collective-permute-start.8
  29.8 1.5 %feature_grad.1 = bf16[128,512]{1,0:T(8,128)(2,1)} custom-call(bf16[2,8,8,512]{3,2,1,0:T(8,128)(2,1)S(1)} %bitcast.14, bf16[2,2,8,512]{3,2,1,0:T(8,128)(2,1)S(1)} %collective-permute-done.refs_0_, bf16[2,8,512]{2,1,0:T(8,128)(2,1)S(1)} %collective-permute-done.1.refs_1_, bf16[2,8,512]{2,1,0:T(8,128)(2,1)S(1)} %collective-permute-done.2.refs_2_, ...), custom_call_target="tpu_custom_call" | custom-call | flops 301989888 | bytes 1048576 | tf_op jit(solution)/shard_map/feature_grad/pallas_call | solution.py:427
  31.3 0.0 collective-permute-done.8.other_ref
  31.3 1.1 %unpack.1 = f32[9,192,64]{2,1,0:T(8,128)} custom-call(f32[432,128]{1,0:T(8,128)S(1)} %convert_add_fusion.own_ref, f32[432,128]{1,0:T(8,128)S(1)} %collective-permute-done.8.other_ref), custom_call_target="tpu_custom_call" | custom-call | bytes 1048576 | tf_op jit(solution)/shard_map/unpack/pallas_call | solution.py:480
  (6 shorter events, 0.1 us)
Async XLA Ops:
  0.6 5.0 %copy-start = (bf16[1,2,8,8,512]{4,3,2,1,0:T(8,128)(2,1)S(1)}, bf16[1,2,8,8,512]{4,3,2,1,0:T(8,128)(2,1)}, u32[]{:S(2)}) copy-start(bf16[1,2,8,8,512]{4,3,2,1,0:T(8,128)(2,1)} %param.4) | copy-start | bytes 393220
  0.6 5.0 %copy-start.1 = (bf16[1,2,8,8,512]{4,3,2,1,0:T(8,128)(2,1)S(1)}, bf16[1,2,8,8,512]{4,3,2,1,0:T(8,128)(2,1)}, u32[]{:S(2)}) copy-start(bf16[1,2,8,8,512]{4,3,2,1,0:T(8,128)(2,1)} %param.5) | copy-start | bytes 393220
  1.5 9.5 %collective-permute-start = (bf16[2,2,8,512]{3,2,1,0:T(8,128)(2,1)S(1)}, bf16[2,2,8,512]{3,2,1,0:T(8,128)(2,1)S(1)}, u32[]{:S(2)}, u32[]{:S(2)}) collective-permute-start(bf16[2,2,8,512]{3,2,1,0:T(8,128)(2,1)S(1)} %get-tuple-element.21), channel_id=1, source_target_pairs={{0,8},{2,10},{4,12},{6,14},{8,0},{10,2},{12,4},{14,6},{1,9},{3,11}... | collective-permute-start | bytes 98312 | tf_op jit(solution)/shard_map/ppermute | solution.py:394
  5.7 3.8 %collective-permute-start.1 = (bf16[2,8,512]{2,1,0:T(8,128)(2,1)S(1)}, bf16[2,8,512]{2,1,0:T(8,128)(2,1)S(1)}, u32[]{:S(2)}, u32[]{:S(2)}) collective-permute-start(bf16[2,8,512]{2,1,0:T(8,128)(2,1)S(1)} %get-tuple-element.23), channel_id=1, source_target_pairs={{0,2},{2,0},{4,6},{6,4},{8,10},{10,8},{12,14},{14,12},{1,3},{3,1},... | collective-permute-start | bytes 49160 | tf_op jit(solution)/shard_map/ppermute | solution.py:401
  7.3 3.7 %collective-permute-start.2 = (bf16[2,8,512]{2,1,0:T(8,128)(2,1)S(1)}, bf16[2,8,512]{2,1,0:T(8,128)(2,1)S(1)}, u32[]{:S(2)}, u32[]{:S(2)}) collective-permute-start(bf16[2,8,512]{2,1,0:T(8,128)(2,1)S(1)} %get-tuple-element.24), channel_id=1, source_target_pairs={{0,2},{2,0},{4,10},{6,8},{8,6},{10,4},{12,14},{14,12},{1,3},{3,1},... | collective-permute-start | bytes 49160 | tf_op jit(solution)/shard_map/ppermute | solution.py:401
  12.1 2.9 %copy-start.2 = (bf16[3,3,3,64,64]{4,3,2,1,0:T(8,128)(2,1)S(1)}, bf16[3,3,3,64,64]{4,3,2,1,0:T(8,128)(2,1)}, u32[]{:S(2)}) copy-start(bf16[3,3,3,64,64]{4,3,2,1,0:T(8,128)(2,1)} %param.6) | copy-start | bytes 663556
  12.1 1.5 %collective-permute-start.3 = (f32[432,128]{1,0:T(8,128)S(1)}, f32[432,128]{1,0:T(8,128)S(1)}, u32[]{:S(2)}, u32[]{:S(2)}) collective-permute-start(f32[432,128]{1,0:T(8,128)S(1)} %get-tuple-element.26), channel_id=1, source_target_pairs={{0,1},{1,0},{2,3},{3,2},{4,5},{5,4},{6,7},{7,6},{8,9},{9,8},{10,11... | collective-permute-start | bytes 663560 | tf_op jit(solution)/shard_map/ppermute | solution.py:438
  13.7 5.9 %collective-permute-start.4 = (bf16[448,128]{1,0:T(8,128)(2,1)S(1)}, bf16[448,128]{1,0:T(8,128)(2,1)S(1)}, u32[]{:S(2)}, u32[]{:S(2)}) collective-permute-start(bf16[448,128]{1,0:T(8,128)(2,1)S(1)} %pad_maximum_fusion.1), channel_id=1, source_target_pairs={{0,8},{1,5},{2,10},{3,7},{4,12},{5,1},{6,14},{7,3},{8,0},{9,13},{1... | collective-permute-start | bytes 344072 | tf_op jit(solution)/shard_map/ppermute | solution.py:470
  15.3 4.3 %collective-permute-start.5 = (bf16[16,128]{1,0:T(8,128)(2,1)S(1)}, bf16[16,128]{1,0:T(8,128)(2,1)S(1)}, u32[]{:S(2)}, u32[]{:S(2)}) collective-permute-start(bf16[16,128]{1,0:T(8,128)(2,1)S(1)} %get-tuple-element.28), channel_id=1, source_target_pairs={{0,2},{2,0},{4,10},{6,8},{8,6},{10,4},{12,14},{14,12},{1,3},{3,1},... | collective-permute-start | bytes 12296 | tf_op jit(solution)/shard_map/ppermute | solution.py:447
  19.6 4.9 %collective-permute-start.6 = (bf16[448,128]{1,0:T(8,128)(2,1)S(1)}, bf16[448,128]{1,0:T(8,128)(2,1)S(1)}, u32[]{:S(2)}, u32[]{:S(2)}) collective-permute-start(bf16[448,128]{1,0:T(8,128)(2,1)S(1)} %pad_maximum_fusion), channel_id=1, source_target_pairs={{0,2},{1,9},{2,0},{3,11},{4,6},{5,13},{6,4},{7,15},{8,10},{9,1},{1... | collective-permute-start | bytes 344072 | tf_op jit(solution)/shard_map/ppermute | solution.py:470
  24.5 5.2 %collective-permute-start.7 = (bf16[432,128]{1,0:T(8,128)(2,1)S(1)}, bf16[432,128]{1,0:T(8,128)(2,1)S(1)}, u32[]{:S(2)}, u32[]{:S(2)}) collective-permute-start(bf16[432,128]{1,0:T(8,128)(2,1)S(1)} %add_convert_fusion), channel_id=1, source_target_pairs={{0,4},{1,3},{2,6},{3,1},{4,0},{5,7},{6,2},{7,5},{8,12},{9,11},{10,... | collective-permute-start | bytes 331784 | tf_op jit(solution)/shard_map/ppermute | solution.py:470
  29.7 1.6 %collective-permute-start.8 = (f32[432,128]{1,0:T(8,128)S(1)}, f32[432,128]{1,0:T(8,128)S(1)}, u32[]{:S(2)}, u32[]{:S(2)}) collective-permute-start(f32[432,128]{1,0:T(8,128)S(1)} %convert_add_fusion.own_ref), channel_id=1, source_target_pairs={{0,1},{1,0},{2,3},{3,2},{4,5},{5,4},{6,7},{7,6},{8,9},{9,8},{10,11... | collective-permute-start | bytes 663560 | tf_op jit(solution)/shard_map/ppermute | solution.py:476

commit v5 on v4

--- a/solution.py
+++ b/solution.py
@@ -60,12 +60,8 @@
 
 def completed(pairs, tiles):
     idle = [tile for tile in range(tiles) if all(tile != a for a, _ in pairs) and all(tile != b for _, b in pairs)]
-    near = [tile for tile in idle if tile ^ 1 in idle]
-    rest = [tile for tile in idle if tile ^ 1 not in idle]
-    pairs = pairs + [(tile, tile ^ 1) for tile in near]
-    for low, high in zip(rest[::2], rest[1::2]):
-        pairs = pairs + [(low, high), (high, low)]
-    return sorted(pairs)
+    active = [(2 * a + core, 2 * b + core) for a, b in pairs for core in range(2)]
+    return sorted(active + [(2 * tile + core, 2 * tile + 1 - core) for tile in idle for core in range(2)])
 
 
 def make_plan(tiles):
@@ -75,11 +71,12 @@
     along_x, along_y, hops = rounds(edges(step_x)), rounds(edges(step_y)), detours(tiles)
     pairs = [[[(tile, one[tile][0]) for tile in sorted(one)] for one in kind] for kind in (along_x, along_y)]
     pairs.append([[hop[:2] for hop in one] for one in hops])
+    meetings = pairs[0]
     pairs = [[completed(one, tiles) for one in kind] for kind in pairs]
     roles = [[{tile: one[tile][1] for tile in one} for one in kind] for kind in (along_x, along_y)]
     roles.append([{hop[0]: (hop[2], 1 - hop[3]) for hop in one} for one in hops])
     roles.append([{hop[1]: hop[2:] for hop in one} for one in hops])
-    return pairs, roles
+    return pairs, roles, meetings
 
 
 class Roles:
@@ -234,10 +231,14 @@
     right = jnp.concatenate(right, axis=1)
     low = lax.broadcasted_iota(jnp.int32, (3 * channels // 2, lanes), 1) < channels
     half = 3 * channels // 2
+    left = []
     for row in range(3):
         value = wide[:, edge * row : edge * row + rows, :].reshape(bricks * rows, -1).astype(BF16)
-        left = jnp.concatenate([value[:, lanes * k : lanes * (k + 2)] for k in range(pairs)], axis=0)
-        grad = lax.dot_general(left, right, (((0,), (0,)), ((), ())), preferred_element_type=F32)
+        left.append(jnp.concatenate([value[:, lanes * k : lanes * (k + 2)] for k in range(pairs)], axis=0))
+    left = jnp.concatenate(left, axis=1)
+    every = lax.dot_general(left, right, (((0,), (0,)), ((), ())), preferred_element_type=F32)
+    for row in range(3):
+        grad = every[2 * lanes * row : 2 * lanes * (row + 1)]
         for col in range(3):
             block = grad[:, lanes * col : lanes * (col + 1)]
             moved = pltpu.roll(block, channels, 1)
@@ -370,7 +371,7 @@
 
 
 def body(tiles, features, cotangent, kernel, neighbours):
-    pairs, roles = make_plan(tiles)
+    pairs, roles, meetings = make_plan(tiles)
     counts = [len(kind) for kind in pairs]
     bricks, edge = features.shape[1:3]
     width = features.shape[-1]
@@ -391,14 +392,14 @@
         name="x_faces",
         vmem=None,
     )(f, c, links)
-    got = [lax.ppermute(x, "space", one) for x, one in zip(faces, pairs[0])]
+    got = [lax.ppermute(x, ("space", "dp"), one) for x, one in zip(faces, pairs[0])]
     faces = call(
         functools.partial(y_faces_kernel, roles, tiles),
         [VMEM] * 3,
         [pltpu.VMEM((2, edge, width), BF16)] * counts[1],
         name="y_faces",
     )(f, c, flags)
-    got += [lax.ppermute(x, "space", one) for x, one in zip(faces, pairs[1])]
+    got += [lax.ppermute(x, ("space", "dp"), one) for x, one in zip(faces, pairs[1])]
     count = 27 * channels * channels // lanes // 2
     line_rows = 4 * width // lanes
     keep, send, *lines = call(
@@ -439,15 +440,15 @@
     bits = [1 << number for number in range(tiles.bit_length() - 1)]
     orders = [bits, bits]
     wire = BF16 if len(bits) <= 3 else F32
-    shared = [bit for bit in bits if pairs[0] == [[(i, i ^ bit) for i in range(tiles)]]]
+    shared = [bit for bit in bits if meetings == [[(i, i ^ bit) for i in range(tiles)]]]
     joined = bool(shared) and len(bits) == 3
     if joined:
         first, last = (bit for bit in bits if bit not in shared)
         orders = [shared + [first, last], [last] + shared + [first]]
-    hops = [lax.ppermute(x, "space", one) for x, one in zip(lines[counts[0] :], pairs[2])]
+    hops = [lax.ppermute(x, ("space", "dp"), one) for x, one in zip(lines[counts[0] :], pairs[2])]
     lines = lines[: counts[0]]
     if not joined:
-        got += [lax.ppermute(x, "space", one) for x, one in zip(lines, pairs[0])]
+        got += [lax.ppermute(x, ("space", "dp"), one) for x, one in zip(lines, pairs[0])]
     ready = 2 if joined else 1
     for number in range(len(bits)):
         step = [

time: 32.6 us -> 31.2 us (0.957)
  waiting for transfers between devices: 12.9 us -> 11.2 us
    ppermute x3, starting transfers between devices: 4.42 us -> 6.46 us  [body(): theirs = lax.ppermute(mine, ('space', 'dp'), step)]
    ppermute x4, starting transfers between devices: 7.53 us -> 5.73 us  [body(): lax.ppermute(x, ('space', 'dp'), one)]
    ppermute x4, waiting for transfers between devices: 3.21 us -> 2.25 us  [body(): lax.ppermute(x, ('space', 'dp'), one)]
    ppermute x3, waiting for transfers between devices: 8.24 us -> 7.46 us  [body(): theirs = lax.ppermute(mine, ('space', 'dp'), step)]
  transfers between devices with their start and end apart: 9 -> 9, of which waited for: 6 -> 5; matrix products, arithmetic and copies ran while one was open for 0% -> 0% of each run, Pallas kernels for 11% -> 11%
where the time goes in v5:
time: 31.2 us; the launch traced here: 30.8 us
  starting transfers between devices  12.3 us (39%)
  waiting for transfers between devices  11.2 us (36%)
  Pallas kernels  6.38 us (20%)
  between operations  0.75 us (2%)
    ppermute x3, waiting for transfers between devices, body(): theirs = lax.ppermute(mine, ('space', 'dp'), step)  7.46 us
    ppermute x3, starting transfers between devices, body(): theirs = lax.ppermute(mine, ('space', 'dp'), step)  6.46 us
    ppermute x4, starting transfers between devices, body(): lax.ppermute(x, ('space', 'dp'), one)  5.73 us
    pallas_call x2, Pallas kernels, conv(): call(functools.partial(conv_kernel, roles, tiles, channels, source, ready...  3.06 us
    ppermute x4, waiting for transfers between devices, body(): lax.ppermute(x, ('space', 'dp'), one)  2.25 us
    ppermute x1, waiting for transfers between devices, body(): part = keep + lax.ppermute(send, 'dp', swap)  1.46 us
    pallas_call x1, Pallas kernels, body(): call(functools.partial(unpack_kernel, 1.0 / math.sqrt(cells)), [VMEM, VME...  1.07 us
    pallas_call x1, Pallas kernels, body(): call(functools.partial(kernel_grad_kernel, roles, tiles, channels), [VMEM...  0.96 us
  transfers between devices with their start and end apart: 9, of which 5 were waited for; matrix products, arithmetic and copies ran while one was open for 0% of the time, Pallas kernels for 11%

profile of v5, /device:TPU:0, one launch (start us, length us, event | category | flops | bytes accessed | tf_op | source)
XLA Modules:
  0.0 30.8 jit_solution(4205604694702136029)
XLA Ops:
  0.6 0.0 copy-start
  0.6 0.0 copy-start.1
  0.7 0.9 %x_faces.1 = (bf16[2,2,8,512]{3,2,1,0:T(8,128)(2,1)S(1)}, f32[16,512]{1,0:T(8,128)S(1)}) custom-call(bf16[2,8,8,512]{3,2,1,0:T(8,128)(2,1)} %bitcast.7, bf16[2,8,8,512]{3,2,1,0:T(8,128)(2,1)} %bitcast.11, s32[2,6]{1,0:T(2,128)} %bitcast.19), custom_call_target="tpu_custom_call" | custom-call | bytes 1048576 | tf_op jit(solution)/shard_map/x_faces/pallas_call | solution.py:387
  1.5 4.1 %collective-permute-start = (bf16[2,2,8,512]{3,2,1,0:T(8,128)(2,1)S(1)}, bf16[2,2,8,512]{3,2,1,0:T(8,128)(2,1)S(1)}, u32[]{:S(2)}, u32[]{:S(2)}) collective-permute-start(bf16[2,2,8,512]{3,2,1,0:T(8,128)(2,1)S(1)} %get-tuple-element.21), channel_id=1, source_target_pairs={{0,8},{1,9},{2,10},{3,11},{4,12},{5,13},{6,14},{7,15},{8,0},{9,1},... | collective-permute-start | bytes 98312 | tf_op jit(solution)/shard_map/ppermute | solution.py:395
  5.6 0.0 copy-done
  5.6 0.0 copy-done.1
  5.7 0.1 y_faces.1
  5.7 1.6 %collective-permute-start.1 = (bf16[2,8,512]{2,1,0:T(8,128)(2,1)S(1)}, bf16[2,8,512]{2,1,0:T(8,128)(2,1)S(1)}, u32[]{:S(2)}, u32[]{:S(2)}) collective-permute-start(bf16[2,8,512]{2,1,0:T(8,128)(2,1)S(1)} %get-tuple-element.23), channel_id=1, source_target_pairs={{0,2},{1,3},{2,0},{3,1},{4,6},{5,7},{6,4},{7,5},{8,10},{9,11},{10,... | collective-permute-start | bytes 49160 | tf_op jit(solution)/shard_map/ppermute | solution.py:402
  7.3 0.0 collective-permute-start.2
  7.3 2.2 %collective-permute-done.1.refs_1_ = bf16[2,8,512]{2,1,0:T(8,128)(2,1)S(1)} collective-permute-done((bf16[2,8,512]{2,1,0:T(8,128)(2,1)S(1)}, bf16[2,8,512]{2,1,0:T(8,128)(2,1)S(1)}, u32[]{:S(2)}, u32[]{:S(2)}) %collective-permute-start.1) | collective-permute-done | bytes 16416 | tf_op jit(solution)/shard_map/ppermute | solution.py:402
  9.5 0.0 collective-permute-done.2.refs_2_
  9.5 0.0 collective-permute-done.refs_0_
  9.5 1.0 %kernel_grad.1 = (f32[432,128]{1,0:T(8,128)S(1)}, f32[432,128]{1,0:T(8,128)S(1)}, bf16[16,128]{1,0:T(8,128)(2,1)S(1)}, bf16[16,128]{1,0:T(8,128)(2,1)S(1)}) custom-call(bf16[2,8,8,512]{3,2,1,0:T(8,128)(2,1)S(1)} %bitcast.9, bf16[2,8,8,512]{3,2,1,0:T(8,128)(2,1)S(1)} %bitcast.13, bf16[2,2,8,512]{3,2,1,0:T(8,128)(2,1)S(1)} %collective-permute-done.refs_0_, ...), custom_call_target="tpu_custom_call" | custom-call | flops 301989888 | bytes 1048576 | tf_op jit(solution)/shard_map/kernel_grad/pallas_call | solution.py:405
  10.5 0.0 copy-start.2
  10.5 0.1 collective-permute-start.3
  10.6 1.5 %collective-permute-done.3 = f32[432,128]{1,0:T(8,128)S(1)} collective-permute-done((f32[432,128]{1,0:T(8,128)S(1)}, f32[432,128]{1,0:T(8,128)S(1)}, u32[]{:S(2)}, u32[]{:S(2)}) %collective-permute-start.3) | collective-permute-done | bytes 221216 | tf_op jit(solution)/shard_map/ppermute | solution.py:439
  12.1 2.8 %collective-permute-start.4 = (bf16[448,128]{1,0:T(8,128)(2,1)S(1)}, bf16[448,128]{1,0:T(8,128)(2,1)S(1)}, u32[]{:S(2)}, u32[]{:S(2)}) collective-permute-start(bf16[448,128]{1,0:T(8,128)(2,1)S(1)} %pad_maximum_fusion.1), channel_id=1, source_target_pairs={{0,8},{1,5},{2,10},{3,7},{4,12},{5,1},{6,14},{7,3},{8,0},{9,13},{1... | collective-permute-start | bytes 344072 | tf_op jit(solution)/shard_map/ppermute | solution.py:471
  14.9 0.0 copy-done.2
  14.9 0.3 %weights.1 = (bf16[9,256,128]{2,1,0:T(8,128)(2,1)S(1)}, bf16[9,128,256]{2,1,0:T(8,128)(2,1)S(1)}) custom-call(bf16[27,64,64]{2,1,0:T(8,128)(2,1)S(1)} %bitcast.15), custom_call_target="tpu_custom_call" | custom-call | bytes 1048576 | tf_op jit(solution)/shard_map/weights/pallas_call | solution.py:419
  15.2 0.1 collective-permute-start.5
  15.3 2.8 %collective-permute-done.4.refs_3_ = bf16[448,128]{1,0:T(8,128)(2,1)S(1)} collective-permute-done((bf16[448,128]{1,0:T(8,128)(2,1)S(1)}, bf16[448,128]{1,0:T(8,128)(2,1)S(1)}, u32[]{:S(2)}, u32[]{:S(2)}) %collective-permute-start.4) | collective-permute-done | bytes 114720 | tf_op jit(solution)/shard_map/ppermute | solution.py:471
  18.2 0.0 collective-permute-done.5.refs_5_
  18.2 1.4 %collective-permute-start.6 = (bf16[448,128]{1,0:T(8,128)(2,1)S(1)}, bf16[448,128]{1,0:T(8,128)(2,1)S(1)}, u32[]{:S(2)}, u32[]{:S(2)}) collective-permute-start(bf16[448,128]{1,0:T(8,128)(2,1)S(1)} %pad_maximum_fusion), channel_id=1, source_target_pairs={{0,2},{1,9},{2,0},{3,11},{4,6},{5,13},{6,4},{7,15},{8,10},{9,1},{1... | collective-permute-start | bytes 344072 | tf_op jit(solution)/shard_map/ppermute | solution.py:471
  19.6 3.5 %collective-permute-done.6.refs_4_ = bf16[448,128]{1,0:T(8,128)(2,1)S(1)} collective-permute-done((bf16[448,128]{1,0:T(8,128)(2,1)S(1)}, bf16[448,128]{1,0:T(8,128)(2,1)S(1)}, u32[]{:S(2)}, u32[]{:S(2)}) %collective-permute-start.6) | collective-permute-done | bytes 114720 | tf_op jit(solution)/shard_map/ppermute | solution.py:471
  23.1 2.3 %collective-permute-start.7 = (bf16[432,128]{1,0:T(8,128)(2,1)S(1)}, bf16[432,128]{1,0:T(8,128)(2,1)S(1)}, u32[]{:S(2)}, u32[]{:S(2)}) collective-permute-start(bf16[432,128]{1,0:T(8,128)(2,1)S(1)} %add_convert_fusion), channel_id=1, source_target_pairs={{0,4},{1,3},{2,6},{3,1},{4,0},{5,7},{6,2},{7,5},{8,12},{9,11},{10,... | collective-permute-start | bytes 331784 | tf_op jit(solution)/shard_map/ppermute | solution.py:471
  25.4 1.5 %response.1 = bf16[128,512]{1,0:T(8,128)(2,1)} custom-call(bf16[2,8,8,512]{3,2,1,0:T(8,128)(2,1)S(1)} %bitcast.10, bf16[2,2,8,512]{3,2,1,0:T(8,128)(2,1)S(1)} %collective-permute-done.refs_0_, bf16[2,8,512]{2,1,0:T(8,128)(2,1)S(1)} %collective-permute-done.1.refs_1_, bf16[2,8,512]{2,1,0:T(8,128)(2,1)S(1)} %collective-permute-done.2.refs_2_, ...), custom_call_target="tpu_custom_call" | custom-call | flops 301989888 | bytes 1048576 | tf_op jit(solution)/shard_map/response/pallas_call | solution.py:428
  26.9 1.2 %collective-permute-done.7 = bf16[432,128]{1,0:T(8,128)(2,1)S(1)} collective-permute-done((bf16[432,128]{1,0:T(8,128)(2,1)S(1)}, bf16[432,128]{1,0:T(8,128)(2,1)S(1)}, u32[]{:S(2)}, u32[]{:S(2)}) %collective-permute-start.7) | collective-permute-done | bytes 110624 | tf_op jit(solution)/shard_map/ppermute | solution.py:471
  28.1 0.1 collective-permute-start.8
  28.2 1.5 %feature_grad.1 = bf16[128,512]{1,0:T(8,128)(2,1)} custom-call(bf16[2,8,8,512]{3,2,1,0:T(8,128)(2,1)S(1)} %bitcast.14, bf16[2,2,8,512]{3,2,1,0:T(8,128)(2,1)S(1)} %collective-permute-done.refs_0_, bf16[2,8,512]{2,1,0:T(8,128)(2,1)S(1)} %collective-permute-done.1.refs_1_, bf16[2,8,512]{2,1,0:T(8,128)(2,1)S(1)} %collective-permute-done.2.refs_2_, ...), custom_call_target="tpu_custom_call" | custom-call | flops 301989888 | bytes 1048576 | tf_op jit(solution)/shard_map/feature_grad/pallas_call | solution.py:428
  29.7 0.0 collective-permute-done.8.other_ref
  29.7 1.1 %unpack.1 = f32[9,192,64]{2,1,0:T(8,128)} custom-call(f32[432,128]{1,0:T(8,128)S(1)} %convert_add_fusion.own_ref, f32[432,128]{1,0:T(8,128)S(1)} %collective-permute-done.8.other_ref), custom_call_target="tpu_custom_call" | custom-call | bytes 1048576 | tf_op jit(solution)/shard_map/unpack/pallas_call | solution.py:481
  (6 shorter events, 0.1 us)
Async XLA Ops:
  0.6 5.0 %copy-start = (bf16[1,2,8,8,512]{4,3,2,1,0:T(8,128)(2,1)S(1)}, bf16[1,2,8,8,512]{4,3,2,1,0:T(8,128)(2,1)}, u32[]{:S(2)}) copy-start(bf16[1,2,8,8,512]{4,3,2,1,0:T(8,128)(2,1)} %param.4) | copy-start | bytes 393220
  0.6 5.0 %copy-start.1 = (bf16[1,2,8,8,512]{4,3,2,1,0:T(8,128)(2,1)S(1)}, bf16[1,2,8,8,512]{4,3,2,1,0:T(8,128)(2,1)}, u32[]{:S(2)}) copy-start(bf16[1,2,8,8,512]{4,3,2,1,0:T(8,128)(2,1)} %param.5) | copy-start | bytes 393220
  1.5 8.0 %collective-permute-start = (bf16[2,2,8,512]{3,2,1,0:T(8,128)(2,1)S(1)}, bf16[2,2,8,512]{3,2,1,0:T(8,128)(2,1)S(1)}, u32[]{:S(2)}, u32[]{:S(2)}) collective-permute-start(bf16[2,2,8,512]{3,2,1,0:T(8,128)(2,1)S(1)} %get-tuple-element.21), channel_id=1, source_target_pairs={{0,8},{1,9},{2,10},{3,11},{4,12},{5,13},{6,14},{7,15},{8,0},{9,1},... | collective-permute-start | bytes 98312 | tf_op jit(solution)/shard_map/ppermute | solution.py:395
  5.7 3.8 %collective-permute-start.1 = (bf16[2,8,512]{2,1,0:T(8,128)(2,1)S(1)}, bf16[2,8,512]{2,1,0:T(8,128)(2,1)S(1)}, u32[]{:S(2)}, u32[]{:S(2)}) collective-permute-start(bf16[2,8,512]{2,1,0:T(8,128)(2,1)S(1)} %get-tuple-element.23), channel_id=1, source_target_pairs={{0,2},{1,3},{2,0},{3,1},{4,6},{5,7},{6,4},{7,5},{8,10},{9,11},{10,... | collective-permute-start | bytes 49160 | tf_op jit(solution)/shard_map/ppermute | solution.py:402
  7.3 2.3 %collective-permute-start.2 = (bf16[2,8,512]{2,1,0:T(8,128)(2,1)S(1)}, bf16[2,8,512]{2,1,0:T(8,128)(2,1)S(1)}, u32[]{:S(2)}, u32[]{:S(2)}) collective-permute-start(bf16[2,8,512]{2,1,0:T(8,128)(2,1)S(1)} %get-tuple-element.24), channel_id=1, source_target_pairs={{0,1},{1,0},{2,3},{3,2},{4,5},{5,4},{6,8},{7,9},{8,6},{9,7},{10,11... | collective-permute-start | bytes 49160 | tf_op jit(solution)/shard_map/ppermute | solution.py:402
  10.5 4.4 %copy-start.2 = (bf16[3,3,3,64,64]{4,3,2,1,0:T(8,128)(2,1)S(1)}, bf16[3,3,3,64,64]{4,3,2,1,0:T(8,128)(2,1)}, u32[]{:S(2)}) copy-start(bf16[3,3,3,64,64]{4,3,2,1,0:T(8,128)(2,1)} %param.6) | copy-start | bytes 663556
  10.5 1.5 %collective-permute-start.3 = (f32[432,128]{1,0:T(8,128)S(1)}, f32[432,128]{1,0:T(8,128)S(1)}, u32[]{:S(2)}, u32[]{:S(2)}) collective-permute-start(f32[432,128]{1,0:T(8,128)S(1)} %get-tuple-element.26), channel_id=1, source_target_pairs={{0,1},{1,0},{2,3},{3,2},{4,5},{5,4},{6,7},{7,6},{8,9},{9,8},{10,11... | collective-permute-start | bytes 663560 | tf_op jit(solution)/shard_map/ppermute | solution.py:439
  12.1 6.0 %collective-permute-start.4 = (bf16[448,128]{1,0:T(8,128)(2,1)S(1)}, bf16[448,128]{1,0:T(8,128)(2,1)S(1)}, u32[]{:S(2)}, u32[]{:S(2)}) collective-permute-start(bf16[448,128]{1,0:T(8,128)(2,1)S(1)} %pad_maximum_fusion.1), channel_id=1, source_target_pairs={{0,8},{1,5},{2,10},{3,7},{4,12},{5,1},{6,14},{7,3},{8,0},{9,13},{1... | collective-permute-start | bytes 344072 | tf_op jit(solution)/shard_map/ppermute | solution.py:471
  15.2 2.9 %collective-permute-start.5 = (bf16[16,128]{1,0:T(8,128)(2,1)S(1)}, bf16[16,128]{1,0:T(8,128)(2,1)S(1)}, u32[]{:S(2)}, u32[]{:S(2)}) collective-permute-start(bf16[16,128]{1,0:T(8,128)(2,1)S(1)} %get-tuple-element.28), channel_id=1, source_target_pairs={{0,1},{1,0},{2,3},{3,2},{4,5},{5,4},{6,8},{7,9},{8,6},{9,7},{10,11... | collective-permute-start | bytes 12296 | tf_op jit(solution)/shard_map/ppermute | solution.py:448
  18.2 4.9 %collective-permute-start.6 = (bf16[448,128]{1,0:T(8,128)(2,1)S(1)}, bf16[448,128]{1,0:T(8,128)(2,1)S(1)}, u32[]{:S(2)}, u32[]{:S(2)}) collective-permute-start(bf16[448,128]{1,0:T(8,128)(2,1)S(1)} %pad_maximum_fusion), channel_id=1, source_target_pairs={{0,2},{1,9},{2,0},{3,11},{4,6},{5,13},{6,4},{7,15},{8,10},{9,1},{1... | collective-permute-start | bytes 344072 | tf_op jit(solution)/shard_map/ppermute | solution.py:471
  23.1 5.0 %collective-permute-start.7 = (bf16[432,128]{1,0:T(8,128)(2,1)S(1)}, bf16[432,128]{1,0:T(8,128)(2,1)S(1)}, u32[]{:S(2)}, u32[]{:S(2)}) collective-permute-start(bf16[432,128]{1,0:T(8,128)(2,1)S(1)} %add_convert_fusion), channel_id=1, source_target_pairs={{0,4},{1,3},{2,6},{3,1},{4,0},{5,7},{6,2},{7,5},{8,12},{9,11},{10,... | collective-permute-start | bytes 331784 | tf_op jit(solution)/shard_map/ppermute | solution.py:471
  28.1 1.6 %collective-permute-start.8 = (f32[432,128]{1,0:T(8,128)S(1)}, f32[432,128]{1,0:T(8,128)S(1)}, u32[]{:S(2)}, u32[]{:S(2)}) collective-permute-start(f32[432,128]{1,0:T(8,128)S(1)} %convert_add_fusion.own_ref), channel_id=1, source_target_pairs={{0,1},{1,0},{2,3},{3,2},{4,5},{5,4},{6,7},{7,6},{8,9},{9,8},{10,11... | collective-permute-start | bytes 663560 | tf_op jit(solution)/shard_map/ppermute | solution.py:477

commit v6 on v5

--- a/solution.py
+++ b/solution.py
@@ -104,6 +104,16 @@
         for number in range(self.counts[1]):
             found = found | self.side(1, number, side)
         return found
+
+
+def half_of(tile, core):
+    for shift in (16, 8, 4, 2, 1):
+        tile = tile ^ (tile >> shift)
+    return core ^ (tile & 1)
+
+
+def my_half():
+    return half_of(lax.axis_index("space"), lax.axis_index("dp"))
 
 
 def masked(keep, x):
@@ -186,16 +196,18 @@
     return jnp.concatenate([rows[each * number + k : each * number + k + 1] for k in range(each)], axis=1)
 
 
-def kernel_grad_kernel(roles, tiles, channels, f_ref, c_ref, *refs):
+def kernel_grad_kernel(roles, tiles, channels, joined, f_ref, c_ref, *refs):
     roles = Roles(roles, tiles)
     counts = roles.counts
     x_refs = refs[: counts[0]]
     y_refs = refs[counts[0] : counts[0] + counts[1]]
     near = counts[0] + counts[1]
     keep_ref, send_ref = refs[near : near + 2]
-    line_refs = refs[near + 2 : near + 2 + counts[0]]
-    hop_refs = refs[near + 2 + counts[0] : near + 2 + counts[0] + counts[2]]
-    wide, tall, packed, lines = refs[near + 2 + counts[0] + counts[2] :]
+    hops_at = near + 2 + (0 if joined else counts[0])
+    line_refs = refs[near + 2 : hops_at]
+    hop_refs = refs[hops_at : hops_at + counts[2]]
+    wide, tall, packed, lines = refs[hops_at + counts[2] :]
+    count = keep_ref.shape[0]
     bricks, edge, _, width = f_ref.shape
     rows = edge * edge
     wide[:, edge : edge + rows, :] = padded(f_ref[...].astype(F32).reshape(bricks, rows, width), channels)
@@ -246,11 +258,14 @@
             second = moved[half : 2 * half] + block[channels + half :]
             at = half * (3 * row + col)
             packed[at : at + half, :] = jnp.where(low, first, second)
-    for number, out in enumerate(line_refs):
+    for number in range(counts[0]):
         up = roles.side(0, number, 1)
         for (source, side), row in halo.items():
             store_line(lines, 2 * source + side, jnp.where(up, row[edge - 1 : edge], row[0:1]))
-        out[...] = lines[...].astype(BF16)
+        if joined:
+            send_ref[count:, :] = lines[...]
+        else:
+            line_refs[number][...] = lines[...].astype(BF16)
     for number, out in enumerate(hop_refs):
         line = jnp.zeros((1, width), F32)
         for across in range(2):
@@ -260,10 +275,9 @@
                 line = jnp.where(hit, planes[across][side, at : at + 1, :], line)
         store_line(lines, 0, line)
         out[...] = lines[...].astype(BF16)
-    count = keep_ref.shape[0]
-    core = lax.axis_index("dp")
-    keep_ref[...] = packed[pl.ds(pl.multiple_of(core * count, 8), count), :]
-    send_ref[...] = packed[pl.ds(pl.multiple_of((1 - core) * count, 8), count), :]
+    own = my_half()
+    keep_ref[...] = packed[pl.ds(pl.multiple_of(own * count, 8), count), :]
+    send_ref[:count, :] = packed[pl.ds(pl.multiple_of((1 - own) * count, 8), count), :]
 
 
 def conv_kernel(roles, tiles, channels, source, ways, v_ref, *refs):
@@ -290,8 +304,7 @@
     each = width // line_refs[0].shape[1]
     arrived = [ref[ref.shape[0] - 4 * each :, :].astype(F32) for ref in line_refs]
     if ways == 2:
-        first_core = lax.axis_index("dp") == 0
-        arrived = [jnp.where(first_core, *arrived)]
+        arrived = [jnp.where(my_half() == 1, *arrived)]
     hops = [load_line(ref[...].astype(F32), 0, each) for ref in hop_refs]
     for side in range(2):
         row = jnp.zeros((edge, width), F32)
@@ -329,7 +342,7 @@
 
 def unpack_kernel(factor, own_ref, other_ref, out_hbm, out_ref, sent):
     count = own_ref.shape[0]
-    first_half = lax.axis_index("dp") == 0
+    first_half = my_half() == 0
     taps, rows, channels = out_ref.shape
     half = rows // 2
 
@@ -400,12 +413,21 @@
         name="y_faces",
     )(f, c, flags)
     got += [lax.ppermute(x, ("space", "dp"), one) for x, one in zip(faces, pairs[1])]
+    bits = [1 << number for number in range(tiles.bit_length() - 1)]
+    orders = [bits, bits]
+    wire = BF16 if len(bits) <= 3 else F32
+    shared = [bit for bit in bits if meetings == [[(i, i ^ bit) for i in range(tiles)]]]
+    joined = bool(shared) and len(bits) == 3
+    if joined:
+        first, last = (bit for bit in bits if bit not in shared)
+        orders = [[first] + shared + [last], shared + [last, first]]
     count = 27 * channels * channels // lanes // 2
     line_rows = 4 * width // lanes
     keep, send, *lines = call(
-        functools.partial(kernel_grad_kernel, roles, tiles, channels),
+        functools.partial(kernel_grad_kernel, roles, tiles, channels, joined),
         [VMEM, VMEM] + [VMEM] * near,
-        [shape((count, lanes), F32)] * 2 + [shape((line_rows, lanes), BF16)] * (counts[0] + counts[2]),
+        [shape((count, lanes), F32), shape((count + line_rows * joined, lanes), F32)]
+        + [shape((line_rows, lanes), BF16)] * (counts[2] if joined else counts[0] + counts[2]),
         [
             pltpu.VMEM((bricks, rows + 2 * edge, width + lanes), F32),
             pltpu.VMEM((bricks, edge, 3 * edge, width), F32),
@@ -436,30 +458,23 @@
 
     cores = lax.axis_size("dp")
     swap = [(0, 1), (1, 0)]
-    part = keep + lax.ppermute(send, "dp", swap)
-    bits = [1 << number for number in range(tiles.bit_length() - 1)]
-    orders = [bits, bits]
-    wire = BF16 if len(bits) <= 3 else F32
-    shared = [bit for bit in bits if meetings == [[(i, i ^ bit) for i in range(tiles)]]]
-    joined = bool(shared) and len(bits) == 3
-    if joined:
-        first, last = (bit for bit in bits if bit not in shared)
-        orders = [shared + [first, last], [last] + shared + [first]]
-    hops = [lax.ppermute(x, ("space", "dp"), one) for x, one in zip(lines[counts[0] :], pairs[2])]
-    lines = lines[: counts[0]]
+    summed = lax.ppermute(send, "dp", swap)
+    part = keep + summed[:count]
     if not joined:
         got += [lax.ppermute(x, ("space", "dp"), one) for x, one in zip(lines, pairs[0])]
+        lines = lines[counts[0] :]
+    hops = [lax.ppermute(x, ("space", "dp"), one) for x, one in zip(lines, pairs[2])]
     ready = 2 if joined else 1
     for number in range(len(bits)):
         step = [
-            (tile * cores + core, (tile ^ order[number]) * cores + core)
+            tuple(end * cores + half_of(end, half) for end in (tile, tile ^ order[number]))
             for tile in range(tiles)
-            for core, order in enumerate(orders)
+            for half, order in enumerate(orders)
         ]
         mine = part.astype(wire)
         carries = joined and number < ready
         if carries:
-            mine = jnp.concatenate([mine, lines[0]], axis=0)
+            mine = jnp.concatenate([mine, summed[count:].astype(wire)], axis=0)
         if number == 1:
             mine, hops, forward, backward = lax.optimization_barrier((mine, hops, forward, backward))
         else:

time: 31.2 us -> 30.9 us (level)
  waiting for transfers between devices: 11.2 us -> 8.13 us
  starting transfers between devices: 12.3 us -> 15.3 us
    ppermute x3, waiting for transfers between devices: 7.46 us -> 4.4 us  [body(): theirs = lax.ppermute(mine, ('space', 'dp'), step)]
    ppermute x4, starting transfers between devices: 5.73 us -> 7.33 us  [body(): lax.ppermute(x, ('space', 'dp'), one)]
    ppermute x3, starting transfers between devices: 6.46 us -> 7.49 us  [body(): theirs = lax.ppermute(mine, ('space', 'dp'), step)]
    ppermute x1, starting transfers between devices: 0.07 us -> 0.45 us  [body(): other = lax.ppermute(part, 'dp', swap)]
where the time goes in v6:
time: 30.9 us; the launch traced here: 30.7 us
  starting transfers between devices  15.3 us (50%)
  waiting for transfers between devices  8.13 us (26%)
  Pallas kernels  6.34 us (21%)
  between operations  0.73 us (2%)
    ppermute x3, starting transfers between devices, body(): theirs = lax.ppermute(mine, ('space', 'dp'), step)  7.49 us
    ppermute x4, starting transfers between devices, body(): lax.ppermute(x, ('space', 'dp'), one)  7.33 us
    ppermute x3, waiting for transfers between devices, body(): theirs = lax.ppermute(mine, ('space', 'dp'), step)  4.4 us
    pallas_call x2, Pallas kernels, conv(): call(functools.partial(conv_kernel, roles, tiles, channels, source, ready...  3.06 us
    ppermute x4, waiting for transfers between devices, body(): lax.ppermute(x, ('space', 'dp'), one)  2.25 us
    ppermute x1, waiting for transfers between devices, body(): summed = lax.ppermute(send, 'dp', swap)  1.48 us
    pallas_call x1, Pallas kernels, body(): call(functools.partial(unpack_kernel, 1.0 / math.sqrt(cells)), [VMEM, VME...  1.07 us
    pallas_call x1, Pallas kernels, body(): call(functools.partial(kernel_grad_kernel, roles, tiles, channels, joined...  0.92 us
  transfers between devices with their start and end apart: 9, of which 5 were waited for; matrix products, arithmetic and copies ran while one was open for 0% of the time, Pallas kernels for 11%

profile of v6, /device:TPU:0, one launch (start us, length us, event | category | flops | bytes accessed | tf_op | source)
XLA Modules:
  0.0 30.7 jit_solution(6912577553269382500)
XLA Ops:
  0.6 0.0 copy-start
  0.6 0.0 copy-start.1
  0.7 0.9 %x_faces.1 = (bf16[2,2,8,512]{3,2,1,0:T(8,128)(2,1)S(1)}, f32[16,512]{1,0:T(8,128)S(1)}) custom-call(bf16[2,8,8,512]{3,2,1,0:T(8,128)(2,1)} %bitcast.7, bf16[2,8,8,512]{3,2,1,0:T(8,128)(2,1)} %bitcast.11, s32[2,6]{1,0:T(2,128)} %bitcast.19), custom_call_target="tpu_custom_call" | custom-call | bytes 1048576 | tf_op jit(solution)/shard_map/x_faces/pallas_call | solution.py:400
  1.5 4.1 %collective-permute-start = (bf16[2,2,8,512]{3,2,1,0:T(8,128)(2,1)S(1)}, bf16[2,2,8,512]{3,2,1,0:T(8,128)(2,1)S(1)}, u32[]{:S(2)}, u32[]{:S(2)}) collective-permute-start(bf16[2,2,8,512]{3,2,1,0:T(8,128)(2,1)S(1)} %get-tuple-element.20), channel_id=1, source_target_pairs={{0,8},{1,9},{2,10},{3,11},{4,12},{5,13},{6,14},{7,15},{8,0},{9,1},... | collective-permute-start | bytes 98312 | tf_op jit(solution)/shard_map/ppermute | solution.py:408
  5.6 0.0 copy-done
  5.6 0.0 copy-done.1
  5.7 0.1 y_faces.1
  5.7 1.6 %collective-permute-start.1 = (bf16[2,8,512]{2,1,0:T(8,128)(2,1)S(1)}, bf16[2,8,512]{2,1,0:T(8,128)(2,1)S(1)}, u32[]{:S(2)}, u32[]{:S(2)}) collective-permute-start(bf16[2,8,512]{2,1,0:T(8,128)(2,1)S(1)} %get-tuple-element.22), channel_id=1, source_target_pairs={{0,2},{1,3},{2,0},{3,1},{4,6},{5,7},{6,4},{7,5},{8,10},{9,11},{10,... | collective-permute-start | bytes 49160 | tf_op jit(solution)/shard_map/ppermute | solution.py:415
  7.3 0.0 collective-permute-start.2
  7.3 2.2 %collective-permute-done.1.refs_1_ = bf16[2,8,512]{2,1,0:T(8,128)(2,1)S(1)} collective-permute-done((bf16[2,8,512]{2,1,0:T(8,128)(2,1)S(1)}, bf16[2,8,512]{2,1,0:T(8,128)(2,1)S(1)}, u32[]{:S(2)}, u32[]{:S(2)}) %collective-permute-start.1) | collective-permute-done | bytes 16416 | tf_op jit(solution)/shard_map/ppermute | solution.py:415
  9.5 0.0 collective-permute-done.2.refs_2_
  9.5 0.0 collective-permute-done.refs_0_
  9.5 0.9 %kernel_grad.1 = (f32[432,128]{1,0:T(8,128)S(1)}, f32[448,128]{1,0:T(8,128)S(1)}, bf16[16,128]{1,0:T(8,128)(2,1)S(1)}) custom-call(bf16[2,8,8,512]{3,2,1,0:T(8,128)(2,1)S(1)} %bitcast.9, bf16[2,8,8,512]{3,2,1,0:T(8,128)(2,1)S(1)} %bitcast.13, bf16[2,2,8,512]{3,2,1,0:T(8,128)(2,1)S(1)} %collective-permute-done.refs_0_, ...), custom_call_target="tpu_custom_call" | custom-call | flops 301989888 | bytes 1048576 | tf_op jit(solution)/shard_map/kernel_grad/pallas_call | solution.py:426
  10.4 0.0 copy-start.2
  10.5 0.1 collective-permute-start.3
  10.5 1.5 %collective-permute-done.3 = f32[448,128]{1,0:T(8,128)S(1)} collective-permute-done((f32[448,128]{1,0:T(8,128)S(1)}, f32[448,128]{1,0:T(8,128)S(1)}, u32[]{:S(2)}, u32[]{:S(2)}) %collective-permute-start.3) | collective-permute-done | bytes 229408 | tf_op jit(solution)/shard_map/ppermute | solution.py:461
  12.1 1.3 %collective-permute-start.4 = (bf16[448,128]{1,0:T(8,128)(2,1)S(1)}, bf16[448,128]{1,0:T(8,128)(2,1)S(1)}, u32[]{:S(2)}, u32[]{:S(2)}) collective-permute-start(bf16[448,128]{1,0:T(8,128)(2,1)S(1)} %pad_maximum_fusion.1), channel_id=1, source_target_pairs={{0,3},{1,8},{3,0},{2,11},{5,6},{4,13},{6,5},{7,14},{9,10},{8,1},{1... | collective-permute-start | bytes 344072 | tf_op jit(solution)/shard_map/ppermute | solution.py:486
  13.4 0.0 copy-done.2
  13.4 0.3 %weights.1 = (bf16[9,256,128]{2,1,0:T(8,128)(2,1)S(1)}, bf16[9,128,256]{2,1,0:T(8,128)(2,1)S(1)}) custom-call(bf16[27,64,64]{2,1,0:T(8,128)(2,1)S(1)} %bitcast.15), custom_call_target="tpu_custom_call" | custom-call | bytes 1048576 | tf_op jit(solution)/shard_map/weights/pallas_call | solution.py:441
  13.7 1.7 %collective-permute-start.5 = (bf16[16,128]{1,0:T(8,128)(2,1)S(1)}, bf16[16,128]{1,0:T(8,128)(2,1)S(1)}, u32[]{:S(2)}, u32[]{:S(2)}) collective-permute-start(bf16[16,128]{1,0:T(8,128)(2,1)S(1)} %get-tuple-element.26), channel_id=1, source_target_pairs={{0,1},{1,0},{2,3},{3,2},{4,5},{5,4},{6,8},{7,9},{8,6},{9,7},{10,11... | collective-permute-start | bytes 12296 | tf_op jit(solution)/shard_map/ppermute | solution.py:466
  15.4 1.0 %collective-permute-done.4.refs_3_ = bf16[448,128]{1,0:T(8,128)(2,1)S(1)} collective-permute-done((bf16[448,128]{1,0:T(8,128)(2,1)S(1)}, bf16[448,128]{1,0:T(8,128)(2,1)S(1)}, u32[]{:S(2)}, u32[]{:S(2)}) %collective-permute-start.4) | collective-permute-done | bytes 114720 | tf_op jit(solution)/shard_map/ppermute | solution.py:486
  16.4 0.0 collective-permute-done.5.refs_5_
  16.4 3.8 %collective-permute-start.6 = (bf16[448,128]{1,0:T(8,128)(2,1)S(1)}, bf16[448,128]{1,0:T(8,128)(2,1)S(1)}, u32[]{:S(2)}, u32[]{:S(2)}) collective-permute-start(bf16[448,128]{1,0:T(8,128)(2,1)S(1)} %pad_maximum_fusion), channel_id=1, source_target_pairs={{0,9},{1,4},{3,10},{2,7},{5,12},{4,1},{6,15},{7,2},{9,0},{8,13},{1... | collective-permute-start | bytes 344072 | tf_op jit(solution)/shard_map/ppermute | solution.py:486
  20.2 2.5 %collective-permute-done.6.refs_4_ = bf16[448,128]{1,0:T(8,128)(2,1)S(1)} collective-permute-done((bf16[448,128]{1,0:T(8,128)(2,1)S(1)}, bf16[448,128]{1,0:T(8,128)(2,1)S(1)}, u32[]{:S(2)}, u32[]{:S(2)}) %collective-permute-start.6) | collective-permute-done | bytes 114720 | tf_op jit(solution)/shard_map/ppermute | solution.py:486
  22.8 2.4 %collective-permute-start.7 = (bf16[432,128]{1,0:T(8,128)(2,1)S(1)}, bf16[432,128]{1,0:T(8,128)(2,1)S(1)}, u32[]{:S(2)}, u32[]{:S(2)}) collective-permute-start(bf16[432,128]{1,0:T(8,128)(2,1)S(1)} %add_convert_fusion), channel_id=1, source_target_pairs={{0,5},{1,2},{3,6},{2,1},{5,0},{4,7},{6,3},{7,4},{9,12},{8,11},{10,... | collective-permute-start | bytes 331784 | tf_op jit(solution)/shard_map/ppermute | solution.py:486
  25.2 1.5 %response.1 = bf16[128,512]{1,0:T(8,128)(2,1)} custom-call(bf16[2,8,8,512]{3,2,1,0:T(8,128)(2,1)S(1)} %bitcast.10, bf16[2,2,8,512]{3,2,1,0:T(8,128)(2,1)S(1)} %collective-permute-done.refs_0_, bf16[2,8,512]{2,1,0:T(8,128)(2,1)S(1)} %collective-permute-done.1.refs_1_, bf16[2,8,512]{2,1,0:T(8,128)(2,1)S(1)} %collective-permute-done.2.refs_2_, ...), custom_call_target="tpu_custom_call" | custom-call | flops 301989888 | bytes 1048576 | tf_op jit(solution)/shard_map/response/pallas_call | solution.py:450
  26.7 0.9 %collective-permute-done.7 = bf16[432,128]{1,0:T(8,128)(2,1)S(1)} collective-permute-done((bf16[432,128]{1,0:T(8,128)(2,1)S(1)}, bf16[432,128]{1,0:T(8,128)(2,1)S(1)}, u32[]{:S(2)}, u32[]{:S(2)}) %collective-permute-start.7) | collective-permute-done | bytes 110624 | tf_op jit(solution)/shard_map/ppermute | solution.py:486
  27.6 0.4 %collective-permute-start.8 = (f32[432,128]{1,0:T(8,128)S(1)}, f32[432,128]{1,0:T(8,128)S(1)}, u32[]{:S(2)}, u32[]{:S(2)}) collective-permute-start(f32[432,128]{1,0:T(8,128)S(1)} %convert_add_fusion.own_ref), channel_id=1, source_target_pairs={{0,1},{1,0},{2,3},{3,2},{4,5},{5,4},{6,7},{7,6},{8,9},{9,8},{10,11... | collective-permute-start | bytes 663560 | tf_op jit(solution)/shard_map/ppermute | solution.py:492
  28.1 1.5 %feature_grad.1 = bf16[128,512]{1,0:T(8,128)(2,1)} custom-call(bf16[2,8,8,512]{3,2,1,0:T(8,128)(2,1)S(1)} %bitcast.14, bf16[2,2,8,512]{3,2,1,0:T(8,128)(2,1)S(1)} %collective-permute-done.refs_0_, bf16[2,8,512]{2,1,0:T(8,128)(2,1)S(1)} %collective-permute-done.1.refs_1_, bf16[2,8,512]{2,1,0:T(8,128)(2,1)S(1)} %collective-permute-done.2.refs_2_, ...), custom_call_target="tpu_custom_call" | custom-call | flops 301989888 | bytes 1048576 | tf_op jit(solution)/shard_map/feature_grad/pallas_call | solution.py:450
  29.6 0.0 collective-permute-done.8.other_ref
  29.6 1.1 %unpack.1 = f32[9,192,64]{2,1,0:T(8,128)} custom-call(f32[432,128]{1,0:T(8,128)S(1)} %convert_add_fusion.own_ref, f32[432,128]{1,0:T(8,128)S(1)} %collective-permute-done.8.other_ref), custom_call_target="tpu_custom_call" | custom-call | bytes 1048576 | tf_op jit(solution)/shard_map/unpack/pallas_call | solution.py:496
  (7 shorter events, 0.1 us)
Async XLA Ops:
  0.6 5.0 %copy-start = (bf16[1,2,8,8,512]{4,3,2,1,0:T(8,128)(2,1)S(1)}, bf16[1,2,8,8,512]{4,3,2,1,0:T(8,128)(2,1)}, u32[]{:S(2)}) copy-start(bf16[1,2,8,8,512]{4,3,2,1,0:T(8,128)(2,1)} %param.4) | copy-start | bytes 393220
  0.6 5.0 %copy-start.1 = (bf16[1,2,8,8,512]{4,3,2,1,0:T(8,128)(2,1)S(1)}, bf16[1,2,8,8,512]{4,3,2,1,0:T(8,128)(2,1)}, u32[]{:S(2)}) copy-start(bf16[1,2,8,8,512]{4,3,2,1,0:T(8,128)(2,1)} %param.5) | copy-start | bytes 393220
  1.5 8.0 %collective-permute-start = (bf16[2,2,8,512]{3,2,1,0:T(8,128)(2,1)S(1)}, bf16[2,2,8,512]{3,2,1,0:T(8,128)(2,1)S(1)}, u32[]{:S(2)}, u32[]{:S(2)}) collective-permute-start(bf16[2,2,8,512]{3,2,1,0:T(8,128)(2,1)S(1)} %get-tuple-element.20), channel_id=1, source_target_pairs={{0,8},{1,9},{2,10},{3,11},{4,12},{5,13},{6,14},{7,15},{8,0},{9,1},... | collective-permute-start | bytes 98312 | tf_op jit(solution)/shard_map/ppermute | solution.py:408
  5.7 3.8 %collective-permute-start.1 = (bf16[2,8,512]{2,1,0:T(8,128)(2,1)S(1)}, bf16[2,8,512]{2,1,0:T(8,128)(2,1)S(1)}, u32[]{:S(2)}, u32[]{:S(2)}) collective-permute-start(bf16[2,8,512]{2,1,0:T(8,128)(2,1)S(1)} %get-tuple-element.22), channel_id=1, source_target_pairs={{0,2},{1,3},{2,0},{3,1},{4,6},{5,7},{6,4},{7,5},{8,10},{9,11},{10,... | collective-permute-start | bytes 49160 | tf_op jit(solution)/shard_map/ppermute | solution.py:415
  7.3 2.3 %collective-permute-start.2 = (bf16[2,8,512]{2,1,0:T(8,128)(2,1)S(1)}, bf16[2,8,512]{2,1,0:T(8,128)(2,1)S(1)}, u32[]{:S(2)}, u32[]{:S(2)}) collective-permute-start(bf16[2,8,512]{2,1,0:T(8,128)(2,1)S(1)} %get-tuple-element.23), channel_id=1, source_target_pairs={{0,1},{1,0},{2,3},{3,2},{4,5},{5,4},{6,8},{7,9},{8,6},{9,7},{10,11... | collective-permute-start | bytes 49160 | tf_op jit(solution)/shard_map/ppermute | solution.py:415
  10.4 2.9 %copy-start.2 = (bf16[3,3,3,64,64]{4,3,2,1,0:T(8,128)(2,1)S(1)}, bf16[3,3,3,64,64]{4,3,2,1,0:T(8,128)(2,1)}, u32[]{:S(2)}) copy-start(bf16[3,3,3,64,64]{4,3,2,1,0:T(8,128)(2,1)} %param.6) | copy-start | bytes 663556
  10.5 1.6 %collective-permute-start.3 = (f32[448,128]{1,0:T(8,128)S(1)}, f32[448,128]{1,0:T(8,128)S(1)}, u32[]{:S(2)}, u32[]{:S(2)}) collective-permute-start(f32[448,128]{1,0:T(8,128)S(1)} %get-tuple-element.25), channel_id=1, source_target_pairs={{0,1},{1,0},{2,3},{3,2},{4,5},{5,4},{6,7},{7,6},{8,9},{9,8},{10,11... | collective-permute-start | bytes 688136 | tf_op jit(solution)/shard_map/ppermute | solution.py:461
  12.1 4.3 %collective-permute-start.4 = (bf16[448,128]{1,0:T(8,128)(2,1)S(1)}, bf16[448,128]{1,0:T(8,128)(2,1)S(1)}, u32[]{:S(2)}, u32[]{:S(2)}) collective-permute-start(bf16[448,128]{1,0:T(8,128)(2,1)S(1)} %pad_maximum_fusion.1), channel_id=1, source_target_pairs={{0,3},{1,8},{3,0},{2,11},{5,6},{4,13},{6,5},{7,14},{9,10},{8,1},{1... | collective-permute-start | bytes 344072 | tf_op jit(solution)/shard_map/ppermute | solution.py:486
  13.7 2.7 %collective-permute-start.5 = (bf16[16,128]{1,0:T(8,128)(2,1)S(1)}, bf16[16,128]{1,0:T(8,128)(2,1)S(1)}, u32[]{:S(2)}, u32[]{:S(2)}) collective-permute-start(bf16[16,128]{1,0:T(8,128)(2,1)S(1)} %get-tuple-element.26), channel_id=1, source_target_pairs={{0,1},{1,0},{2,3},{3,2},{4,5},{5,4},{6,8},{7,9},{8,6},{9,7},{10,11... | collective-permute-start | bytes 12296 | tf_op jit(solution)/shard_map/ppermute | solution.py:466
  16.4 6.3 %collective-permute-start.6 = (bf16[448,128]{1,0:T(8,128)(2,1)S(1)}, bf16[448,128]{1,0:T(8,128)(2,1)S(1)}, u32[]{:S(2)}, u32[]{:S(2)}) collective-permute-start(bf16[448,128]{1,0:T(8,128)(2,1)S(1)} %pad_maximum_fusion), channel_id=1, source_target_pairs={{0,9},{1,4},{3,10},{2,7},{5,12},{4,1},{6,15},{7,2},{9,0},{8,13},{1... | collective-permute-start | bytes 344072 | tf_op jit(solution)/shard_map/ppermute | solution.py:486
  22.8 4.8 %collective-permute-start.7 = (bf16[432,128]{1,0:T(8,128)(2,1)S(1)}, bf16[432,128]{1,0:T(8,128)(2,1)S(1)}, u32[]{:S(2)}, u32[]{:S(2)}) collective-permute-start(bf16[432,128]{1,0:T(8,128)(2,1)S(1)} %add_convert_fusion), channel_id=1, source_target_pairs={{0,5},{1,2},{3,6},{2,1},{5,0},{4,7},{6,3},{7,4},{9,12},{8,11},{10,... | collective-permute-start | bytes 331784 | tf_op jit(solution)/shard_map/ppermute | solution.py:486
  27.6 2.0 %collective-permute-start.8 = (f32[432,128]{1,0:T(8,128)S(1)}, f32[432,128]{1,0:T(8,128)S(1)}, u32[]{:S(2)}, u32[]{:S(2)}) collective-permute-start(f32[432,128]{1,0:T(8,128)S(1)} %convert_add_fusion.own_ref), channel_id=1, source_target_pairs={{0,1},{1,0},{2,3},{3,2},{4,5},{5,4},{6,7},{7,6},{8,9},{9,8},{10,11... | collective-permute-start | bytes 663560 | tf_op jit(solution)/shard_map/ppermute | solution.py:492

commit v7 on v6

--- a/solution.py
+++ b/solution.py
@@ -122,9 +122,12 @@
 
 def x_faces_kernel(roles, tiles, f_hbm, c_hbm, link_hbm, *refs):
     roles = Roles(roles, tiles)
-    *x_refs, flag_ref, link_ref, arrived = refs
+    *x_refs, f_ref, c_ref, flag_ref, link_ref, arrived = refs
     edge = f_hbm.shape[1]
-    copies = [pltpu.make_async_copy(link_hbm, link_ref, arrived.at[0])]
+    copies = [
+        pltpu.make_async_copy(source, target, arrived.at[number])
+        for number, (source, target) in enumerate(((link_hbm, link_ref), (f_hbm, f_ref), (c_hbm, c_ref)))
+    ]
     for number, out in enumerate(x_refs):
         plane = jnp.where(roles.side(0, number, 1), edge - 1, 0)
         for source, ref in enumerate((f_hbm, c_hbm)):
@@ -196,35 +199,58 @@
     return jnp.concatenate([rows[each * number + k : each * number + k + 1] for k in range(each)], axis=1)
 
 
-def kernel_grad_kernel(roles, tiles, channels, joined, f_ref, c_ref, *refs):
+def stacked(rows, lanes, wide):
+    steps = range((rows.shape[1] - wide) // lanes + 1)
+    return jnp.concatenate([rows[:, lanes * k : lanes * k + wide] for k in steps], axis=0).astype(BF16)
+
+
+def outer(left, right):
+    return lax.dot_general(left, right, (((0,), (0,)), ((), ())), preferred_element_type=F32)
+
+
+def local_grad_kernel(channels, f_ref, c_ref, out_ref, wide, tall):
+    bricks, edge, _, width = f_ref.shape
+    rows = edge * edge
+    lanes = 2 * channels
+    wide[:, :edge, :] = jnp.zeros_like(wide[:, :edge, :])
+    wide[:, edge + rows :, :] = jnp.zeros_like(wide[:, edge + rows :, :])
+    wide[:, edge : edge + rows, :] = padded(f_ref[...].astype(F32).reshape(bricks, rows, width), channels)
+    own = c_ref[...].astype(F32)
+    none = jnp.zeros((edge, 1, width), F32)
+    tall[:, :, edge : 2 * edge, :] = own
+    tall[0, :, edge - 1 : edge, :] = none
+    tall[1, :, edge - 1 : edge, :] = own[0, :, edge - 1 :, :]
+    tall[0, :, 2 * edge : 2 * edge + 1, :] = own[1, :, 0:1, :]
+    tall[1, :, 2 * edge : 2 * edge + 1, :] = none
+    left, right = [], []
+    for tap in range(3):
+        value = wide[:, edge * tap : edge * tap + rows, :].reshape(bricks * rows, -1)
+        left.append(stacked(value, lanes, 2 * lanes))
+        value = tall[:, :, edge + 1 - tap : 2 * edge + 1 - tap, :].reshape(bricks * rows, width)
+        right.append(stacked(value, lanes, lanes))
+    out_ref[...] = outer(jnp.concatenate(left, axis=1), jnp.concatenate(right, axis=1))
+
+
+def kernel_grad_kernel(roles, tiles, channels, joined, f_ref, c_ref, local_ref, *refs):
     roles = Roles(roles, tiles)
     counts = roles.counts
     x_refs = refs[: counts[0]]
-    y_refs = refs[counts[0] : counts[0] + counts[1]]
     near = counts[0] + counts[1]
+    y_refs = refs[counts[0] : near]
     keep_ref, send_ref = refs[near : near + 2]
     hops_at = near + 2 + (0 if joined else counts[0])
     line_refs = refs[near + 2 : hops_at]
     hop_refs = refs[hops_at : hops_at + counts[2]]
-    wide, tall, packed, lines = refs[hops_at + counts[2] :]
+    tall, row_ref, packed, lines = refs[hops_at + counts[2] :]
     count = keep_ref.shape[0]
     bricks, edge, _, width = f_ref.shape
-    rows = edge * edge
-    wide[:, edge : edge + rows, :] = padded(f_ref[...].astype(F32).reshape(bricks, rows, width), channels)
+    lanes = 2 * channels
     planes = []
     for side in range(2):
-        start = side * (edge + rows)
         plane = jnp.zeros((bricks, edge, width), F32)
         for number, ref in enumerate(x_refs):
             plane = jnp.where(roles.side(0, number, side), ref[0].astype(F32), plane)
         planes.append(plane)
-        plane = padded(plane, channels)
-        for brick in range(bricks):
-            wide[brick, start : start + edge, :] = plane[brick]
-    own = c_ref[...].astype(F32)
-    tall[:, :, edge : 2 * edge, :] = own
-    tall[1, :, edge - 1 : edge, :] = own[0, :, edge - 1 :, :]
-    tall[0, :, 2 * edge : 2 * edge + 1, :] = own[1, :, 0:1, :]
     halo = {}
     for side in range(2):
         for source in range(2):
@@ -232,27 +258,37 @@
             for number, ref in enumerate(y_refs):
                 row = jnp.where(roles.side(1, number, side), ref[source].astype(F32), row)
             halo[source, side] = row
-        at = 2 * edge if side else edge - 1
-        tall[side, :, at : at + 1, :] = halo[1, side][:, None, :]
-    lanes = 2 * channels
-    pairs = width // lanes
-    right = []
-    for col in range(3):
-        value = tall[:, :, edge + 1 - col : 2 * edge + 1 - col, :].reshape(bricks * rows, width).astype(BF16)
-        right.append(jnp.concatenate([value[:, lanes * k : lanes * (k + 1)] for k in range(pairs)], axis=0))
-    right = jnp.concatenate(right, axis=1)
-    low = lax.broadcasted_iota(jnp.int32, (3 * channels // 2, lanes), 1) < channels
+    across = []
+    for side, plane in enumerate(planes):
+        at = (edge - 1) * side
+        own = [c_ref[brick, at].astype(F32) for brick in range(bricks)]
+        below = (halo[1, 0][at : at + 1], own[0][edge - 1 :])
+        above = (own[1][0:1], halo[1, 1][at : at + 1])
+        for brick in range(bricks):
+            tall[brick, edge : 2 * edge, :] = own[brick]
+            tall[brick, edge - 1 : edge, :] = below[brick]
+            tall[brick, 2 * edge : 2 * edge + 1, :] = above[brick]
+        left = stacked(padded(plane, channels).reshape(bricks * edge, -1), lanes, 2 * lanes)
+        right = []
+        for tap in range(3):
+            value = tall[:, edge + 1 - tap : 2 * edge + 1 - tap, :].reshape(bricks * edge, width)
+            right.append(stacked(value, lanes, lanes))
+        across.append(outer(left, jnp.concatenate(right, axis=1)))
+    along = []
+    row_ref[...] = jnp.zeros_like(row_ref)
+    for side in range(2):
+        row_ref[edge : 2 * edge, :] = padded(f_ref[side].astype(F32)[:, (edge - 1) * side, :], channels)
+        left = [stacked(row_ref[edge - 1 + tap : 2 * edge - 1 + tap, :], lanes, 2 * lanes) for tap in range(3)]
+        along.append(outer(jnp.concatenate(left, axis=1), stacked(halo[1, side], lanes, lanes)))
     half = 3 * channels // 2
-    left = []
+    low = lax.broadcasted_iota(jnp.int32, (half, lanes), 1) < channels
     for row in range(3):
-        value = wide[:, edge * row : edge * row + rows, :].reshape(bricks * rows, -1).astype(BF16)
-        left.append(jnp.concatenate([value[:, lanes * k : lanes * (k + 2)] for k in range(pairs)], axis=0))
-    left = jnp.concatenate(left, axis=1)
-    every = lax.dot_general(left, right, (((0,), (0,)), ((), ())), preferred_element_type=F32)
-    for row in range(3):
-        grad = every[2 * lanes * row : 2 * lanes * (row + 1)]
         for col in range(3):
-            block = grad[:, lanes * col : lanes * (col + 1)]
+            block = local_ref[2 * lanes * row : 2 * lanes * (row + 1), lanes * col : lanes * (col + 1)]
+            if row != 1:
+                block = block + across[row // 2][:, lanes * col : lanes * (col + 1)]
+            if col != 1:
+                block = block + along[1 - col // 2][2 * lanes * row : 2 * lanes * (row + 1)]
             moved = pltpu.roll(block, channels, 1)
             first = block[:half] + moved[channels : channels + half]
             second = moved[half : 2 * half] + block[channels + half :]
@@ -397,11 +433,12 @@
     links = neighbours.reshape(bricks, 6)
 
     near = counts[0] + counts[1]
-    *faces, flags = call(
+    *faces, f, c, flags = call(
         functools.partial(x_faces_kernel, roles, tiles),
         [HBM, HBM, HBM],
-        [pltpu.VMEM((2, bricks, edge, width), BF16)] * counts[0] + [pltpu.VMEM((16, width), F32)],
-        [pltpu.SMEM(links.shape, jnp.int32), pltpu.SemaphoreType.DMA((4 * counts[0] + 1,))],
+        [pltpu.VMEM((2, bricks, edge, width), BF16)] * counts[0]
+        + [pltpu.VMEM(f.shape, BF16), pltpu.VMEM(c.shape, BF16), pltpu.VMEM((16, width), F32)],
+        [pltpu.SMEM(links.shape, jnp.int32), pltpu.SemaphoreType.DMA((4 * counts[0] + 3,))],
         name="x_faces",
         vmem=None,
     )(f, c, links)
@@ -423,20 +460,31 @@
         orders = [[first] + shared + [last], shared + [last, first]]
     count = 27 * channels * channels // lanes // 2
     line_rows = 4 * width // lanes
+    local = call(
+        functools.partial(local_grad_kernel, channels),
+        [VMEM, VMEM],
+        pltpu.VMEM((6 * lanes, 3 * lanes), F32),
+        [
+            pltpu.VMEM((bricks, rows + 2 * edge, width + lanes), F32),
+            pltpu.VMEM((bricks, edge, 3 * edge, width), F32),
+        ],
+        flops=2 * 768 * 384 * 512,
+        name="local_grad",
+    )(f, c)
     keep, send, *lines = call(
         functools.partial(kernel_grad_kernel, roles, tiles, channels, joined),
-        [VMEM, VMEM] + [VMEM] * near,
+        [VMEM] * (3 + near),
         [shape((count, lanes), F32), shape((count + line_rows * joined, lanes), F32)]
         + [shape((line_rows, lanes), BF16)] * (counts[2] if joined else counts[0] + counts[2]),
         [
-            pltpu.VMEM((bricks, rows + 2 * edge, width + lanes), F32),
-            pltpu.VMEM((bricks, edge, 3 * edge, width), F32),
+            pltpu.VMEM((bricks, 3 * edge, width), F32),
+            pltpu.VMEM((3 * edge, width + lanes), F32),
             pltpu.VMEM((2 * count, lanes), F32),
             pltpu.VMEM((line_rows, lanes), F32),
         ],
-        flops=2 * 768 * 384 * 512,
+        flops=2 * 768 * 384 * 64,
         name="kernel_grad",
-    )(f, c, *got)
+    )(f, c, local, *got)
 
     forward, backward = call(
         weights_kernel,
@@ -475,7 +523,7 @@
         carries = joined and number < ready
         if carries:
             mine = jnp.concatenate([mine, summed[count:].astype(wire)], axis=0)
-        if number == 1:
+        if number == ready:
             mine, hops, forward, backward = lax.optimization_barrier((mine, hops, forward, backward))
         else:
             mine = lax.optimization_barrier(mine)

time: 30.9 us -> 30.4 us (0.984)
  starting transfers between devices: 15.3 us -> 13.2 us
  waiting for transfers between devices: 8.13 us -> 9.24 us
  Pallas kernels: 6.34 us -> 6.89 us
    ppermute x3, waiting for transfers between devices: 4.4 us -> 6.26 us  [body(): theirs = lax.ppermute(mine, ('space', 'dp'), step)]
    ppermute x4, starting transfers between devices: 7.33 us -> 5.73 us  [body(): lax.ppermute(x, ('space', 'dp'), one)]
    ppermute x4, waiting for transfers between devices: 2.25 us -> 1.51 us  [body(): lax.ppermute(x, ('space', 'dp'), one)]
    pallas_call x0 -> x1, Pallas kernels: none -> 0.73 us  [body(): call(functools.partial(local_grad_kernel, channels), [VMEM, VMEM], pltpu....]
    pallas_call x1, Pallas kernels: 0.92 us -> 0.61 us  [body(): call(functools.partial(kernel_grad_kernel, roles, tiles, channels, joined...]
  transfers between devices with their start and end apart: 9 -> 9, of which waited for: 5 -> 5; matrix products, arithmetic and copies ran while one was open for 0% -> 0% of each run, Pallas kernels for 11% -> 14%
where the time goes in v7:
time: 30.4 us; the launch traced here: 30.2 us
  starting transfers between devices  13.2 us (43%)
  waiting for transfers between devices  9.24 us (30%)
  Pallas kernels  6.89 us (23%)
  between operations  0.73 us (2%)
    ppermute x3, starting transfers between devices, body(): theirs = lax.ppermute(mine, ('space', 'dp'), step)  7.24 us
    ppermute x3, waiting for transfers between devices, body(): theirs = lax.ppermute(mine, ('space', 'dp'), step)  6.26 us
    ppermute x4, starting transfers between devices, body(): lax.ppermute(x, ('space', 'dp'), one)  5.73 us
    pallas_call x2, Pallas kernels, conv(): call(functools.partial(conv_kernel, roles, tiles, channels, source, ready...  3.04 us
    ppermute x4, waiting for transfers between devices, body(): lax.ppermute(x, ('space', 'dp'), one)  1.51 us
    ppermute x1, waiting for transfers between devices, body(): summed = lax.ppermute(send, 'dp', swap)  1.48 us
    pallas_call x1, Pallas kernels, body(): call(functools.partial(unpack_kernel, 1.0 / math.sqrt(cells)), [VMEM, VME...  1.07 us
    pallas_call x1, Pallas kernels, body(): call(functools.partial(x_faces_kernel, roles, tiles), [HBM, HBM, HBM], [p...  1.04 us
  transfers between devices with their start and end apart: 9, of which 5 were waited for; matrix products, arithmetic and copies ran while one was open for 0% of the time, Pallas kernels for 14%

profile of v7, /device:TPU:0, one launch (start us, length us, event | category | flops | bytes accessed | tf_op | source)
XLA Modules:
  0.0 30.2 jit_solution(7868628958686875267)
XLA Ops:
  0.6 1.0 %x_faces.1 = (bf16[2,2,8,512]{3,2,1,0:T(8,128)(2,1)S(1)}, bf16[2,8,8,512]{3,2,1,0:T(8,128)(2,1)S(1)}, bf16[2,8,8,512]{3,2,1,0:T(8,128)(2,1)S(1)}, f32[16,512]{1,0:T(8,128)S(1)}) custom-call(bf16[2,8,8,512]{3,2,1,0:T(8,128)(2,1)} %bitcast.11, bf16[2,8,8,512]{3,2,1,0:T(8,128)(2,1)} %bitcast.12, s32[2,6]{1,0:T(2,128)} %bitcast.13), custom_call_target="tpu_custom_call" | custom-call | bytes 1048576 | tf_op jit(solution)/shard_map/x_faces/pallas_call | solution.py:436
  1.7 4.1 %collective-permute-start = (bf16[2,2,8,512]{3,2,1,0:T(8,128)(2,1)S(1)}, bf16[2,2,8,512]{3,2,1,0:T(8,128)(2,1)S(1)}, u32[]{:S(2)}, u32[]{:S(2)}) collective-permute-start(bf16[2,2,8,512]{3,2,1,0:T(8,128)(2,1)S(1)} %get-tuple-element.24), channel_id=1, source_target_pairs={{0,8},{1,9},{2,10},{3,11},{4,12},{5,13},{6,14},{7,15},{8,0},{9,1},... | collective-permute-start | bytes 98312 | tf_op jit(solution)/shard_map/ppermute | solution.py:445
  5.8 0.1 y_faces.1
  5.8 1.6 %collective-permute-start.1 = (bf16[2,8,512]{2,1,0:T(8,128)(2,1)S(1)}, bf16[2,8,512]{2,1,0:T(8,128)(2,1)S(1)}, u32[]{:S(2)}, u32[]{:S(2)}) collective-permute-start(bf16[2,8,512]{2,1,0:T(8,128)(2,1)S(1)} %get-tuple-element.26), channel_id=1, source_target_pairs={{0,2},{1,3},{2,0},{3,1},{4,6},{5,7},{6,4},{7,5},{8,10},{9,11},{10,... | collective-permute-start | bytes 49160 | tf_op jit(solution)/shard_map/ppermute | solution.py:452
  7.4 0.0 collective-permute-start.2
  7.4 0.7 %local_grad.1.local_ref = f32[768,384]{1,0:T(8,128)S(1)} custom-call(bf16[2,8,8,512]{3,2,1,0:T(8,128)(2,1)S(1)} %get-tuple-element.22.f_ref.v_ref, bf16[2,8,8,512]{3,2,1,0:T(8,128)(2,1)S(1)} %get-tuple-element.23.c_ref.v_ref), custom_call_target="tpu_custom_call" | custom-call | flops 301989888 | bytes 1048576 | tf_op jit(solution)/shard_map/local_grad/pallas_call | solution.py:463
  8.1 0.0 copy-start
  8.1 1.5 %collective-permute-done.1.refs_1_ = bf16[2,8,512]{2,1,0:T(8,128)(2,1)S(1)} collective-permute-done((bf16[2,8,512]{2,1,0:T(8,128)(2,1)S(1)}, bf16[2,8,512]{2,1,0:T(8,128)(2,1)S(1)}, u32[]{:S(2)}, u32[]{:S(2)}) %collective-permute-start.1) | collective-permute-done | bytes 16416 | tf_op jit(solution)/shard_map/ppermute | solution.py:452
  9.6 0.0 collective-permute-done.2.refs_2_
  9.6 0.0 collective-permute-done.refs_0_
  9.6 0.6 %kernel_grad.1 = (f32[432,128]{1,0:T(8,128)S(1)}, f32[448,128]{1,0:T(8,128)S(1)}, bf16[16,128]{1,0:T(8,128)(2,1)S(1)}) custom-call(bf16[2,8,8,512]{3,2,1,0:T(8,128)(2,1)S(1)} %get-tuple-element.22.f_ref.v_ref, bf16[2,8,8,512]{3,2,1,0:T(8,128)(2,1)S(1)} %get-tuple-element.23.c_ref.v_ref, f32[768,384]{1,0:T(8,128)S(1)} %local_grad.1.local_ref, ...), custom_call_target="tpu_custom_call" | custom-call | flops 37748736 | bytes 1048576 | tf_op jit(solution)/shard_map/kernel_grad/pallas_call | solution.py:474
  10.3 0.1 collective-permute-start.3
  10.3 1.5 %collective-permute-done.3 = f32[448,128]{1,0:T(8,128)S(1)} collective-permute-done((f32[448,128]{1,0:T(8,128)S(1)}, f32[448,128]{1,0:T(8,128)S(1)}, u32[]{:S(2)}, u32[]{:S(2)}) %collective-permute-start.3) | collective-permute-done | bytes 229408 | tf_op jit(solution)/shard_map/ppermute | solution.py:509
  11.9 1.3 %collective-permute-start.4 = (bf16[448,128]{1,0:T(8,128)(2,1)S(1)}, bf16[448,128]{1,0:T(8,128)(2,1)S(1)}, u32[]{:S(2)}, u32[]{:S(2)}) collective-permute-start(bf16[448,128]{1,0:T(8,128)(2,1)S(1)} %pad_maximum_fusion.1), channel_id=1, source_target_pairs={{0,3},{1,8},{3,0},{2,11},{5,6},{4,13},{6,5},{7,14},{9,10},{8,1},{1... | collective-permute-start | bytes 344072 | tf_op jit(solution)/shard_map/ppermute | solution.py:534
  13.2 3.0 %collective-permute-done.4.refs_3_ = bf16[448,128]{1,0:T(8,128)(2,1)S(1)} collective-permute-done((bf16[448,128]{1,0:T(8,128)(2,1)S(1)}, bf16[448,128]{1,0:T(8,128)(2,1)S(1)}, u32[]{:S(2)}, u32[]{:S(2)}) %collective-permute-start.4) | collective-permute-done | bytes 114720 | tf_op jit(solution)/shard_map/ppermute | solution.py:534
  16.2 2.8 %collective-permute-start.5 = (bf16[448,128]{1,0:T(8,128)(2,1)S(1)}, bf16[448,128]{1,0:T(8,128)(2,1)S(1)}, u32[]{:S(2)}, u32[]{:S(2)}) collective-permute-start(bf16[448,128]{1,0:T(8,128)(2,1)S(1)} %pad_maximum_fusion), channel_id=1, source_target_pairs={{0,9},{1,4},{3,10},{2,7},{5,12},{4,1},{6,15},{7,2},{9,0},{8,13},{1... | collective-permute-start | bytes 344072 | tf_op jit(solution)/shard_map/ppermute | solution.py:534
  19.0 0.0 copy-done
  19.0 0.3 %weights.1 = (bf16[9,256,128]{2,1,0:T(8,128)(2,1)S(1)}, bf16[9,128,256]{2,1,0:T(8,128)(2,1)S(1)}) custom-call(bf16[27,64,64]{2,1,0:T(8,128)(2,1)S(1)} %bitcast.7), custom_call_target="tpu_custom_call" | custom-call | bytes 1048576 | tf_op jit(solution)/shard_map/weights/pallas_call | solution.py:489
  19.4 0.1 collective-permute-start.6
  19.5 2.4 %collective-permute-done.5.refs_4_ = bf16[448,128]{1,0:T(8,128)(2,1)S(1)} collective-permute-done((bf16[448,128]{1,0:T(8,128)(2,1)S(1)}, bf16[448,128]{1,0:T(8,128)(2,1)S(1)}, u32[]{:S(2)}, u32[]{:S(2)}) %collective-permute-start.5) | collective-permute-done | bytes 114720 | tf_op jit(solution)/shard_map/ppermute | solution.py:534
  21.9 0.0 collective-permute-done.6.refs_5_
  21.9 3.1 %collective-permute-start.7 = (bf16[432,128]{1,0:T(8,128)(2,1)S(1)}, bf16[432,128]{1,0:T(8,128)(2,1)S(1)}, u32[]{:S(2)}, u32[]{:S(2)}) collective-permute-start(bf16[432,128]{1,0:T(8,128)(2,1)S(1)} %add_convert_fusion), channel_id=1, source_target_pairs={{0,5},{1,2},{3,6},{2,1},{5,0},{4,7},{6,3},{7,4},{9,12},{8,11},{10,... | collective-permute-start | bytes 331784 | tf_op jit(solution)/shard_map/ppermute | solution.py:534
  25.0 1.5 %response.1 = bf16[128,512]{1,0:T(8,128)(2,1)} custom-call(bf16[2,8,8,512]{3,2,1,0:T(8,128)(2,1)S(1)} %get-tuple-element.22.f_ref.v_ref, bf16[2,2,8,512]{3,2,1,0:T(8,128)(2,1)S(1)} %collective-permute-done.refs_0_, bf16[2,8,512]{2,1,0:T(8,128)(2,1)S(1)} %collective-permute-done.1.refs_1_, bf16[2,8,512]{2,1,0:T(8,128)(2,1)S(1)} %collective-permute-done.2.refs_2_, ...), custom_call_target="tpu_custom_call" | custom-call | flops 301989888 | bytes 1048576 | tf_op jit(solution)/shard_map/response/pallas_call | solution.py:498
  26.5 0.9 %collective-permute-done.7 = bf16[432,128]{1,0:T(8,128)(2,1)S(1)} collective-permute-done((bf16[432,128]{1,0:T(8,128)(2,1)S(1)}, bf16[432,128]{1,0:T(8,128)(2,1)S(1)}, u32[]{:S(2)}, u32[]{:S(2)}) %collective-permute-start.7) | collective-permute-done | bytes 110624 | tf_op jit(solution)/shard_map/ppermute | solution.py:534
  27.4 0.2 collective-permute-start.8
  27.6 1.5 %feature_grad.1 = bf16[128,512]{1,0:T(8,128)(2,1)} custom-call(bf16[2,8,8,512]{3,2,1,0:T(8,128)(2,1)S(1)} %get-tuple-element.23.c_ref.v_ref, bf16[2,2,8,512]{3,2,1,0:T(8,128)(2,1)S(1)} %collective-permute-done.refs_0_, bf16[2,8,512]{2,1,0:T(8,128)(2,1)S(1)} %collective-permute-done.1.refs_1_, bf16[2,8,512]{2,1,0:T(8,128)(2,1)S(1)} %collective-permute-done.2.refs_2_, ...), custom_call_target="tpu_custom_call" | custom-call | flops 301989888 | bytes 1048576 | tf_op jit(solution)/shard_map/feature_grad/pallas_call | solution.py:498
  29.2 0.0 collective-permute-done.8.other_ref
  29.2 1.1 %unpack.1 = f32[9,192,64]{2,1,0:T(8,128)} custom-call(f32[432,128]{1,0:T(8,128)S(1)} %convert_add_fusion.own_ref, f32[432,128]{1,0:T(8,128)S(1)} %collective-permute-done.8.other_ref), custom_call_target="tpu_custom_call" | custom-call | bytes 1048576 | tf_op jit(solution)/shard_map/unpack/pallas_call | solution.py:544
  (7 shorter events, 0.1 us)
Async XLA Ops:
  1.7 8.0 %collective-permute-start = (bf16[2,2,8,512]{3,2,1,0:T(8,128)(2,1)S(1)}, bf16[2,2,8,512]{3,2,1,0:T(8,128)(2,1)S(1)}, u32[]{:S(2)}, u32[]{:S(2)}) collective-permute-start(bf16[2,2,8,512]{3,2,1,0:T(8,128)(2,1)S(1)} %get-tuple-element.24), channel_id=1, source_target_pairs={{0,8},{1,9},{2,10},{3,11},{4,12},{5,13},{6,14},{7,15},{8,0},{9,1},... | collective-permute-start | bytes 98312 | tf_op jit(solution)/shard_map/ppermute | solution.py:445
  5.8 3.8 %collective-permute-start.1 = (bf16[2,8,512]{2,1,0:T(8,128)(2,1)S(1)}, bf16[2,8,512]{2,1,0:T(8,128)(2,1)S(1)}, u32[]{:S(2)}, u32[]{:S(2)}) collective-permute-start(bf16[2,8,512]{2,1,0:T(8,128)(2,1)S(1)} %get-tuple-element.26), channel_id=1, source_target_pairs={{0,2},{1,3},{2,0},{3,1},{4,6},{5,7},{6,4},{7,5},{8,10},{9,11},{10,... | collective-permute-start | bytes 49160 | tf_op jit(solution)/shard_map/ppermute | solution.py:452
  7.4 2.3 %collective-permute-start.2 = (bf16[2,8,512]{2,1,0:T(8,128)(2,1)S(1)}, bf16[2,8,512]{2,1,0:T(8,128)(2,1)S(1)}, u32[]{:S(2)}, u32[]{:S(2)}) collective-permute-start(bf16[2,8,512]{2,1,0:T(8,128)(2,1)S(1)} %get-tuple-element.27), channel_id=1, source_target_pairs={{0,1},{1,0},{2,3},{3,2},{4,5},{5,4},{6,8},{7,9},{8,6},{9,7},{10,11... | collective-permute-start | bytes 49160 | tf_op jit(solution)/shard_map/ppermute | solution.py:452
  8.1 10.9 %copy-start = (bf16[3,3,3,64,64]{4,3,2,1,0:T(8,128)(2,1)S(1)}, bf16[3,3,3,64,64]{4,3,2,1,0:T(8,128)(2,1)}, u32[]{:S(2)}) copy-start(bf16[3,3,3,64,64]{4,3,2,1,0:T(8,128)(2,1)} %param.6) | copy-start | bytes 663556
  10.3 1.6 %collective-permute-start.3 = (f32[448,128]{1,0:T(8,128)S(1)}, f32[448,128]{1,0:T(8,128)S(1)}, u32[]{:S(2)}, u32[]{:S(2)}) collective-permute-start(f32[448,128]{1,0:T(8,128)S(1)} %get-tuple-element.29), channel_id=1, source_target_pairs={{0,1},{1,0},{2,3},{3,2},{4,5},{5,4},{6,7},{7,6},{8,9},{9,8},{10,11... | collective-permute-start | bytes 688136 | tf_op jit(solution)/shard_map/ppermute | solution.py:509
  11.9 4.3 %collective-permute-start.4 = (bf16[448,128]{1,0:T(8,128)(2,1)S(1)}, bf16[448,128]{1,0:T(8,128)(2,1)S(1)}, u32[]{:S(2)}, u32[]{:S(2)}) collective-permute-start(bf16[448,128]{1,0:T(8,128)(2,1)S(1)} %pad_maximum_fusion.1), channel_id=1, source_target_pairs={{0,3},{1,8},{3,0},{2,11},{5,6},{4,13},{6,5},{7,14},{9,10},{8,1},{1... | collective-permute-start | bytes 344072 | tf_op jit(solution)/shard_map/ppermute | solution.py:534
  16.2 5.6 %collective-permute-start.5 = (bf16[448,128]{1,0:T(8,128)(2,1)S(1)}, bf16[448,128]{1,0:T(8,128)(2,1)S(1)}, u32[]{:S(2)}, u32[]{:S(2)}) collective-permute-start(bf16[448,128]{1,0:T(8,128)(2,1)S(1)} %pad_maximum_fusion), channel_id=1, source_target_pairs={{0,9},{1,4},{3,10},{2,7},{5,12},{4,1},{6,15},{7,2},{9,0},{8,13},{1... | collective-permute-start | bytes 344072 | tf_op jit(solution)/shard_map/ppermute | solution.py:534
  19.4 2.5 %collective-permute-start.6 = (bf16[16,128]{1,0:T(8,128)(2,1)S(1)}, bf16[16,128]{1,0:T(8,128)(2,1)S(1)}, u32[]{:S(2)}, u32[]{:S(2)}) collective-permute-start(bf16[16,128]{1,0:T(8,128)(2,1)S(1)} %get-tuple-element.30), channel_id=1, source_target_pairs={{0,1},{1,0},{2,3},{3,2},{4,5},{5,4},{6,8},{7,9},{8,6},{9,7},{10,11... | collective-permute-start | bytes 12296 | tf_op jit(solution)/shard_map/ppermute | solution.py:514
  21.9 5.6 %collective-permute-start.7 = (bf16[432,128]{1,0:T(8,128)(2,1)S(1)}, bf16[432,128]{1,0:T(8,128)(2,1)S(1)}, u32[]{:S(2)}, u32[]{:S(2)}) collective-permute-start(bf16[432,128]{1,0:T(8,128)(2,1)S(1)} %add_convert_fusion), channel_id=1, source_target_pairs={{0,5},{1,2},{3,6},{2,1},{5,0},{4,7},{6,3},{7,4},{9,12},{8,11},{10,... | collective-permute-start | bytes 331784 | tf_op jit(solution)/shard_map/ppermute | solution.py:534
  27.4 1.7 %collective-permute-start.8 = (f32[432,128]{1,0:T(8,128)S(1)}, f32[432,128]{1,0:T(8,128)S(1)}, u32[]{:S(2)}, u32[]{:S(2)}) collective-permute-start(f32[432,128]{1,0:T(8,128)S(1)} %convert_add_fusion.own_ref), channel_id=1, source_target_pairs={{0,1},{1,0},{2,3},{3,2},{4,5},{5,4},{6,7},{7,6},{8,9},{9,8},{10,11... | collective-permute-start | bytes 663560 | tf_op jit(solution)/shard_map/ppermute | solution.py:540

commit v8 on v7

--- a/solution.py
+++ b/solution.py
@@ -120,20 +120,15 @@
     return jnp.where(keep, x, jnp.zeros_like(x))
 
 
-def x_faces_kernel(roles, tiles, f_hbm, c_hbm, link_hbm, *refs):
+def faces_kernel(roles, tiles, f_hbm, c_hbm, link_hbm, *refs):
     roles = Roles(roles, tiles)
-    *x_refs, f_ref, c_ref, flag_ref, link_ref, arrived = refs
+    *out_refs, f_ref, c_ref, link_ref, arrived = refs
+    x_refs, y_refs = out_refs[: roles.counts[0]], out_refs[roles.counts[0] :]
     edge = f_hbm.shape[1]
     copies = [
         pltpu.make_async_copy(source, target, arrived.at[number])
         for number, (source, target) in enumerate(((link_hbm, link_ref), (f_hbm, f_ref), (c_hbm, c_ref)))
     ]
-    for number, out in enumerate(x_refs):
-        plane = jnp.where(roles.side(0, number, 1), edge - 1, 0)
-        for source, ref in enumerate((f_hbm, c_hbm)):
-            for brick in range(2):
-                at = arrived.at[len(copies)]
-                copies.append(pltpu.make_async_copy(ref.at[brick, plane], out.at[source, brick], at))
     for copy in copies:
         copy.start()
     for copy in copies:
@@ -141,23 +136,16 @@
     linked = [[link_ref[brick, way] >= 0 for way in range(4)] for brick in range(2)]
     for number, out in enumerate(x_refs):
         up = roles.side(0, number, 1)
+        plane = jnp.where(up, edge - 1, 0)
         for brick in range(2):
-
-            @pl.when(jnp.logical_not(jnp.where(up, linked[brick][1], linked[brick][0])))
-            def _():
-                out[:, brick] = jnp.zeros_like(out[:, brick])
-
-    for row, flag in enumerate((linked[0][2], linked[1][3])):
-        flag_ref[8 * row : 8 * row + 8, :] = jnp.full((8, flag_ref.shape[1]), jnp.where(flag, 1.0, 0.0), F32)
-
-
-def y_faces_kernel(roles, tiles, f_ref, c_ref, flag_ref, *y_refs):
-    roles = Roles(roles, tiles)
-    edge = f_ref.shape[1]
+            keep = jnp.where(up, linked[brick][1], linked[brick][0])
+            for source, ref in enumerate((f_ref, c_ref)):
+                out[source, brick] = masked(keep, ref[brick, plane])
+
     rows = []
     for ref in (f_ref, c_ref):
-        low = ref[0].astype(F32)[:, 0, :] * flag_ref[:8]
-        high = ref[1].astype(F32)[:, edge - 1, :] * flag_ref[8:]
+        low = masked(linked[0][2], ref[0].astype(F32)[:, 0, :])
+        high = masked(linked[1][3], ref[1].astype(F32)[:, edge - 1, :])
         rows.append((low, high))
     for number, out in enumerate(y_refs):
         up = roles.side(1, number, 1)
@@ -340,7 +328,7 @@
     each = width // line_refs[0].shape[1]
     arrived = [ref[ref.shape[0] - 4 * each :, :].astype(F32) for ref in line_refs]
     if ways == 2:
-        arrived = [jnp.where(my_half() == 1, *arrived)]
+        arrived = [jnp.where(my_half() == 0, *arrived)]
     hops = [load_line(ref[...].astype(F32), 0, each) for ref in hop_refs]
     for side in range(2):
         row = jnp.zeros((edge, width), F32)
@@ -433,23 +421,17 @@
     links = neighbours.reshape(bricks, 6)
 
     near = counts[0] + counts[1]
-    *faces, f, c, flags = call(
-        functools.partial(x_faces_kernel, roles, tiles),
+    *faces, f, c = call(
+        functools.partial(faces_kernel, roles, tiles),
         [HBM, HBM, HBM],
         [pltpu.VMEM((2, bricks, edge, width), BF16)] * counts[0]
-        + [pltpu.VMEM(f.shape, BF16), pltpu.VMEM(c.shape, BF16), pltpu.VMEM((16, width), F32)],
-        [pltpu.SMEM(links.shape, jnp.int32), pltpu.SemaphoreType.DMA((4 * counts[0] + 3,))],
-        name="x_faces",
+        + [pltpu.VMEM((2, edge, width), BF16)] * counts[1]
+        + [pltpu.VMEM(f.shape, BF16), pltpu.VMEM(c.shape, BF16)],
+        [pltpu.SMEM(links.shape, jnp.int32), pltpu.SemaphoreType.DMA((3,))],
+        name="faces",
         vmem=None,
     )(f, c, links)
-    got = [lax.ppermute(x, ("space", "dp"), one) for x, one in zip(faces, pairs[0])]
-    faces = call(
-        functools.partial(y_faces_kernel, roles, tiles),
-        [VMEM] * 3,
-        [pltpu.VMEM((2, edge, width), BF16)] * counts[1],
-        name="y_faces",
-    )(f, c, flags)
-    got += [lax.ppermute(x, ("space", "dp"), one) for x, one in zip(faces, pairs[1])]
+    got = [lax.ppermute(x, ("space", "dp"), one) for x, one in zip(faces, pairs[0] + pairs[1])]
     bits = [1 << number for number in range(tiles.bit_length() - 1)]
     orders = [bits, bits]
     wire = BF16 if len(bits) <= 3 else F32
@@ -457,7 +439,7 @@
     joined = bool(shared) and len(bits) == 3
     if joined:
         first, last = (bit for bit in bits if bit not in shared)
-        orders = [[first] + shared + [last], shared + [last, first]]
+        orders = [shared + [last, first], [first] + shared + [last]]
     count = 27 * channels * channels // lanes // 2
     line_rows = 4 * width // lanes
     local = call(

time: 30.4 us -> 30.1 us (level)
  starting transfers between devices: 13.2 us -> 12 us
  waiting for transfers between devices: 9.24 us -> 10.1 us
    ppermute x3, starting transfers between devices: 7.24 us -> 5.22 us  [body(): theirs = lax.ppermute(mine, ('space', 'dp'), step)]
    ppermute x3, waiting for transfers between devices: 6.26 us -> 7.16 us  [body(): theirs = lax.ppermute(mine, ('space', 'dp'), step)]
    ppermute x4, starting transfers between devices: 5.73 us -> 6.28 us  [body(): lax.ppermute(x, ('space', 'dp'), one)]
    pallas_call x2 -> x1, Pallas kernels: 1.1 us -> 1.15 us  [body(): call(functools.partial(faces_kernel, roles, tiles), [HBM, HBM, HBM], [plt...]
where the time goes in v8:
time: 30.1 us; the launch traced here: 30 us
  starting transfers between devices  12 us (40%)
  waiting for transfers between devices  10.1 us (34%)
  Pallas kernels  6.94 us (23%)
  between operations  0.72 us (2%)
    ppermute x3, waiting for transfers between devices, body(): theirs = lax.ppermute(mine, ('space', 'dp'), step)  7.16 us
    ppermute x4, starting transfers between devices, body(): lax.ppermute(x, ('space', 'dp'), one)  6.28 us
    ppermute x3, starting transfers between devices, body(): theirs = lax.ppermute(mine, ('space', 'dp'), step)  5.22 us
    pallas_call x2, Pallas kernels, conv(): call(functools.partial(conv_kernel, roles, tiles, channels, source, ready...  3.04 us
    ppermute x4, waiting for transfers between devices, body(): lax.ppermute(x, ('space', 'dp'), one)  1.51 us
    ppermute x1, waiting for transfers between devices, body(): summed = lax.ppermute(send, 'dp', swap)  1.48 us
    pallas_call x1, Pallas kernels, body(): call(functools.partial(faces_kernel, roles, tiles), [HBM, HBM, HBM], [plt...  1.15 us
    pallas_call x1, Pallas kernels, body(): call(functools.partial(unpack_kernel, 1.0 / math.sqrt(cells)), [VMEM, VME...  1.07 us
  transfers between devices with their start and end apart: 9, of which 5 were waited for; matrix products, arithmetic and copies ran while one was open for 0% of the time, Pallas kernels for 14%

profile of v8, /device:TPU:0, one launch (start us, length us, event | category | flops | bytes accessed | tf_op | source)
XLA Modules:
  0.0 30.0 jit_solution(5081286735723498374)
XLA Ops:
  0.6 1.1 %faces.1 = (bf16[2,2,8,512]{3,2,1,0:T(8,128)(2,1)S(1)}, bf16[2,8,512]{2,1,0:T(8,128)(2,1)S(1)}, bf16[2,8,512]{2,1,0:T(8,128)(2,1)S(1)}, bf16[2,8,8,512]{3,2,1,0:T(8,128)(2,1)S(1)}, bf16[2,8,8,512]{3,2,1,0:T(8,128)(2,1)S(1)}) custom-call(bf16[2,8,8,512]{3,2,1,0:T(8,128)(2,1)} %bitcast.11, bf16[2,8,8,512]{3,2,1,0:T(8,128)(2,1)} %bitcast.12, s32[2,6]{1,0:T(2,128)} %bitcast.13), custom_call_target="tpu_custom_call" | custom-call | bytes 1048576 | tf_op jit(solution)/shard_map/faces/pallas_call | solution.py:424
  1.8 4.1 %collective-permute-start = (bf16[2,2,8,512]{3,2,1,0:T(8,128)(2,1)S(1)}, bf16[2,2,8,512]{3,2,1,0:T(8,128)(2,1)S(1)}, u32[]{:S(2)}, u32[]{:S(2)}) collective-permute-start(bf16[2,2,8,512]{3,2,1,0:T(8,128)(2,1)S(1)} %get-tuple-element.23), channel_id=1, source_target_pairs={{0,8},{1,9},{2,10},{3,11},{4,12},{5,13},{6,14},{7,15},{8,0},{9,1},... | collective-permute-start | bytes 98312 | tf_op jit(solution)/shard_map/ppermute | solution.py:434
  5.9 1.5 %collective-permute-start.1 = (bf16[2,8,512]{2,1,0:T(8,128)(2,1)S(1)}, bf16[2,8,512]{2,1,0:T(8,128)(2,1)S(1)}, u32[]{:S(2)}, u32[]{:S(2)}) collective-permute-start(bf16[2,8,512]{2,1,0:T(8,128)(2,1)S(1)} %get-tuple-element.24), channel_id=1, source_target_pairs={{0,2},{1,3},{2,0},{3,1},{4,6},{5,7},{6,4},{7,5},{8,10},{9,11},{10,... | collective-permute-start | bytes 49160 | tf_op jit(solution)/shard_map/ppermute | solution.py:434
  7.4 0.0 collective-permute-start.2
  7.4 0.7 %local_grad.1.local_ref = f32[768,384]{1,0:T(8,128)S(1)} custom-call(bf16[2,8,8,512]{3,2,1,0:T(8,128)(2,1)S(1)} %get-tuple-element.21.f_ref.v_ref, bf16[2,8,8,512]{3,2,1,0:T(8,128)(2,1)S(1)} %get-tuple-element.22.c_ref.v_ref), custom_call_target="tpu_custom_call" | custom-call | flops 301989888 | bytes 1048576 | tf_op jit(solution)/shard_map/local_grad/pallas_call | solution.py:445
  8.1 0.0 copy-start
  8.1 1.5 %collective-permute-done.1.refs_1_ = bf16[2,8,512]{2,1,0:T(8,128)(2,1)S(1)} collective-permute-done((bf16[2,8,512]{2,1,0:T(8,128)(2,1)S(1)}, bf16[2,8,512]{2,1,0:T(8,128)(2,1)S(1)}, u32[]{:S(2)}, u32[]{:S(2)}) %collective-permute-start.1) | collective-permute-done | bytes 16416 | tf_op jit(solution)/shard_map/ppermute | solution.py:434
  9.6 0.0 collective-permute-done.2.refs_2_
  9.6 0.0 collective-permute-done.refs_0_
  9.6 0.6 %kernel_grad.1 = (f32[432,128]{1,0:T(8,128)S(1)}, f32[448,128]{1,0:T(8,128)S(1)}, bf16[16,128]{1,0:T(8,128)(2,1)S(1)}) custom-call(bf16[2,8,8,512]{3,2,1,0:T(8,128)(2,1)S(1)} %get-tuple-element.21.f_ref.v_ref, bf16[2,8,8,512]{3,2,1,0:T(8,128)(2,1)S(1)} %get-tuple-element.22.c_ref.v_ref, f32[768,384]{1,0:T(8,128)S(1)} %local_grad.1.local_ref, ...), custom_call_target="tpu_custom_call" | custom-call | flops 37748736 | bytes 1048576 | tf_op jit(solution)/shard_map/kernel_grad/pallas_call | solution.py:456
  10.2 0.1 collective-permute-start.3
  10.3 1.5 %collective-permute-done.3 = f32[448,128]{1,0:T(8,128)S(1)} collective-permute-done((f32[448,128]{1,0:T(8,128)S(1)}, f32[448,128]{1,0:T(8,128)S(1)}, u32[]{:S(2)}, u32[]{:S(2)}) %collective-permute-start.3) | collective-permute-done | bytes 229408 | tf_op jit(solution)/shard_map/ppermute | solution.py:491
  11.9 2.5 %collective-permute-start.4 = (bf16[448,128]{1,0:T(8,128)(2,1)S(1)}, bf16[448,128]{1,0:T(8,128)(2,1)S(1)}, u32[]{:S(2)}, u32[]{:S(2)}) collective-permute-start(bf16[448,128]{1,0:T(8,128)(2,1)S(1)} %pad_maximum_fusion.1), channel_id=1, source_target_pairs={{0,9},{1,2},{3,10},{2,1},{5,12},{4,7},{6,15},{7,4},{9,0},{8,11},{1... | collective-permute-start | bytes 344072 | tf_op jit(solution)/shard_map/ppermute | solution.py:516
  14.4 2.7 %collective-permute-done.4.refs_3_ = bf16[448,128]{1,0:T(8,128)(2,1)S(1)} collective-permute-done((bf16[448,128]{1,0:T(8,128)(2,1)S(1)}, bf16[448,128]{1,0:T(8,128)(2,1)S(1)}, u32[]{:S(2)}, u32[]{:S(2)}) %collective-permute-start.4) | collective-permute-done | bytes 114720 | tf_op jit(solution)/shard_map/ppermute | solution.py:516
  17.1 1.4 %collective-permute-start.5 = (bf16[448,128]{1,0:T(8,128)(2,1)S(1)}, bf16[448,128]{1,0:T(8,128)(2,1)S(1)}, u32[]{:S(2)}, u32[]{:S(2)}) collective-permute-start(bf16[448,128]{1,0:T(8,128)(2,1)S(1)} %pad_maximum_fusion), channel_id=1, source_target_pairs={{0,5},{1,8},{3,6},{2,11},{5,0},{4,13},{6,3},{7,14},{9,12},{8,1},{1... | collective-permute-start | bytes 344072 | tf_op jit(solution)/shard_map/ppermute | solution.py:516
  18.5 0.0 copy-done
  18.5 0.3 %weights.1 = (bf16[9,256,128]{2,1,0:T(8,128)(2,1)S(1)}, bf16[9,128,256]{2,1,0:T(8,128)(2,1)S(1)}) custom-call(bf16[27,64,64]{2,1,0:T(8,128)(2,1)S(1)} %bitcast.7), custom_call_target="tpu_custom_call" | custom-call | bytes 1048576 | tf_op jit(solution)/shard_map/weights/pallas_call | solution.py:471
  18.8 0.7 %collective-permute-start.6 = (bf16[16,128]{1,0:T(8,128)(2,1)S(1)}, bf16[16,128]{1,0:T(8,128)(2,1)S(1)}, u32[]{:S(2)}, u32[]{:S(2)}) collective-permute-start(bf16[16,128]{1,0:T(8,128)(2,1)S(1)} %get-tuple-element.28), channel_id=1, source_target_pairs={{0,1},{1,0},{2,3},{3,2},{4,5},{5,4},{6,8},{7,9},{8,6},{9,7},{10,11... | collective-permute-start | bytes 12296 | tf_op jit(solution)/shard_map/ppermute | solution.py:496
  19.5 3.1 %collective-permute-done.5.refs_4_ = bf16[448,128]{1,0:T(8,128)(2,1)S(1)} collective-permute-done((bf16[448,128]{1,0:T(8,128)(2,1)S(1)}, bf16[448,128]{1,0:T(8,128)(2,1)S(1)}, u32[]{:S(2)}, u32[]{:S(2)}) %collective-permute-start.5) | collective-permute-done | bytes 114720 | tf_op jit(solution)/shard_map/ppermute | solution.py:516
  22.6 0.0 collective-permute-done.6.refs_5_
  22.7 1.3 %collective-permute-start.7 = (bf16[432,128]{1,0:T(8,128)(2,1)S(1)}, bf16[432,128]{1,0:T(8,128)(2,1)S(1)}, u32[]{:S(2)}, u32[]{:S(2)}) collective-permute-start(bf16[432,128]{1,0:T(8,128)(2,1)S(1)} %add_convert_fusion), channel_id=1, source_target_pairs={{0,3},{1,4},{3,0},{2,7},{5,6},{4,1},{6,5},{7,2},{9,10},{8,13},{10,... | collective-permute-start | bytes 331784 | tf_op jit(solution)/shard_map/ppermute | solution.py:516
  24.0 1.5 %response.1 = bf16[128,512]{1,0:T(8,128)(2,1)} custom-call(bf16[2,8,8,512]{3,2,1,0:T(8,128)(2,1)S(1)} %get-tuple-element.21.f_ref.v_ref, bf16[2,2,8,512]{3,2,1,0:T(8,128)(2,1)S(1)} %collective-permute-done.refs_0_, bf16[2,8,512]{2,1,0:T(8,128)(2,1)S(1)} %collective-permute-done.1.refs_1_, bf16[2,8,512]{2,1,0:T(8,128)(2,1)S(1)} %collective-permute-done.2.refs_2_, ...), custom_call_target="tpu_custom_call" | custom-call | flops 301989888 | bytes 1048576 | tf_op jit(solution)/shard_map/response/pallas_call | solution.py:480
  25.5 1.4 %collective-permute-done.7 = bf16[432,128]{1,0:T(8,128)(2,1)S(1)} collective-permute-done((bf16[432,128]{1,0:T(8,128)(2,1)S(1)}, bf16[432,128]{1,0:T(8,128)(2,1)S(1)}, u32[]{:S(2)}, u32[]{:S(2)}) %collective-permute-start.7) | collective-permute-done | bytes 110624 | tf_op jit(solution)/shard_map/ppermute | solution.py:516
  26.9 0.5 %collective-permute-start.8 = (f32[432,128]{1,0:T(8,128)S(1)}, f32[432,128]{1,0:T(8,128)S(1)}, u32[]{:S(2)}, u32[]{:S(2)}) collective-permute-start(f32[432,128]{1,0:T(8,128)S(1)} %convert_add_fusion.own_ref), channel_id=1, source_target_pairs={{0,1},{1,0},{2,3},{3,2},{4,5},{5,4},{6,7},{7,6},{8,9},{9,8},{10,11... | collective-permute-start | bytes 663560 | tf_op jit(solution)/shard_map/ppermute | solution.py:522
  27.4 1.5 %feature_grad.1 = bf16[128,512]{1,0:T(8,128)(2,1)} custom-call(bf16[2,8,8,512]{3,2,1,0:T(8,128)(2,1)S(1)} %get-tuple-element.22.c_ref.v_ref, bf16[2,2,8,512]{3,2,1,0:T(8,128)(2,1)S(1)} %collective-permute-done.refs_0_, bf16[2,8,512]{2,1,0:T(8,128)(2,1)S(1)} %collective-permute-done.1.refs_1_, bf16[2,8,512]{2,1,0:T(8,128)(2,1)S(1)} %collective-permute-done.2.refs_2_, ...), custom_call_target="tpu_custom_call" | custom-call | flops 301989888 | bytes 1048576 | tf_op jit(solution)/shard_map/feature_grad/pallas_call | solution.py:480
  28.9 0.0 collective-permute-done.8.other_ref
  28.9 1.1 %unpack.1 = f32[9,192,64]{2,1,0:T(8,128)} custom-call(f32[432,128]{1,0:T(8,128)S(1)} %convert_add_fusion.own_ref, f32[432,128]{1,0:T(8,128)S(1)} %collective-permute-done.8.other_ref), custom_call_target="tpu_custom_call" | custom-call | bytes 1048576 | tf_op jit(solution)/shard_map/unpack/pallas_call | solution.py:526
  (7 shorter events, 0.1 us)
Async XLA Ops:
  1.8 7.8 %collective-permute-start = (bf16[2,2,8,512]{3,2,1,0:T(8,128)(2,1)S(1)}, bf16[2,2,8,512]{3,2,1,0:T(8,128)(2,1)S(1)}, u32[]{:S(2)}, u32[]{:S(2)}) collective-permute-start(bf16[2,2,8,512]{3,2,1,0:T(8,128)(2,1)S(1)} %get-tuple-element.23), channel_id=1, source_target_pairs={{0,8},{1,9},{2,10},{3,11},{4,12},{5,13},{6,14},{7,15},{8,0},{9,1},... | collective-permute-start | bytes 98312 | tf_op jit(solution)/shard_map/ppermute | solution.py:434
  5.9 3.7 %collective-permute-start.1 = (bf16[2,8,512]{2,1,0:T(8,128)(2,1)S(1)}, bf16[2,8,512]{2,1,0:T(8,128)(2,1)S(1)}, u32[]{:S(2)}, u32[]{:S(2)}) collective-permute-start(bf16[2,8,512]{2,1,0:T(8,128)(2,1)S(1)} %get-tuple-element.24), channel_id=1, source_target_pairs={{0,2},{1,3},{2,0},{3,1},{4,6},{5,7},{6,4},{7,5},{8,10},{9,11},{10,... | collective-permute-start | bytes 49160 | tf_op jit(solution)/shard_map/ppermute | solution.py:434
  7.4 2.3 %collective-permute-start.2 = (bf16[2,8,512]{2,1,0:T(8,128)(2,1)S(1)}, bf16[2,8,512]{2,1,0:T(8,128)(2,1)S(1)}, u32[]{:S(2)}, u32[]{:S(2)}) collective-permute-start(bf16[2,8,512]{2,1,0:T(8,128)(2,1)S(1)} %get-tuple-element.25), channel_id=1, source_target_pairs={{0,1},{1,0},{2,3},{3,2},{4,5},{5,4},{6,8},{7,9},{8,6},{9,7},{10,11... | collective-permute-start | bytes 49160 | tf_op jit(solution)/shard_map/ppermute | solution.py:434
  8.1 10.4 %copy-start = (bf16[3,3,3,64,64]{4,3,2,1,0:T(8,128)(2,1)S(1)}, bf16[3,3,3,64,64]{4,3,2,1,0:T(8,128)(2,1)}, u32[]{:S(2)}) copy-start(bf16[3,3,3,64,64]{4,3,2,1,0:T(8,128)(2,1)} %param.6) | copy-start | bytes 663556
  10.2 1.6 %collective-permute-start.3 = (f32[448,128]{1,0:T(8,128)S(1)}, f32[448,128]{1,0:T(8,128)S(1)}, u32[]{:S(2)}, u32[]{:S(2)}) collective-permute-start(f32[448,128]{1,0:T(8,128)S(1)} %get-tuple-element.27), channel_id=1, source_target_pairs={{0,1},{1,0},{2,3},{3,2},{4,5},{5,4},{6,7},{7,6},{8,9},{9,8},{10,11... | collective-permute-start | bytes 688136 | tf_op jit(solution)/shard_map/ppermute | solution.py:491
  11.9 5.2 %collective-permute-start.4 = (bf16[448,128]{1,0:T(8,128)(2,1)S(1)}, bf16[448,128]{1,0:T(8,128)(2,1)S(1)}, u32[]{:S(2)}, u32[]{:S(2)}) collective-permute-start(bf16[448,128]{1,0:T(8,128)(2,1)S(1)} %pad_maximum_fusion.1), channel_id=1, source_target_pairs={{0,9},{1,2},{3,10},{2,1},{5,12},{4,7},{6,15},{7,4},{9,0},{8,11},{1... | collective-permute-start | bytes 344072 | tf_op jit(solution)/shard_map/ppermute | solution.py:516
  17.1 5.5 %collective-permute-start.5 = (bf16[448,128]{1,0:T(8,128)(2,1)S(1)}, bf16[448,128]{1,0:T(8,128)(2,1)S(1)}, u32[]{:S(2)}, u32[]{:S(2)}) collective-permute-start(bf16[448,128]{1,0:T(8,128)(2,1)S(1)} %pad_maximum_fusion), channel_id=1, source_target_pairs={{0,5},{1,8},{3,6},{2,11},{5,0},{4,13},{6,3},{7,14},{9,12},{8,1},{1... | collective-permute-start | bytes 344072 | tf_op jit(solution)/shard_map/ppermute | solution.py:516
  18.8 3.8 %collective-permute-start.6 = (bf16[16,128]{1,0:T(8,128)(2,1)S(1)}, bf16[16,128]{1,0:T(8,128)(2,1)S(1)}, u32[]{:S(2)}, u32[]{:S(2)}) collective-permute-start(bf16[16,128]{1,0:T(8,128)(2,1)S(1)} %get-tuple-element.28), channel_id=1, source_target_pairs={{0,1},{1,0},{2,3},{3,2},{4,5},{5,4},{6,8},{7,9},{8,6},{9,7},{10,11... | collective-permute-start | bytes 12296 | tf_op jit(solution)/shard_map/ppermute | solution.py:496
  22.7 4.2 %collective-permute-start.7 = (bf16[432,128]{1,0:T(8,128)(2,1)S(1)}, bf16[432,128]{1,0:T(8,128)(2,1)S(1)}, u32[]{:S(2)}, u32[]{:S(2)}) collective-permute-start(bf16[432,128]{1,0:T(8,128)(2,1)S(1)} %add_convert_fusion), channel_id=1, source_target_pairs={{0,3},{1,4},{3,0},{2,7},{5,6},{4,1},{6,5},{7,2},{9,10},{8,13},{10,... | collective-permute-start | bytes 331784 | tf_op jit(solution)/shard_map/ppermute | solution.py:516
  26.9 2.0 %collective-permute-start.8 = (f32[432,128]{1,0:T(8,128)S(1)}, f32[432,128]{1,0:T(8,128)S(1)}, u32[]{:S(2)}, u32[]{:S(2)}) collective-permute-start(f32[432,128]{1,0:T(8,128)S(1)} %convert_add_fusion.own_ref), channel_id=1, source_target_pairs={{0,1},{1,0},{2,3},{3,2},{4,5},{5,4},{6,7},{7,6},{8,9},{9,8},{10,11... | collective-permute-start | bytes 663560 | tf_op jit(solution)/shard_map/ppermute | solution.py:522

commit v9 on v8

--- a/solution.py
+++ b/solution.py
@@ -287,7 +287,7 @@
         for (source, side), row in halo.items():
             store_line(lines, 2 * source + side, jnp.where(up, row[edge - 1 : edge], row[0:1]))
         if joined:
-            send_ref[count:, :] = lines[...]
+            send_ref[count:, :] = lines[...].astype(send_ref.dtype)
         else:
             line_refs[number][...] = lines[...].astype(BF16)
     for number, out in enumerate(hop_refs):
@@ -301,7 +301,7 @@
         out[...] = lines[...].astype(BF16)
     own = my_half()
     keep_ref[...] = packed[pl.ds(pl.multiple_of(own * count, 8), count), :]
-    send_ref[:count, :] = packed[pl.ds(pl.multiple_of((1 - own) * count, 8), count), :]
+    send_ref[:count, :] = packed[pl.ds(pl.multiple_of((1 - own) * count, 8), count), :].astype(send_ref.dtype)
 
 
 def conv_kernel(roles, tiles, channels, source, ways, v_ref, *refs):
@@ -456,7 +456,7 @@
     keep, send, *lines = call(
         functools.partial(kernel_grad_kernel, roles, tiles, channels, joined),
         [VMEM] * (3 + near),
-        [shape((count, lanes), F32), shape((count + line_rows * joined, lanes), F32)]
+        [shape((count, lanes), F32), shape((count + line_rows * joined, lanes), wire)]
         + [shape((line_rows, lanes), BF16)] * (counts[2] if joined else counts[0] + counts[2]),
         [
             pltpu.VMEM((bricks, 3 * edge, width), F32),
@@ -489,7 +489,7 @@
     cores = lax.axis_size("dp")
     swap = [(0, 1), (1, 0)]
     summed = lax.ppermute(send, "dp", swap)
-    part = keep + summed[:count]
+    part = keep + summed[:count].astype(F32)
     if not joined:
         got += [lax.ppermute(x, ("space", "dp"), one) for x, one in zip(lines, pairs[0])]
         lines = lines[counts[0] :]

time: 30.1 us -> 30 us (level)
  no operation moved by 1% of the time
where the time goes in v9:
time: 30 us; the launch traced here: 29.8 us
  starting transfers between devices  12.1 us (40%)
  waiting for transfers between devices  9.96 us (33%)
  Pallas kernels  6.93 us (23%)
  between operations  0.72 us (2%)
    ppermute x3, waiting for transfers between devices, body(): theirs = lax.ppermute(mine, ('space', 'dp'), step)  7.14 us
    ppermute x4, starting transfers between devices, body(): lax.ppermute(x, ('space', 'dp'), one)  6.27 us
    ppermute x3, starting transfers between devices, body(): theirs = lax.ppermute(mine, ('space', 'dp'), step)  5.25 us
    pallas_call x2, Pallas kernels, conv(): call(functools.partial(conv_kernel, roles, tiles, channels, source, ready...  3.04 us
    ppermute x4, waiting for transfers between devices, body(): lax.ppermute(x, ('space', 'dp'), one)  1.51 us
    ppermute x1, waiting for transfers between devices, body(): summed = lax.ppermute(send, 'dp', swap)  1.31 us
    pallas_call x1, Pallas kernels, body(): call(functools.partial(faces_kernel, roles, tiles), [HBM, HBM, HBM], [plt...  1.15 us
    pallas_call x1, Pallas kernels, body(): call(functools.partial(unpack_kernel, 1.0 / math.sqrt(cells)), [VMEM, VME...  1.07 us
  transfers between devices with their start and end apart: 9, of which 5 were waited for; matrix products, arithmetic and copies ran while one was open for 0% of the time, Pallas kernels for 14%

profile of v9, /device:TPU:0, one launch (start us, length us, event | category | flops | bytes accessed | tf_op | source)
XLA Modules:
  0.0 29.8 jit_solution(4735988460282922198)
XLA Ops:
  0.6 1.1 %faces.1 = (bf16[2,2,8,512]{3,2,1,0:T(8,128)(2,1)S(1)}, bf16[2,8,512]{2,1,0:T(8,128)(2,1)S(1)}, bf16[2,8,512]{2,1,0:T(8,128)(2,1)S(1)}, bf16[2,8,8,512]{3,2,1,0:T(8,128)(2,1)S(1)}, bf16[2,8,8,512]{3,2,1,0:T(8,128)(2,1)S(1)}) custom-call(bf16[2,8,8,512]{3,2,1,0:T(8,128)(2,1)} %bitcast.11, bf16[2,8,8,512]{3,2,1,0:T(8,128)(2,1)} %bitcast.12, s32[2,6]{1,0:T(2,128)} %bitcast.13), custom_call_target="tpu_custom_call" | custom-call | bytes 1048576 | tf_op jit(solution)/shard_map/faces/pallas_call | solution.py:424
  1.8 4.1 %collective-permute-start = (bf16[2,2,8,512]{3,2,1,0:T(8,128)(2,1)S(1)}, bf16[2,2,8,512]{3,2,1,0:T(8,128)(2,1)S(1)}, u32[]{:S(2)}, u32[]{:S(2)}) collective-permute-start(bf16[2,2,8,512]{3,2,1,0:T(8,128)(2,1)S(1)} %get-tuple-element.23), channel_id=1, source_target_pairs={{0,8},{1,9},{2,10},{3,11},{4,12},{5,13},{6,14},{7,15},{8,0},{9,1},... | collective-permute-start | bytes 98312 | tf_op jit(solution)/shard_map/ppermute | solution.py:434
  5.9 1.5 %collective-permute-start.1 = (bf16[2,8,512]{2,1,0:T(8,128)(2,1)S(1)}, bf16[2,8,512]{2,1,0:T(8,128)(2,1)S(1)}, u32[]{:S(2)}, u32[]{:S(2)}) collective-permute-start(bf16[2,8,512]{2,1,0:T(8,128)(2,1)S(1)} %get-tuple-element.24), channel_id=1, source_target_pairs={{0,2},{1,3},{2,0},{3,1},{4,6},{5,7},{6,4},{7,5},{8,10},{9,11},{10,... | collective-permute-start | bytes 49160 | tf_op jit(solution)/shard_map/ppermute | solution.py:434
  7.4 0.0 collective-permute-start.2
  7.4 0.7 %local_grad.1.local_ref = f32[768,384]{1,0:T(8,128)S(1)} custom-call(bf16[2,8,8,512]{3,2,1,0:T(8,128)(2,1)S(1)} %get-tuple-element.21.f_ref.v_ref, bf16[2,8,8,512]{3,2,1,0:T(8,128)(2,1)S(1)} %get-tuple-element.22.c_ref.v_ref), custom_call_target="tpu_custom_call" | custom-call | flops 301989888 | bytes 1048576 | tf_op jit(solution)/shard_map/local_grad/pallas_call | solution.py:445
  8.1 0.0 copy-start
  8.1 1.5 %collective-permute-done.1.refs_1_ = bf16[2,8,512]{2,1,0:T(8,128)(2,1)S(1)} collective-permute-done((bf16[2,8,512]{2,1,0:T(8,128)(2,1)S(1)}, bf16[2,8,512]{2,1,0:T(8,128)(2,1)S(1)}, u32[]{:S(2)}, u32[]{:S(2)}) %collective-permute-start.1) | collective-permute-done | bytes 16416 | tf_op jit(solution)/shard_map/ppermute | solution.py:434
  9.6 0.0 collective-permute-done.2.refs_2_
  9.6 0.0 collective-permute-done.refs_0_
  9.6 0.6 %kernel_grad.1 = (f32[432,128]{1,0:T(8,128)S(1)}, bf16[448,128]{1,0:T(8,128)(2,1)S(1)}, bf16[16,128]{1,0:T(8,128)(2,1)S(1)}) custom-call(bf16[2,8,8,512]{3,2,1,0:T(8,128)(2,1)S(1)} %get-tuple-element.21.f_ref.v_ref, bf16[2,8,8,512]{3,2,1,0:T(8,128)(2,1)S(1)} %get-tuple-element.22.c_ref.v_ref, f32[768,384]{1,0:T(8,128)S(1)} %local_grad.1.local_ref, ...), custom_call_target="tpu_custom_call" | custom-call | flops 37748736 | bytes 1048576 | tf_op jit(solution)/shard_map/kernel_grad/pallas_call | solution.py:456
  10.2 0.1 collective-permute-start.3
  10.3 1.3 %collective-permute-done.3 = bf16[448,128]{1,0:T(8,128)(2,1)S(1)} collective-permute-done((bf16[448,128]{1,0:T(8,128)(2,1)S(1)}, bf16[448,128]{1,0:T(8,128)(2,1)S(1)}, u32[]{:S(2)}, u32[]{:S(2)}) %collective-permute-start.3) | collective-permute-done | bytes 114720 | tf_op jit(solution)/shard_map/ppermute | solution.py:491
  11.7 2.5 %collective-permute-start.4 = (bf16[448,128]{1,0:T(8,128)(2,1)S(1)}, bf16[448,128]{1,0:T(8,128)(2,1)S(1)}, u32[]{:S(2)}, u32[]{:S(2)}) collective-permute-start(bf16[448,128]{1,0:T(8,128)(2,1)S(1)} %pad_maximum_fusion.1), channel_id=1, source_target_pairs={{0,9},{1,2},{3,10},{2,1},{5,12},{4,7},{6,15},{7,4},{9,0},{8,11},{1... | collective-permute-start | bytes 344072 | tf_op jit(solution)/shard_map/ppermute | solution.py:516
  14.2 2.6 %collective-permute-done.4.refs_3_ = bf16[448,128]{1,0:T(8,128)(2,1)S(1)} collective-permute-done((bf16[448,128]{1,0:T(8,128)(2,1)S(1)}, bf16[448,128]{1,0:T(8,128)(2,1)S(1)}, u32[]{:S(2)}, u32[]{:S(2)}) %collective-permute-start.4) | collective-permute-done | bytes 114720 | tf_op jit(solution)/shard_map/ppermute | solution.py:516
  16.9 1.4 %collective-permute-start.5 = (bf16[448,128]{1,0:T(8,128)(2,1)S(1)}, bf16[448,128]{1,0:T(8,128)(2,1)S(1)}, u32[]{:S(2)}, u32[]{:S(2)}) collective-permute-start(bf16[448,128]{1,0:T(8,128)(2,1)S(1)} %pad_maximum_fusion), channel_id=1, source_target_pairs={{0,5},{1,8},{3,6},{2,11},{5,0},{4,13},{6,3},{7,14},{9,12},{8,1},{1... | collective-permute-start | bytes 344072 | tf_op jit(solution)/shard_map/ppermute | solution.py:516
  18.3 0.0 copy-done
  18.3 0.3 %weights.1 = (bf16[9,256,128]{2,1,0:T(8,128)(2,1)S(1)}, bf16[9,128,256]{2,1,0:T(8,128)(2,1)S(1)}) custom-call(bf16[27,64,64]{2,1,0:T(8,128)(2,1)S(1)} %bitcast.7), custom_call_target="tpu_custom_call" | custom-call | bytes 1048576 | tf_op jit(solution)/shard_map/weights/pallas_call | solution.py:471
  18.7 0.7 %collective-permute-start.6 = (bf16[16,128]{1,0:T(8,128)(2,1)S(1)}, bf16[16,128]{1,0:T(8,128)(2,1)S(1)}, u32[]{:S(2)}, u32[]{:S(2)}) collective-permute-start(bf16[16,128]{1,0:T(8,128)(2,1)S(1)} %get-tuple-element.28), channel_id=1, source_target_pairs={{0,1},{1,0},{2,3},{3,2},{4,5},{5,4},{6,8},{7,9},{8,6},{9,7},{10,11... | collective-permute-start | bytes 12296 | tf_op jit(solution)/shard_map/ppermute | solution.py:496
  19.3 3.1 %collective-permute-done.5.refs_4_ = bf16[448,128]{1,0:T(8,128)(2,1)S(1)} collective-permute-done((bf16[448,128]{1,0:T(8,128)(2,1)S(1)}, bf16[448,128]{1,0:T(8,128)(2,1)S(1)}, u32[]{:S(2)}, u32[]{:S(2)}) %collective-permute-start.5) | collective-permute-done | bytes 114720 | tf_op jit(solution)/shard_map/ppermute | solution.py:516
  22.5 0.0 collective-permute-done.6.refs_5_
  22.5 1.3 %collective-permute-start.7 = (bf16[432,128]{1,0:T(8,128)(2,1)S(1)}, bf16[432,128]{1,0:T(8,128)(2,1)S(1)}, u32[]{:S(2)}, u32[]{:S(2)}) collective-permute-start(bf16[432,128]{1,0:T(8,128)(2,1)S(1)} %add_convert_fusion), channel_id=1, source_target_pairs={{0,3},{1,4},{3,0},{2,7},{5,6},{4,1},{6,5},{7,2},{9,10},{8,13},{10,... | collective-permute-start | bytes 331784 | tf_op jit(solution)/shard_map/ppermute | solution.py:516
  23.8 1.5 %response.1 = bf16[128,512]{1,0:T(8,128)(2,1)} custom-call(bf16[2,8,8,512]{3,2,1,0:T(8,128)(2,1)S(1)} %get-tuple-element.21.f_ref.v_ref, bf16[2,2,8,512]{3,2,1,0:T(8,128)(2,1)S(1)} %collective-permute-done.refs_0_, bf16[2,8,512]{2,1,0:T(8,128)(2,1)S(1)} %collective-permute-done.1.refs_1_, bf16[2,8,512]{2,1,0:T(8,128)(2,1)S(1)} %collective-permute-done.2.refs_2_, ...), custom_call_target="tpu_custom_call" | custom-call | flops 301989888 | bytes 1048576 | tf_op jit(solution)/shard_map/response/pallas_call | solution.py:480
  25.3 1.4 %collective-permute-done.7 = bf16[432,128]{1,0:T(8,128)(2,1)S(1)} collective-permute-done((bf16[432,128]{1,0:T(8,128)(2,1)S(1)}, bf16[432,128]{1,0:T(8,128)(2,1)S(1)}, u32[]{:S(2)}, u32[]{:S(2)}) %collective-permute-start.7) | collective-permute-done | bytes 110624 | tf_op jit(solution)/shard_map/ppermute | solution.py:516
  26.7 0.5 %collective-permute-start.8 = (f32[432,128]{1,0:T(8,128)S(1)}, f32[432,128]{1,0:T(8,128)S(1)}, u32[]{:S(2)}, u32[]{:S(2)}) collective-permute-start(f32[432,128]{1,0:T(8,128)S(1)} %convert_add_fusion.own_ref), channel_id=1, source_target_pairs={{0,1},{1,0},{2,3},{3,2},{4,5},{5,4},{6,7},{7,6},{8,9},{9,8},{10,11... | collective-permute-start | bytes 663560 | tf_op jit(solution)/shard_map/ppermute | solution.py:522
  27.2 1.5 %feature_grad.1 = bf16[128,512]{1,0:T(8,128)(2,1)} custom-call(bf16[2,8,8,512]{3,2,1,0:T(8,128)(2,1)S(1)} %get-tuple-element.22.c_ref.v_ref, bf16[2,2,8,512]{3,2,1,0:T(8,128)(2,1)S(1)} %collective-permute-done.refs_0_, bf16[2,8,512]{2,1,0:T(8,128)(2,1)S(1)} %collective-permute-done.1.refs_1_, bf16[2,8,512]{2,1,0:T(8,128)(2,1)S(1)} %collective-permute-done.2.refs_2_, ...), custom_call_target="tpu_custom_call" | custom-call | flops 301989888 | bytes 1048576 | tf_op jit(solution)/shard_map/feature_grad/pallas_call | solution.py:480
  28.8 0.0 collective-permute-done.8.other_ref
  28.8 1.1 %unpack.1 = f32[9,192,64]{2,1,0:T(8,128)} custom-call(f32[432,128]{1,0:T(8,128)S(1)} %convert_add_fusion.own_ref, f32[432,128]{1,0:T(8,128)S(1)} %collective-permute-done.8.other_ref), custom_call_target="tpu_custom_call" | custom-call | bytes 1048576 | tf_op jit(solution)/shard_map/unpack/pallas_call | solution.py:526
  (7 shorter events, 0.1 us)
Async XLA Ops:
  1.8 7.8 %collective-permute-start = (bf16[2,2,8,512]{3,2,1,0:T(8,128)(2,1)S(1)}, bf16[2,2,8,512]{3,2,1,0:T(8,128)(2,1)S(1)}, u32[]{:S(2)}, u32[]{:S(2)}) collective-permute-start(bf16[2,2,8,512]{3,2,1,0:T(8,128)(2,1)S(1)} %get-tuple-element.23), channel_id=1, source_target_pairs={{0,8},{1,9},{2,10},{3,11},{4,12},{5,13},{6,14},{7,15},{8,0},{9,1},... | collective-permute-start | bytes 98312 | tf_op jit(solution)/shard_map/ppermute | solution.py:434
  5.9 3.7 %collective-permute-start.1 = (bf16[2,8,512]{2,1,0:T(8,128)(2,1)S(1)}, bf16[2,8,512]{2,1,0:T(8,128)(2,1)S(1)}, u32[]{:S(2)}, u32[]{:S(2)}) collective-permute-start(bf16[2,8,512]{2,1,0:T(8,128)(2,1)S(1)} %get-tuple-element.24), channel_id=1, source_target_pairs={{0,2},{1,3},{2,0},{3,1},{4,6},{5,7},{6,4},{7,5},{8,10},{9,11},{10,... | collective-permute-start | bytes 49160 | tf_op jit(solution)/shard_map/ppermute | solution.py:434
  7.4 2.3 %collective-permute-start.2 = (bf16[2,8,512]{2,1,0:T(8,128)(2,1)S(1)}, bf16[2,8,512]{2,1,0:T(8,128)(2,1)S(1)}, u32[]{:S(2)}, u32[]{:S(2)}) collective-permute-start(bf16[2,8,512]{2,1,0:T(8,128)(2,1)S(1)} %get-tuple-element.25), channel_id=1, source_target_pairs={{0,1},{1,0},{2,3},{3,2},{4,5},{5,4},{6,8},{7,9},{8,6},{9,7},{10,11... | collective-permute-start | bytes 49160 | tf_op jit(solution)/shard_map/ppermute | solution.py:434
  8.1 10.2 %copy-start = (bf16[3,3,3,64,64]{4,3,2,1,0:T(8,128)(2,1)S(1)}, bf16[3,3,3,64,64]{4,3,2,1,0:T(8,128)(2,1)}, u32[]{:S(2)}) copy-start(bf16[3,3,3,64,64]{4,3,2,1,0:T(8,128)(2,1)} %param.6) | copy-start | bytes 663556
  10.2 1.4 %collective-permute-start.3 = (bf16[448,128]{1,0:T(8,128)(2,1)S(1)}, bf16[448,128]{1,0:T(8,128)(2,1)S(1)}, u32[]{:S(2)}, u32[]{:S(2)}) collective-permute-start(bf16[448,128]{1,0:T(8,128)(2,1)S(1)} %get-tuple-element.27), channel_id=1, source_target_pairs={{0,1},{1,0},{2,3},{3,2},{4,5},{5,4},{6,7},{7,6},{8,9},{9,8},{10,11... | collective-permute-start | bytes 344072 | tf_op jit(solution)/shard_map/ppermute | solution.py:491
  11.7 5.2 %collective-permute-start.4 = (bf16[448,128]{1,0:T(8,128)(2,1)S(1)}, bf16[448,128]{1,0:T(8,128)(2,1)S(1)}, u32[]{:S(2)}, u32[]{:S(2)}) collective-permute-start(bf16[448,128]{1,0:T(8,128)(2,1)S(1)} %pad_maximum_fusion.1), channel_id=1, source_target_pairs={{0,9},{1,2},{3,10},{2,1},{5,12},{4,7},{6,15},{7,4},{9,0},{8,11},{1... | collective-permute-start | bytes 344072 | tf_op jit(solution)/shard_map/ppermute | solution.py:516
  16.9 5.5 %collective-permute-start.5 = (bf16[448,128]{1,0:T(8,128)(2,1)S(1)}, bf16[448,128]{1,0:T(8,128)(2,1)S(1)}, u32[]{:S(2)}, u32[]{:S(2)}) collective-permute-start(bf16[448,128]{1,0:T(8,128)(2,1)S(1)} %pad_maximum_fusion), channel_id=1, source_target_pairs={{0,5},{1,8},{3,6},{2,11},{5,0},{4,13},{6,3},{7,14},{9,12},{8,1},{1... | collective-permute-start | bytes 344072 | tf_op jit(solution)/shard_map/ppermute | solution.py:516
  18.7 3.8 %collective-permute-start.6 = (bf16[16,128]{1,0:T(8,128)(2,1)S(1)}, bf16[16,128]{1,0:T(8,128)(2,1)S(1)}, u32[]{:S(2)}, u32[]{:S(2)}) collective-permute-start(bf16[16,128]{1,0:T(8,128)(2,1)S(1)} %get-tuple-element.28), channel_id=1, source_target_pairs={{0,1},{1,0},{2,3},{3,2},{4,5},{5,4},{6,8},{7,9},{8,6},{9,7},{10,11... | collective-permute-start | bytes 12296 | tf_op jit(solution)/shard_map/ppermute | solution.py:496
  22.5 4.2 %collective-permute-start.7 = (bf16[432,128]{1,0:T(8,128)(2,1)S(1)}, bf16[432,128]{1,0:T(8,128)(2,1)S(1)}, u32[]{:S(2)}, u32[]{:S(2)}) collective-permute-start(bf16[432,128]{1,0:T(8,128)(2,1)S(1)} %add_convert_fusion), channel_id=1, source_target_pairs={{0,3},{1,4},{3,0},{2,7},{5,6},{4,1},{6,5},{7,2},{9,10},{8,13},{10,... | collective-permute-start | bytes 331784 | tf_op jit(solution)/shard_map/ppermute | solution.py:516
  26.7 2.0 %collective-permute-start.8 = (f32[432,128]{1,0:T(8,128)S(1)}, f32[432,128]{1,0:T(8,128)S(1)}, u32[]{:S(2)}, u32[]{:S(2)}) collective-permute-start(f32[432,128]{1,0:T(8,128)S(1)} %convert_add_fusion.own_ref), channel_id=1, source_target_pairs={{0,1},{1,0},{2,3},{3,2},{4,5},{5,4},{6,7},{7,6},{8,9},{9,8},{10,11... | collective-permute-start | bytes 663560 | tf_op jit(solution)/shard_map/ppermute | solution.py:522
